TPU v7x, 128 devices: a whole 4x4x4 slice. The times are simulated.
128 devices in a mesh: ctx: 4 (over z_hi, core), req: 32 (over x, y, z_lo).
Axes of the slice: x: 4, y: 4, z: 4 (z_hi: 2, z_lo: 2; z = z_hi * 2 + z_lo), core: 2. Of those that a mesh axis runs over, the one named last changes fastest.
Arguments:
- pre_latent: bfloat16 [32, 256, 576], P('req', 'ctx')
- pre_qlat: bfloat16 [32, 256, 8, 512], P('req', 'ctx')
- pre_qrope: bfloat16 [32, 256, 8, 64], P('req', 'ctx'), may hold values from -6 to 6
- pre_resid: bfloat16 [32, 256, 2048], P('req', 'ctx'), may hold values from -6 to 6
- block_order: int32 [8], replicated, may hold values from 0 to 7, each once
- dec_new: bfloat16 [4, 32, 576], P(None, 'req')
- dec_qlat: bfloat16 [4, 32, 8, 512], P(None, 'req')
- dec_qrope: bfloat16 [4, 32, 8, 64], P(None, 'req'), may hold values from -6 to 6
- dec_resid: bfloat16 [4, 32, 2048], P(None, 'req'), may hold values from -6 to 6
- cache_len: int32 [4, 32], P(None, 'req'), may hold values from 1 to 2047
- page_table: int32 [4, 32, 32], P(None, 'req', 'ctx'), may hold values from 0 to 31, as said below
- cache_pool: bfloat16 [4096, 64, 576], P(('ctx', 'req')), may hold values from -6 to 6
- w_uv: bfloat16 [8, 512, 128], replicated, may hold values from -0.25 to 0.25
- w_out: bfloat16 [1024, 2048], replicated, may hold values from -0.1875 to 0.1875
- norm_gain: float32 [2048], replicated, may hold values from 0.1 to 1.9
- router: float32 [2048, 64], replicated, may hold values from -0.125 to 0.125
- routes: int32 [8320, 6], P(('ctx', 'req')), may hold values from 0 to 63, all different within a row; in each aligned block of 65 rows (0 to 64, 65 to 129, ...) at most 8 rows name the same one
- w_gate: bfloat16 [128, 2048, 704], P(('ctx', 'req')), may hold values from -0.125 to 0.125
- w_up: bfloat16 [128, 2048, 704], P(('ctx', 'req')), may hold values from -0.125 to 0.125
- w_down: bfloat16 [128, 704, 2048], P(('ctx', 'req')), may hold values from -0.15625 to 0.15625
Outputs:
- pre_out: bfloat16 [32, 256, 2048], P('req', 'ctx')
- dec_out: bfloat16 [4, 32, 2048], P('ctx', 'req')
- cache_out: bfloat16 [4096, 64, 576], P(('ctx', 'req'))
Inputs may be any that keep to these rules, and one draw needn't show every extreme that they name: `routes`: each row names 6 different experts; within the rows of one device no expert is named by more than 8 rows. `block_order`: each block appears once. `page_table`: for each request group and each 8 columns held by one ctx device, the entries of the 4 requests name each of that device's 32 pages once.
All inputs are finite; a program needn't handle non-finite values.
Results may differ from a plain program's by a relative error of at most 0.019.
Values may be sent and summed in bfloat16 or wider, within the bound.
A program may use at most 128 MiB of HBM per device.

v0:
```python
import jax
import jax.numpy as jnp
from jax import lax
from jax.sharding import PartitionSpec as P

DC = 512
DR = 64
DN = 128


THETA = 50000.0
ROUTE_SCALE = 2.446
EPSILON = 1e-06
NEG_FILL = -1e30


def joined(part, axis, combine):
    gathered = jax.tree.map(lambda a: lax.all_gather(a, axis), part)

    def take(source):
        return jax.tree.map(lambda a: lax.dynamic_index_in_dim(a, source, 0, False), gathered)

    return lax.fori_loop(
        1, lax.axis_size(axis), lambda source, state: combine(state, take(source)), take(0)
    )


def rope_tables(positions, rope_width):
    halfway = rope_width // 2
    inverse = THETA ** (-(jnp.arange(halfway).astype(jnp.float32) * 2.0) / rope_width)
    angles = positions.astype(jnp.float32)[..., None] * inverse
    return (jnp.cos(angles), jnp.sin(angles))


def rotate(values, cos_table, sin_table):
    halfway = values.shape[-1] // 2
    leading = values[..., :halfway].astype(jnp.float32)
    trailing = values[..., halfway:].astype(jnp.float32)
    return jnp.concatenate(
        [leading * cos_table - trailing * sin_table, trailing * cos_table + leading * sin_table],
        axis=-1,
    )


def block_position(block_order, global_rows, shard_rows):
    shard_id = global_rows // shard_rows
    within = global_rows % shard_rows
    half_rows = shard_rows // 2
    return block_order[2 * shard_id + within // half_rows] * half_rows + within % half_rows


def expert_half(inputs, gate_part, up_part, down_part):
    flat_rows = inputs.reshape(-1, inputs.shape[-1])
    gate_out = jnp.dot(flat_rows, gate_part, preferred_element_type=jnp.float32)
    upward = jnp.dot(flat_rows, up_part, preferred_element_type=jnp.float32)
    hidden = (jax.nn.silu(gate_out) * upward).astype(jnp.bfloat16)
    partial_out = jnp.dot(hidden, down_part, preferred_element_type=jnp.float32).astype(
        jnp.bfloat16
    )
    return partial_out.reshape(inputs.shape)


def merge_softmax(earlier, later):
    left_peak, left_total, left_accum = earlier
    right_peak, right_total, right_accum = later
    new_peak = jnp.maximum(left_peak, right_peak)
    left_factor = jnp.exp(left_peak - new_peak)
    right_factor = jnp.exp(right_peak - new_peak)
    merged_total = left_total * left_factor + right_total * right_factor
    merged_accum = left_accum * left_factor[..., None] + right_accum * right_factor[..., None]
    return (new_peak, merged_total, merged_accum)


def body(
    pre_latent,
    pre_qlat,
    pre_qrope,
    pre_resid,
    block_order,
    dec_new,
    dec_qlat,
    dec_qrope,
    dec_resid,
    cache_len,
    page_table,
    cache_pool,
    w_uv,
    w_out,
    norm_gain,
    router,
    routes,
    w_gate,
    w_up,
    w_down,
):
    ctx_count = lax.axis_size("ctx")
    ctx_index = lax.axis_index("ctx")
    score_scale = (DN + DR) ** (-0.5)
    latent = pre_latent[0]
    shard_rows = latent.shape[0]
    local_rows = jnp.arange(shard_rows)
    own_pos = block_position(block_order, ctx_index * shard_rows + local_rows, shard_rows)
    cos_table, sin_table = rope_tables(own_pos, DR)
    key_rope = rotate(latent[:, DC:], cos_table, sin_table).astype(jnp.bfloat16)
    stored = jnp.concatenate([latent[:, :DC], key_rope], axis=-1)[None]
    rotated = rotate(pre_qrope[0], cos_table[:, None, :], sin_table[:, None, :]).astype(
        jnp.bfloat16
    )
    queries = jnp.concatenate([pre_qlat[0], rotated], axis=-1)
    head_count = queries.shape[1]
    running_max = jnp.full((head_count, shard_rows), NEG_FILL, jnp.float32)
    moving = lax.all_gather(stored, "ctx", axis=1, tiled=True)[0]
    key_pos = block_position(block_order, jnp.arange(moving.shape[0]), shard_rows)
    scores = (
        jnp.einsum("qhd,kd->hqk", queries, moving, preferred_element_type=jnp.float32) * score_scale
    )
    visible = (key_pos[None, :] <= own_pos[:, None])[None]
    masked = jnp.where(visible, scores, NEG_FILL)
    new_peak = jnp.maximum(running_max, jnp.max(masked, axis=-1))
    weights = jnp.where(visible, jnp.exp(masked - new_peak[..., None]), 0.0)
    totals = jnp.sum(weights, axis=-1)
    accumulated = jnp.einsum(
        "hqk,kc->qhc",
        weights.astype(jnp.bfloat16),
        moving[:, :DC],
        preferred_element_type=jnp.float32,
    )
    running_max, totals, accumulated = (new_peak, totals, accumulated)
    pre_mixed = (accumulated / jnp.transpose(totals)[:, :, None]).astype(jnp.bfloat16)
    lengths = cache_len[:, 0]
    tables = page_table[:, 0, :]
    request_count = tables.shape[0]
    pages_dev = tables.shape[1]
    page_rows = cache_pool.shape[1]
    slot_count = cache_pool.shape[0]
    window_rows = pages_dev * page_rows
    cos_new, sin_new = rope_tables(lengths, DR)
    new_rope = rotate(dec_new[:, 0, DC:], cos_new, sin_new).astype(jnp.bfloat16)
    new_rows = jnp.concatenate([dec_new[:, 0, :DC], new_rope], axis=-1)
    page_index = lengths // page_rows
    owner_ctx = page_index // pages_dev
    slot_of = jnp.take_along_axis(tables, (page_index % pages_dev)[:, None], axis=1)[:, 0]
    target = jnp.where(
        owner_ctx == ctx_index, slot_of * page_rows + lengths % page_rows, slot_count * page_rows
    )
    flat_pool = (
        cache_pool.reshape(slot_count * page_rows, cache_pool.shape[2])
        .at[target]
        .set(new_rows, mode="drop")
    )
    gather_rows = (tables[:, :, None] * page_rows + jnp.arange(page_rows)[None, None, :]).reshape(
        request_count, window_rows
    )
    cached = flat_pool[gather_rows]
    cache_pos = ctx_index * window_rows + jnp.arange(window_rows)
    query_rot = rotate(dec_qrope[:, 0], cos_new[:, None, :], sin_new[:, None, :]).astype(
        jnp.bfloat16
    )
    dec_queries = jnp.concatenate([dec_qlat[:, 0], query_rot], axis=-1)
    dec_scores = (
        jnp.einsum("rhd,rkd->rhk", dec_queries, cached, preferred_element_type=jnp.float32)
        * score_scale
    )
    dec_visible = (cache_pos[None, :] <= lengths[:, None])[:, None, :]
    dec_masked = jnp.where(dec_visible, dec_scores, NEG_FILL)
    local_peak = jnp.max(dec_masked, axis=-1)
    dec_weights = jnp.where(dec_visible, jnp.exp(dec_masked - local_peak[..., None]), 0.0)
    local_total = jnp.sum(dec_weights, axis=-1)
    local_accum = jnp.einsum(
        "rhk,rkc->rhc",
        dec_weights.astype(jnp.bfloat16),
        cached[:, :, :DC],
        preferred_element_type=jnp.float32,
    )
    merged_peak, merged_total, merged_accum = joined(
        (local_peak, local_total, local_accum), "ctx", merge_softmax
    )
    dec_mixed = (merged_accum / merged_total[..., None]).astype(jnp.bfloat16)
    dec_share = request_count // ctx_count
    own_mixed = lax.dynamic_slice_in_dim(dec_mixed, ctx_index * dec_share, dec_share, 0)
    own_resid = lax.dynamic_slice_in_dim(dec_resid[:, 0], ctx_index * dec_share, dec_share, 0)
    mixed_all = jnp.concatenate([pre_mixed, own_mixed], axis=0)
    resid_all = jnp.concatenate([pre_resid[0], own_resid], axis=0)
    values = jnp.einsum("nhc,hcv->nhv", mixed_all, w_uv, preferred_element_type=jnp.float32).astype(
        jnp.bfloat16
    )
    hidden_state = resid_all.astype(jnp.float32) + jnp.dot(
        values.reshape(values.shape[0], -1), w_out, preferred_element_type=jnp.float32
    )
    normed = (
        hidden_state
        * lax.rsqrt(jnp.mean(hidden_state * hidden_state, axis=-1, keepdims=True) + EPSILON)
        * norm_gain
    ).astype(jnp.bfloat16)
    logits = jnp.dot(normed.astype(jnp.float32), router, precision=lax.Precision.HIGHEST)
    probable = jax.nn.sigmoid(logits)
    chosen = jnp.take_along_axis(probable, routes, axis=1)
    mixing = ROUTE_SCALE * chosen / jnp.sum(chosen, axis=1, keepdims=True)
    row_count = normed.shape[0]
    width = normed.shape[1]
    top_count = routes.shape[1]
    expert_count = router.shape[1]
    devices = ctx_count * lax.axis_size("req")
    capacity = 2 * ((row_count * top_count + 2 * expert_count - 1) // (2 * expert_count))
    expert_hits = (
        (routes[:, :, None] == jnp.arange(expert_count)[None, None, :]).astype(jnp.int32).sum(1)
    )
    before = jnp.cumsum(expert_hits, axis=0) - expert_hits
    slot_index = jnp.take_along_axis(before, routes, axis=1)
    target_slot = (routes * capacity + slot_index).reshape(-1)
    row_ids = jnp.repeat(jnp.arange(row_count), top_count)
    slot_table = (
        jnp.full((expert_count * capacity,), row_count, jnp.int32).at[target_slot].set(row_ids)
    )
    padded = jnp.concatenate([normed, jnp.zeros((1, width), jnp.bfloat16)], axis=0)
    outgoing = padded[slot_table].reshape(expert_count, capacity, width)
    doubled = jnp.broadcast_to(outgoing[:, None], (expert_count, 2, capacity, width)).reshape(
        devices, capacity, width
    )
    partial_out = expert_half(
        lax.all_to_all(doubled, ("ctx", "req"), split_axis=0, concat_axis=0, tiled=True),
        w_gate[0],
        w_up[0],
        w_down[0],
    )
    returned = lax.all_to_all(
        partial_out, ("ctx", "req"), split_axis=0, concat_axis=0, tiled=True
    ).reshape(expert_count, 2, capacity, width)
    results = (returned[:, 0].astype(jnp.float32) + returned[:, 1].astype(jnp.float32)).astype(
        jnp.bfloat16
    )
    picked = results.reshape(expert_count * capacity, width)[target_slot].reshape(
        row_count, top_count, width
    )
    moe = jnp.sum(mixing[:, :, None] * picked.astype(jnp.float32), axis=1)
    final = (hidden_state + moe).astype(jnp.bfloat16)
    pre_out = final[:shard_rows][None]
    dec_out = final[shard_rows:][:, None]
    cache_out = flat_pool.reshape(cache_pool.shape)
    return (pre_out, dec_out, cache_out)


def solution(mesh):
    in_specs = (
        P("req", "ctx", None),
        P("req", "ctx", None, None),
        P("req", "ctx", None, None),
        P("req", "ctx", None),
        P(),
        P(None, "req", None),
        P(None, "req", None, None),
        P(None, "req", None, None),
        P(None, "req", None),
        P(None, "req"),
        P(None, "req", "ctx"),
        P(("ctx", "req"), None, None),
        P(),
        P(),
        P(),
        P(),
        P(("ctx", "req"), None),
        P(("ctx", "req"), None, None),
        P(("ctx", "req"), None, None),
        P(("ctx", "req"), None, None),
    )
    out_specs = (P("req", "ctx", None), P("ctx", "req", None), P(("ctx", "req"), None, None))
    return jax.shard_map(body, mesh=mesh, in_specs=in_specs, out_specs=out_specs, check_vma=False)
```

profile of v0, /device:TPU:8, one launch (start us, length us, event | category | flops | bytes accessed | tf_op | source)
XLA Modules:
  0.0 253.8 jit_solution(5457439540793279715)
XLA Ops:
  0.7 3.6 %copy.119 = bf16[32,64,576]{2,1,0:T(8,128)(2,1)} copy(bf16[32,64,576]{2,1,0:T(8,128)(2,1)} %param.33) | data formatting | bytes 4718592
  4.5 0.6 gather_fusion.3
  5.7 4.5 %scatter_custom_fusion = bf16[2048,576]{1,0:T(8,128)(2,1)} fusion(bf16[2048,576]{1,0:T(8,128)(2,1)} %bitcast.169, s32[4]{0:T(128)S(1)} %get-tuple-element.227, bf16[4,32]{1,0:T(4,128)(2,1)S(1)} %get-tuple-element.216, bf16[]{:T(256)} %constant.352, bf16[4,32]{1,0:T(4,128)(2,1)S(1)} %get-tuple-element.217, bf16[4,512]{1,0:T(4,128)(2,1)S(1)} %slice_bitcast_fusion.6), kind=kCustom, calls=%fused_computation.120 | custom fusion | flops 13824 | bytes 2365952 | tf_op jit(solution)/shard_map/scatter | solution.py:149
  10.1 11.6 %gather_fusion = bf16[2048,576]{1,0:T(8,128)(2,1)} fusion(bf16[2048,576]{1,0:T(8,128)(2,1)} %scatter_custom_fusion, s32[2048]{0:T(1024)S(1)} %broadcast_clamp_fusion), kind=kCustom, calls=%fused_computation | custom fusion | bytes 4726784 | tf_op jit(solution)/shard_map/gather | solution.py:154
  21.8 2.7 %fusion.103 = (f32[4,8]{1,0:T(4,128)S(1)}, f32[4,8,512]{2,1,0:T(8,128)S(1)}) fusion(bf16[4,512,576]{2,1,0:T(8,128)(2,1)} %bitcast.173, bf16[4,8,32]{2,1,0:T(8,128)(2,1)S(1)} %get-tuple-element.209, bf16[4,8,32]{2,1,0:T(8,128)(2,1)S(1)} %get-tuple-element.208, bf16[4,8,512]{2,1,0:T(8,128)(2,1)S(1)} %bitcast.185, pred[4,512]{1,0:T(4,128)(4,1)S(1)} %broadcast_compare_fusion.1), kind=kOutput, calls=%fused_computation.237 | convolution fusion | flops 19034080 | bytes 2463872 | tf_op jit(solution)/shard_map/rhd,rkd->rhk/dot_general | solution.py:161
  24.6 0.4 fusion.11
  25.0 0.2 fusion.50
  25.2 0.7 fusion.102
  26.0 0.1 reshape.710
  26.3 4.6 %gather_fusion.5 = s32[390]{0:T(512)S(1)} fusion(s32[65,64]{1,0:T(8,128)S(1)} %sub.92, s32[390]{0:T(512)S(1)} %reshape.710), kind=kCustom, calls=%fused_computation.5 | custom fusion | bytes 6240 | tf_op jit(solution)/shard_map/jit(take_along_axis)/gather | solution.py:209
  31.3 0.1 reshape.640
  31.5 0.1 reshape.734
  31.6 2.9 %scatter_custom_fusion.1 = s32[512]{0:T(512)S(1)} fusion(s32[390]{0:T(512)S(1)} %bitcast.190, s32[390]{0:T(512)S(1)} %reshape.734, s32[]{:T(128)} %constant.277.clone.1), kind=kCustom, calls=%fused_computation.213 | custom fusion | bytes 2052 | tf_op jit(solution)/shard_map/scatter | solution.py:213
  34.6 0.8 slice.109
  35.4 4.3 %compare_select_fusion.5 = s32[256,1]{0,1:T(1,128)S(1)} fusion(s32[]{:T(128)} %bitcast.8, s32[]{:T(128)} %bitcast.9, s32[]{:T(128)} %bitcast.10, s32[]{:T(128)} %bitcast.11, s32[]{:T(128)} %bitcast.12, s32[]{:T(128)} %bitcast.14, s32[]{:T(128)} %bitcast.13), kind=kLoop, calls=%fused_computation.135 | loop fusion | flops 11264 | bytes 1052 | tf_op jit(solution)/shard_map/gather | solution.py:49
  39.7 5.0 %fusion.100 = (f32[64]{0:T(128)S(1)}, s32[64]{0:T(128)S(1)}) fusion(s32[]{:T(128)S(6)} %mul.333, s32[]{:T(128)} %bitcast.14, s32[]{:T(128)} %bitcast.13, s32[]{:T(128)} %bitcast.12, s32[]{:T(128)} %bitcast.11, s32[]{:T(128)} %bitcast.10, s32[]{:T(128)} %bitcast.9, s32[]{:T(128)} %bitcast.8, s32[]{:T(128)} %bitcast.7), kind=kLoop, calls=%fused_computation.235 | loop fusion | flops 5120 | bytes 548 | tf_op jit(solution)/shard_map/convert_element_type | solution.py:31
  44.7 1.0 fusion.57
  45.7 0.9 copy.104
  46.7 8.5 %all-gather = bf16[256,576]{1,0:T(8,128)(2,1)S(1)} all-gather(bf16[64,576]{1,0:T(8,128)(2,1)S(1)} %pad_maximum_fusion), channel_id=2, replica_groups=mesh['ctx'=4,'req'=32] {'ctx'}, dimensions={0}, use_global_device_ids=true | all-gather | bytes 368640 | tf_op jit(solution)/shard_map/all_gather | solution.py:112
  55.2 0.2 copy.103
  55.4 0.7 fusion.80
  56.1 0.1 fusion.42
  56.3 0.5 fusion.104
  56.8 0.3 fusion.38
  57.1 1.2 fusion.18
  58.2 6.7 %all-gather.4 = f32[4,4,8]{2,1,0:T(4,128)S(1)} all-gather(f32[1,4,8]{2,1,0:T(4,128)S(1)} %bitcast.188), channel_id=3, replica_groups=mesh['ctx'=4,'req'=32] {'ctx'}, dimensions={0}, use_global_device_ids=true | all-gather | bytes 640 | tf_op jit(solution)/shard_map/all_gather | solution.py:18
  64.9 6.7 %all-gather.5 = f32[4,4,8]{2,1,0:T(4,128)S(1)} all-gather(f32[1,4,8]{2,1,0:T(4,128)S(1)} %bitcast.189), channel_id=4, replica_groups=mesh['ctx'=4,'req'=32] {'ctx'}, dimensions={0}, use_global_device_ids=true | all-gather | bytes 640 | tf_op jit(solution)/shard_map/all_gather | solution.py:18
  71.5 7.3 %all-gather.3 = f32[16,8,512]{2,1,0:T(8,128)S(1)} all-gather(f32[4,8,512]{2,1,0:T(8,128)S(1)} %fusion.11), channel_id=5, replica_groups=mesh['ctx'=4,'req'=32] {'ctx'}, dimensions={0}, use_global_device_ids=true | all-gather | bytes 327680 | tf_op jit(solution)/shard_map/all_gather | solution.py:18
  78.8 0.4 while.19
  79.5 1.7 fusion.25
  81.4 3.2 %multiply_reduce_fusion.1 = (f32[65]{0:T(128)S(1)}, f32[65,2048]{1,0:T(8,128)S(1)}) fusion(bf16[65,1024]{1,0:T(8,128)(2,1)S(1)} %bitcast.179, bf16[1024,2048]{1,0:T(8,128)(2,1)} %param.35, bf16[1,2048]{1,0:T(2,128)(2,1)S(1)} %dynamic-slice_bitcast_fusion, bf16[64,2048]{1,0:T(8,128)(2,1)} %bitcast.182), kind=kOutput, calls=%fused_computation.57 | convolution fusion | flops 273561536 | bytes 5126404 | tf_op jit(solution)/shard_map/dot_general | solution.py:187
  84.6 0.8 copy-done.3
  85.6 3.3 %gather_fusion.1 = bf16[512,2048]{1,0:T(8,128)(2,1)} fusion(bf16[66,2048]{1,0:T(8,128)(2,1)S(1)} %concatenate.39, s32[1024]{0:T(1024)S(1)} %pad_clamp_fusion.1), kind=kCustom, calls=%fused_computation.1 | custom fusion | bytes 4196352 | tf_op jit(solution)/shard_map/gather | solution.py:216
  88.9 2.1 broadcast_in_dim.129
  91.0 65.2 %all_to_all.10 = bf16[128,8,2048]{2,1,0:T(8,128)(2,1)S(1)} all-to-all(bf16[128,8,2048]{2,1,0:T(8,128)(2,1)S(1)} %bitcast.175), channel_id=1, replica_groups=mesh['ctx'=4,'req'=32] {'ctx','req'}, dimensions={0} | all-to-all | bytes 8388608 | tf_op jit(solution)/shard_map/all_to_all | solution.py:221
  156.3 2.0 copy-done.5
  158.2 4.8 %fusion.5 = f32[1024,704]{0,1:T(8,128)} fusion(bf16[128,8,2048]{2,1,0:T(8,128)(2,1)S(1)} %all_to_all.10, bf16[1,2048,704]{1,2,0:T(8,128)(2,1)S(1)} %copy-done.15), kind=kOutput, calls=%fused_computation.19 | convolution fusion | flops 2952790016 | bytes 9961472 | tf_op jit(solution)/shard_map/dot_general | solution.py:54
  163.1 11.1 %convert_bitcast_fusion = bf16[128,8,2048]{2,1,0:T(8,128)(2,1)} fusion(bf16[1,704,2048]{2,1,0:T(8,128)(2,1)S(1)} %copy-done, f32[1024,704]{0,1:T(8,128)} %fusion.5, bf16[1,2048,704]{1,2,0:T(8,128)(2,1)} %param.40, bf16[128,8,2048]{2,1,0:T(8,128)(2,1)} %copy-done.5), kind=kOutput, calls=%fused_computation.22 | convolution fusion | flops 5912002560 | bytes 17039360 | tf_op jit(solution)/shard_map/dot_general | solution.py:57
  174.2 5.0 %all-to-all-start.1 = ((bf16[128,8,2048]{2,1,0:T(8,128)(2,1)}), bf16[128,8,2048]{2,1,0:T(8,128)(2,1)}, u32[]{:S(2)}, u32[]{:S(2)}) async-start(bf16[128,8,2048]{2,1,0:T(8,128)(2,1)} %convert_bitcast_fusion), calls=%async_computation.1 | async-start | bytes 8388608 | tf_op jit(solution)/shard_map/all_to_all | solution.py:226
  179.2 1.5 fusion.29
  180.6 4.8 %gather_fusion.4 = f32[390]{0:T(512)S(1)} fusion(f32[65,64]{0,1:T(8,128)S(1)} %fusion.29, s32[390]{0:T(512)S(1)} %reshape.710), kind=kCustom, calls=%fused_computation.4 | custom fusion | bytes 6240 | tf_op jit(solution)/shard_map/jit(take_along_axis)/gather | solution.py:197
  185.8 47.4 %all-to-all-done.1 = bf16[128,8,2048]{2,1,0:T(8,128)(2,1)} async-done(((bf16[128,8,2048]{2,1,0:T(8,128)(2,1)}), bf16[128,8,2048]{2,1,0:T(8,128)(2,1)}, u32[]{:S(2)}, u32[]{:S(2)}) %all-to-all-start.1) | async-done | bytes 4194336 | tf_op jit(solution)/shard_map/all_to_all | solution.py:226
  233.2 4.5 %fusion.10 = bf16[512,2048]{1,0:T(8,128)(2,1)} fusion(bf16[64,2,8,2048]{3,2,1,0:T(8,128)(2,1)} %bitcast.53), kind=kLoop, calls=%fused_computation.28 | loop fusion | flops 4194304 | bytes 6291456 | tf_op jit(solution)/shard_map/convert_element_type | solution.py:229
  237.6 6.9 %gather_fusion.2 = bf16[390,2048]{1,0:T(8,128)(2,1)} fusion(bf16[512,2048]{1,0:T(8,128)(2,1)} %fusion.10, s32[1024]{0:T(1024)S(1)} %pad_clamp_fusion), kind=kCustom, calls=%fused_computation.2 | custom fusion | bytes 3196440 | tf_op jit(solution)/shard_map/gather | solution.py:232
  244.6 3.9 %reshape.647 = f32[65,6,2048]{2,1,0:T(8,128)} reshape(bf16[390,2048]{1,0:T(8,128)(2,1)} %gather_fusion.2) | data formatting | bytes 4792320 | tf_op jit(solution)/shard_map/convert_element_type | solution.py:235
  248.5 3.8 %multiply_reduce_fusion = f32[65,2048]{1,0:T(8,128)S(1)} fusion(f32[65,6,2048]{2,1,0:T(8,128)} %reshape.647, f32[65,6]{1,0:T(8,128)S(1)} %copy.89), kind=kLoop, calls=%fused_computation.16 | loop fusion | flops 1464320 | bytes 3728920 | tf_op jit(solution)/shard_map/reduce_sum | solution.py:235
  252.4 0.6 slice_bitcast_fusion.5
  253.0 0.7 slice_bitcast_fusion.2
  (95 shorter events, 2.8 us)
Async XLA Ops:
  0.6 162.4 %copy-start = (bf16[1,704,2048]{2,1,0:T(8,128)(2,1)S(1)}, bf16[1,704,2048]{2,1,0:T(8,128)(2,1)}, u32[]{:S(2)}) copy-start(bf16[1,704,2048]{2,1,0:T(8,128)(2,1)} %param.41) | copy-start | bytes 8650756
  0.6 3.7 %copy-start.12 = (bf16[4,1,576]{2,0,1:T(4,128)(2,1)S(1)}, bf16[4,1,576]{2,0,1:T(4,128)(2,1)}, u32[]{:S(2)}) copy-start(bf16[4,1,576]{2,0,1:T(4,128)(2,1)} %param.27) | copy-start | bytes 13828
  0.7 3.8 %copy-start.14 = (s32[4,1]{0,1:T(1,128)S(1)}, s32[4,1]{0,1:T(1,128)}, u32[]{:S(2)}) copy-start(s32[4,1]{0,1:T(1,128)} %param.31) | copy-start | bytes 52
  0.7 3.9 %copy-start.1 = (s32[4,1,8]{2,1,0:T(1,128)S(1)}, s32[4,1,8]{2,1,0:T(1,128)}, u32[]{:S(2)}) copy-start(s32[4,1,8]{2,1,0:T(1,128)} %param.32) | copy-start | bytes 388
  0.7 3.7 %copy-start.7 = (s32[65,6]{0,1:T(8,128)S(1)}, s32[65,6]{0,1:T(8,128)}, u32[]{:S(2)}) copy-start(s32[65,6]{0,1:T(8,128)} %param.38) | copy-start | bytes 4684
  10.1 11.6 %copy-start.9 = (bf16[4,1,8,64]{3,2,1,0:T(8,128)(2,1)S(1)}, bf16[4,1,8,64]{3,2,1,0:T(8,128)(2,1)}, u32[]{:S(2)}) copy-start(bf16[4,1,8,64]{3,2,1,0:T(8,128)(2,1)} %param.29) | copy-start | bytes 12292
  10.1 11.7 %copy-start.8 = (bf16[4,1,8,512]{3,2,1,0:T(8,128)(2,1)S(1)}, bf16[4,1,8,512]{3,2,1,0:T(8,128)(2,1)}, u32[]{:S(2)}) copy-start(bf16[4,1,8,512]{3,2,1,0:T(8,128)(2,1)} %param.28) | copy-start | bytes 98308
  21.7 2.8 %copy-start.2 = (bf16[2048,576]{1,0:T(8,128)(2,1)S(1)}, bf16[2048,576]{1,0:T(8,128)(2,1)}, u32[]{:S(2)}) copy-start(bf16[2048,576]{1,0:T(8,128)(2,1)} %gather_fusion) | copy-start | bytes 7077892
  21.7 3.5 %copy-start.10 = (s32[8]{0:T(128)S(1)}, s32[8]{0:T(128)}, u32[]{:S(2)}) copy-start(s32[8]{0:T(128)} %param.26) | copy-start | bytes 100
  26.3 28.9 %copy-start.6 = (bf16[1,64,8,512]{3,2,1,0:T(8,128)(2,1)S(1)}, bf16[1,64,8,512]{3,2,1,0:T(8,128)(2,1)}, u32[]{:S(2)}) copy-start(bf16[1,64,8,512]{3,2,1,0:T(8,128)(2,1)} %param.23) | copy-start | bytes 1572868
  57.0 22.3 %copy-start.13 = (bf16[4,1,2048]{2,0,1:T(4,128)(2,1)S(1)}, bf16[4,1,2048]{2,0,1:T(4,128)(2,1)}, u32[]{:S(2)}) copy-start(bf16[4,1,2048]{2,0,1:T(4,128)(2,1)} %param.30) | copy-start | bytes 49156
  81.3 4.1 %copy-start.11 = (f32[2048]{0:T(1024)S(1)}, f32[2048]{0:T(1024)}, u32[]{:S(2)}) copy-start(f32[2048]{0:T(1024)} %param.36) | copy-start | bytes 24580
  84.6 0.8 copy-start.3
  91.0 67.2 %copy-start.15 = (bf16[1,2048,704]{1,2,0:T(8,128)(2,1)S(1)}, bf16[1,2048,704]{1,2,0:T(8,128)(2,1)}, u32[]{:S(2)}) copy-start(bf16[1,2048,704]{1,2,0:T(8,128)(2,1)} %param.39) | copy-start | bytes 8650756
  156.3 2.0 copy-start.5
  174.2 59.0 %all-to-all-start.1 = ((bf16[128,8,2048]{2,1,0:T(8,128)(2,1)}), bf16[128,8,2048]{2,1,0:T(8,128)(2,1)}, u32[]{:S(2)}, u32[]{:S(2)}) async-start(bf16[128,8,2048]{2,1,0:T(8,128)(2,1)} %convert_bitcast_fusion), calls=%async_computation.1 | async-start | bytes 8388608 | tf_op jit(solution)/shard_map/all_to_all | solution.py:226
  248.5 3.9 %copy-start.4 = (f32[65,2048]{1,0:T(8,128)S(1)}, f32[65,2048]{1,0:T(8,128)}, u32[]{:S(2)}) copy-start(f32[65,2048]{1,0:T(8,128)} %copy-done.3) | copy-start | bytes 1597444
where the time goes:
time: 255 us; the launch traced here: 254 us
  blocking collectives  94.3 us (37%)
  local copies, waits for them, and re-layouts  53.1 us (21%)
  waiting for transfers between devices  47.4 us (19%)
  matrix products  27.2 us (11%)
  other arithmetic  25.6 us (10%)
  starting transfers between devices  4.98 us (2%)
    all_to_all x1, blocking collectives, body(): lax.all_to_all(doubled, ('ctx', 'req'), split_axis=0, concat_axis=0, tile...  65.2 us
    all_to_all x1, waiting for transfers between devices, body(): lax.all_to_all(partial_out, ('ctx', 'req'), split_axis=0, concat_axis=0,...  47.4 us
    all_gather x3, blocking collectives, joined(): gathered = jax.tree.map(lambda a: lax.all_gather(a, axis), part)  20.6 us
    gather x1, local copies, waits for them, and re-layouts, body(): cached = flat_pool[gather_rows]  11.6 us
    dot_general x1, matrix products, expert_half(): jnp.dot(hidden, down_part, preferred_element_type=jnp.float32)  11.1 us
    all_gather x1, blocking collectives, body(): moving = lax.all_gather(stored, 'ctx', axis=1, tiled=True)[0]  8.47 us
    unnamed x39, local copies, waits for them, and re-layouts  7.59 us
    gather x1, local copies, waits for them, and re-layouts, body(): results.reshape(expert_count * capacity, width)[target_slot]  6.94 us
  transfers between devices with their start and end apart: 1, of which 1 were waited for; matrix products, arithmetic and copies ran while one was open for 3% of the time, Pallas kernels for 0%

commit v1 on v0

--- a/solution.py
+++ b/solution.py
@@ -102,21 +102,97 @@
     own_pos = block_position(block_order, ctx_index * shard_rows + local_rows, shard_rows)
     cos_table, sin_table = rope_tables(own_pos, DR)
     key_rope = rotate(latent[:, DC:], cos_table, sin_table).astype(jnp.bfloat16)
-    stored = jnp.concatenate([latent[:, :DC], key_rope], axis=-1)[None]
+    stored = jnp.concatenate([latent[:, :DC], key_rope], axis=-1)
     rotated = rotate(pre_qrope[0], cos_table[:, None, :], sin_table[:, None, :]).astype(
         jnp.bfloat16
     )
     queries = jnp.concatenate([pre_qlat[0], rotated], axis=-1)
     head_count = queries.shape[1]
-    running_max = jnp.full((head_count, shard_rows), NEG_FILL, jnp.float32)
-    moving = lax.all_gather(stored, "ctx", axis=1, tiled=True)[0]
-    key_pos = block_position(block_order, jnp.arange(moving.shape[0]), shard_rows)
+
+    lengths = cache_len[:, 0]
+    tables = page_table[:, 0, :]
+    request_count = tables.shape[0]
+    pages_dev = tables.shape[1]
+    page_rows = cache_pool.shape[1]
+    slot_count = cache_pool.shape[0]
+    row_width = cache_pool.shape[2]
+    cos_new, sin_new = rope_tables(lengths, DR)
+    new_rope = rotate(dec_new[:, 0, DC:], cos_new, sin_new).astype(jnp.bfloat16)
+    new_rows = jnp.concatenate([dec_new[:, 0, :DC], new_rope], axis=-1)
+    page_index = lengths // page_rows
+    owner_ctx = page_index // pages_dev
+    page_hit = tables[:, :, None] == jnp.arange(slot_count)[None, None, :]
+    slot_of = jnp.sum(
+        jnp.where((jnp.arange(pages_dev)[None, :] == (page_index % pages_dev)[:, None])[:, :, None],
+                  page_hit, False).astype(jnp.int32) * jnp.arange(slot_count)[None, None, :],
+        axis=(1, 2),
+    )
+    flat_pool = cache_pool.reshape(slot_count * page_rows, row_width)
+    for request in range(request_count):
+        owned = owner_ctx[request] == ctx_index
+        spot = jnp.where(owned, slot_of[request] * page_rows + lengths[request] % page_rows, 0)
+        old_row = lax.dynamic_slice_in_dim(flat_pool, spot, 1, 0)
+        row = jnp.where(owned, new_rows[request][None], old_row)
+        flat_pool = lax.dynamic_update_slice_in_dim(flat_pool, row, spot, 0)
+    page_valid = jnp.any(page_hit, axis=1)
+    page_logical = jnp.sum(page_hit.astype(jnp.int32) * jnp.arange(pages_dev)[None, :, None], axis=1)
+    page_start = (ctx_index * pages_dev + page_logical) * page_rows
+    key_pos = (page_start[:, :, None] + jnp.arange(page_rows)[None, None, :]).reshape(
+        request_count, slot_count * page_rows
+    )
+    dec_visible = (
+        jnp.repeat(page_valid, page_rows, axis=1) & (key_pos <= lengths[:, None])
+    )[:, None, :]
+    query_rot = rotate(dec_qrope[:, 0], cos_new[:, None, :], sin_new[:, None, :]).astype(
+        jnp.bfloat16
+    )
+    dec_queries = jnp.concatenate([dec_qlat[:, 0], query_rot], axis=-1)
+    dec_scores = (
+        jnp.einsum("rhd,kd->rhk", dec_queries, flat_pool, preferred_element_type=jnp.float32)
+        * score_scale
+    )
+    dec_masked = jnp.where(dec_visible, dec_scores, NEG_FILL)
+    local_peak = jnp.max(dec_masked, axis=-1)
+    dec_weights = jnp.where(dec_visible, jnp.exp(dec_masked - local_peak[..., None]), 0.0)
+    local_total = jnp.sum(dec_weights, axis=-1)
+    local_accum = jnp.einsum(
+        "rhk,kc->rhc",
+        dec_weights.astype(jnp.bfloat16),
+        flat_pool[:, :DC],
+        preferred_element_type=jnp.float32,
+    )
+
+    dec_block = jnp.concatenate(
+        [
+            local_accum.reshape(request_count * head_count, DC),
+            local_peak.reshape(-1, 1),
+            local_total.reshape(-1, 1),
+            jnp.zeros((request_count * head_count, row_width - DC - 2), jnp.float32),
+        ],
+        axis=1,
+    )
+    packed = jnp.concatenate([stored.astype(jnp.float32), dec_block], axis=0)
+    gathered = lax.all_gather(packed, "ctx")
+    moving = gathered[:, :shard_rows].reshape(ctx_count * shard_rows, row_width).astype(jnp.bfloat16)
+    dec_parts = gathered[:, shard_rows:].reshape(ctx_count, request_count, head_count, row_width)
+    dec_share = request_count // ctx_count
+    own_parts = lax.dynamic_slice_in_dim(dec_parts, ctx_index * dec_share, dec_share, 1)
+    part_accum = own_parts[..., :DC]
+    part_peak = own_parts[..., DC]
+    part_total = own_parts[..., DC + 1]
+    merged_peak = jnp.max(part_peak, axis=0)
+    factor = jnp.exp(part_peak - merged_peak[None])
+    merged_total = jnp.sum(part_total * factor, axis=0)
+    merged_accum = jnp.sum(part_accum * factor[..., None], axis=0)
+    own_mixed = (merged_accum / merged_total[..., None]).astype(jnp.bfloat16)
+
+    key_pos_pre = block_position(block_order, jnp.arange(moving.shape[0]), shard_rows)
     scores = (
         jnp.einsum("qhd,kd->hqk", queries, moving, preferred_element_type=jnp.float32) * score_scale
     )
-    visible = (key_pos[None, :] <= own_pos[:, None])[None]
+    visible = (key_pos_pre[None, :] <= own_pos[:, None])[None]
     masked = jnp.where(visible, scores, NEG_FILL)
-    new_peak = jnp.maximum(running_max, jnp.max(masked, axis=-1))
+    new_peak = jnp.max(masked, axis=-1)
     weights = jnp.where(visible, jnp.exp(masked - new_peak[..., None]), 0.0)
     totals = jnp.sum(weights, axis=-1)
     accumulated = jnp.einsum(
@@ -125,59 +201,8 @@
         moving[:, :DC],
         preferred_element_type=jnp.float32,
     )
-    running_max, totals, accumulated = (new_peak, totals, accumulated)
     pre_mixed = (accumulated / jnp.transpose(totals)[:, :, None]).astype(jnp.bfloat16)
-    lengths = cache_len[:, 0]
-    tables = page_table[:, 0, :]
-    request_count = tables.shape[0]
-    pages_dev = tables.shape[1]
-    page_rows = cache_pool.shape[1]
-    slot_count = cache_pool.shape[0]
-    window_rows = pages_dev * page_rows
-    cos_new, sin_new = rope_tables(lengths, DR)
-    new_rope = rotate(dec_new[:, 0, DC:], cos_new, sin_new).astype(jnp.bfloat16)
-    new_rows = jnp.concatenate([dec_new[:, 0, :DC], new_rope], axis=-1)
-    page_index = lengths // page_rows
-    owner_ctx = page_index // pages_dev
-    slot_of = jnp.take_along_axis(tables, (page_index % pages_dev)[:, None], axis=1)[:, 0]
-    target = jnp.where(
-        owner_ctx == ctx_index, slot_of * page_rows + lengths % page_rows, slot_count * page_rows
-    )
-    flat_pool = (
-        cache_pool.reshape(slot_count * page_rows, cache_pool.shape[2])
-        .at[target]
-        .set(new_rows, mode="drop")
-    )
-    gather_rows = (tables[:, :, None] * page_rows + jnp.arange(page_rows)[None, None, :]).reshape(
-        request_count, window_rows
-    )
-    cached = flat_pool[gather_rows]
-    cache_pos = ctx_index * window_rows + jnp.arange(window_rows)
-    query_rot = rotate(dec_qrope[:, 0], cos_new[:, None, :], sin_new[:, None, :]).astype(
-        jnp.bfloat16
-    )
-    dec_queries = jnp.concatenate([dec_qlat[:, 0], query_rot], axis=-1)
-    dec_scores = (
-        jnp.einsum("rhd,rkd->rhk", dec_queries, cached, preferred_element_type=jnp.float32)
-        * score_scale
-    )
-    dec_visible = (cache_pos[None, :] <= lengths[:, None])[:, None, :]
-    dec_masked = jnp.where(dec_visible, dec_scores, NEG_FILL)
-    local_peak = jnp.max(dec_masked, axis=-1)
-    dec_weights = jnp.where(dec_visible, jnp.exp(dec_masked - local_peak[..., None]), 0.0)
-    local_total = jnp.sum(dec_weights, axis=-1)
-    local_accum = jnp.einsum(
-        "rhk,rkc->rhc",
-        dec_weights.astype(jnp.bfloat16),
-        cached[:, :, :DC],
-        preferred_element_type=jnp.float32,
-    )
-    merged_peak, merged_total, merged_accum = joined(
-        (local_peak, local_total, local_accum), "ctx", merge_softmax
-    )
-    dec_mixed = (merged_accum / merged_total[..., None]).astype(jnp.bfloat16)
-    dec_share = request_count // ctx_count
-    own_mixed = lax.dynamic_slice_in_dim(dec_mixed, ctx_index * dec_share, dec_share, 0)
+
     own_resid = lax.dynamic_slice_in_dim(dec_resid[:, 0], ctx_index * dec_share, dec_share, 0)
     mixed_all = jnp.concatenate([pre_mixed, own_mixed], axis=0)
     resid_all = jnp.concatenate([pre_resid[0], own_resid], axis=0)
@@ -194,26 +219,27 @@
     ).astype(jnp.bfloat16)
     logits = jnp.dot(normed.astype(jnp.float32), router, precision=lax.Precision.HIGHEST)
     probable = jax.nn.sigmoid(logits)
-    chosen = jnp.take_along_axis(probable, routes, axis=1)
-    mixing = ROUTE_SCALE * chosen / jnp.sum(chosen, axis=1, keepdims=True)
     row_count = normed.shape[0]
     width = normed.shape[1]
     top_count = routes.shape[1]
     expert_count = router.shape[1]
     devices = ctx_count * lax.axis_size("req")
     capacity = 2 * ((row_count * top_count + 2 * expert_count - 1) // (2 * expert_count))
-    expert_hits = (
-        (routes[:, :, None] == jnp.arange(expert_count)[None, None, :]).astype(jnp.int32).sum(1)
-    )
-    before = jnp.cumsum(expert_hits, axis=0) - expert_hits
-    slot_index = jnp.take_along_axis(before, routes, axis=1)
-    target_slot = (routes * capacity + slot_index).reshape(-1)
-    row_ids = jnp.repeat(jnp.arange(row_count), top_count)
-    slot_table = (
-        jnp.full((expert_count * capacity,), row_count, jnp.int32).at[target_slot].set(row_ids)
-    )
-    padded = jnp.concatenate([normed, jnp.zeros((1, width), jnp.bfloat16)], axis=0)
-    outgoing = padded[slot_table].reshape(expert_count, capacity, width)
+    route_hit = routes[:, :, None] == jnp.arange(expert_count)[None, None, :]
+    chosen = jnp.sum(jnp.where(route_hit, probable[:, None, :], 0.0), axis=-1)
+    mixing = ROUTE_SCALE * chosen / jnp.sum(chosen, axis=1, keepdims=True)
+    expert_hits = route_hit.astype(jnp.int32).sum(1)
+    earlier = (jnp.arange(row_count)[None, :] < jnp.arange(row_count)[:, None]).astype(jnp.bfloat16)
+    before = jnp.dot(
+        earlier, expert_hits.astype(jnp.bfloat16), preferred_element_type=jnp.float32
+    ).astype(jnp.int32)
+    slot_index = jnp.sum(jnp.where(route_hit, before[:, None, :], 0), axis=-1)
+    target_slot = routes * capacity + slot_index
+    slot_hit = target_slot[:, :, None] == jnp.arange(expert_count * capacity)[None, None, :]
+    dispatch = jnp.any(slot_hit, axis=1).astype(jnp.bfloat16)
+    outgoing = lax.dot_general(
+        dispatch, normed, (((0,), (0,)), ((), ())), preferred_element_type=jnp.float32
+    ).astype(jnp.bfloat16).reshape(expert_count, capacity, width)
     doubled = jnp.broadcast_to(outgoing[:, None], (expert_count, 2, capacity, width)).reshape(
         devices, capacity, width
     )
@@ -228,11 +254,9 @@
     ).reshape(expert_count, 2, capacity, width)
     results = (returned[:, 0].astype(jnp.float32) + returned[:, 1].astype(jnp.float32)).astype(
         jnp.bfloat16
-    )
-    picked = results.reshape(expert_count * capacity, width)[target_slot].reshape(
-        row_count, top_count, width
-    )
-    moe = jnp.sum(mixing[:, :, None] * picked.astype(jnp.float32), axis=1)
+    ).reshape(expert_count * capacity, width)
+    combine = jnp.sum(jnp.where(slot_hit, mixing[:, :, None], 0.0), axis=1)
+    moe = jnp.dot(combine, results.astype(jnp.float32), precision=lax.Precision.HIGHEST)
     final = (hidden_state + moe).astype(jnp.bfloat16)
     pre_out = final[:shard_rows][None]
     dec_out = final[shard_rows:][:, None]

time: 255 us -> 227 us (0.89)
  local copies, waits for them, and re-layouts: 53.1 us -> 22.1 us
  blocking collectives: 94.3 us -> 77 us
  between operations: 1.14 us -> 14 us
  matrix products: 27.2 us -> 36.9 us
  other arithmetic: 25.6 us -> 18.9 us
  waiting for transfers between devices: 47.4 us -> 51.8 us
    gather x12 -> x0, local copies, waits for them, and re-layouts: 32.6 us -> none  [the longest x1 11.6 us: body(): cached = flat_pool[gather_rows]]
    all_gather x4 -> x1, blocking collectives: 29.1 us -> 12 us  [body(): gathered = lax.all_gather(packed, 'ctx')]
    dot_general x2 -> x5, matrix products: 3.19 us -> 8.56 us  [the longest x1 3.67 us: body(): jnp.dot(combine, results.astype(jnp.float32), precision=lax.Precision.HIG...]
    dynamic_update_slice x0 -> x4, local copies, waits for them, and re-layouts: none -> 5.3 us  [body(): flat_pool = lax.dynamic_update_slice_in_dim(flat_pool, row, spot, 0)]
    convert_element_type x4 -> x2, other arithmetic: 4.75 us -> 0.17 us  [the longest x1 0.09 us: body(): own_mixed = (merged_accum / merged_total[..., None]).astype(jnp.bfloat16)]
    scatter x1 -> x0, other arithmetic: 4.46 us -> none  [body(): flat_pool = cache_pool.reshape(slot_count * page_rows, cache_pool.shape[2...]
    all_to_all x1, waiting for transfers between devices: 47.4 us -> 51.8 us  [body(): lax.all_to_all(partial_out, ('ctx', 'req'), split_axis=0, concat_axis=0,...]
    convert_element_type x1 -> x0, local copies, waits for them, and re-layouts: 3.92 us -> none  [body(): moe = jnp.sum(mixing[:, :, None] * picked.astype(jnp.float32), axis=1)]
  transfers between devices with their start and end apart: 1 -> 1, of which waited for: 1 -> 1; matrix products, arithmetic and copies ran while one was open for 3% -> 1% of each run, Pallas kernels for 0% -> 0%
where the time goes in v1:
time: 227 us; the launch traced here: 225 us
  blocking collectives  77 us (34%)
  waiting for transfers between devices  51.8 us (23%)
  matrix products  36.9 us (16%)
  local copies, waits for them, and re-layouts  22.1 us (10%)
  other arithmetic  18.9 us (8%)
  between operations  14 us (6%)
  starting transfers between devices  4.76 us (2%)
    all_to_all x1, blocking collectives, body(): lax.all_to_all(doubled, ('ctx', 'req'), split_axis=0, concat_axis=0, tile...  65 us
    all_to_all x1, waiting for transfers between devices, body(): lax.all_to_all(partial_out, ('ctx', 'req'), split_axis=0, concat_axis=0,...  51.8 us
    all_gather x1, blocking collectives, body(): gathered = lax.all_gather(packed, 'ctx')  12 us
    dot_general x1, matrix products, expert_half(): jnp.dot(hidden, down_part, preferred_element_type=jnp.float32)  11.1 us
    unnamed x49, local copies, waits for them, and re-layouts  6.85 us
    dynamic_update_slice x4, local copies, waits for them, and re-layouts, body(): flat_pool = lax.dynamic_update_slice_in_dim(flat_pool, row, spot, 0)  5.3 us
    convert_element_type x1, other arithmetic, rope_tables(): angles = positions.astype(jnp.float32)[..., None] * inverse  4.97 us
    gather x2, other arithmetic, block_position(): block_order[2 * shard_id + within // half_rows] * half_rows  4.92 us
  transfers between devices with their start and end apart: 1, of which 1 were waited for; matrix products, arithmetic and copies ran while one was open for 1% of the time, Pallas kernels for 0%

profile of v1, /device:TPU:8, one launch (start us, length us, event | category | flops | bytes accessed | tf_op | source)
XLA Modules:
  0.0 225.5 jit_solution(10079078876404796633)
XLA Ops:
  0.7 3.6 %copy.76 = bf16[32,64,576]{2,1,0:T(8,128)(2,1)} copy(bf16[32,64,576]{2,1,0:T(8,128)(2,1)} %param.31) | data formatting | bytes 4718592
  4.3 0.7 fusion.115
  9.1 0.2 select_reduce_fusion.5
  9.3 0.7 fusion.116
  10.0 0.6 fusion.117
  19.8 0.7 broadcast_select_fusion.3
  20.6 1.3 dynamic_update_slice.12
  21.9 0.7 broadcast_select_fusion.2
  22.6 1.3 dynamic_update_slice.13
  23.9 0.7 broadcast_select_fusion.1
  24.6 1.3 dynamic_update_slice.14
  26.0 0.7 broadcast_select_fusion
  26.7 1.3 dynamic_update_slice.15
  28.6 2.8 %fusion.118 = (f32[4,8]{1,0:T(4,128)S(1)}, f32[4,8,2048]{2,1,0:T(8,128)S(1)}) fusion(bf16[2048,576]{1,0:T(8,128)(2,1)} %dynamic_update_slice.15, bf16[4,8,32]{2,1,0:T(8,128)(2,1)S(1)} %get-tuple-element.17, bf16[4,8,32]{2,1,0:T(8,128)(2,1)S(1)} %get-tuple-element.16, bf16[4,8,512]{2,1,0:T(8,128)(2,1)S(1)} %bitcast.178, pred[4,2048]{1,0:T(4,128)(4,1)S(1)} %fusion.73), kind=kOutput, calls=%fused_computation.239 | convolution fusion | flops 75804640 | bytes 2666624 | tf_op jit(solution)/shard_map/rhd,kd->rhk/dot_general | solution.py:151
  31.5 1.1 fusion.39
  32.7 0.8 fusion.57
  33.5 0.8 reshape.785
  34.2 0.6 compare_reduce_fusion
  34.8 1.4 reshape.786
  36.2 1.6 fusion.114
  37.8 0.8 slice.178
  38.7 4.3 %compare_select_fusion.1 = s32[256,1]{0,1:T(1,128)S(1)} fusion(s32[]{:T(128)} %bitcast.5, s32[]{:T(128)} %bitcast.6, s32[]{:T(128)} %bitcast.7, s32[]{:T(128)} %bitcast.8, s32[]{:T(128)} %bitcast.9, s32[]{:T(128)} %bitcast.11, s32[]{:T(128)} %bitcast.10), kind=kLoop, calls=%fused_computation.135 | loop fusion | flops 11264 | bytes 1052 | tf_op jit(solution)/shard_map/gather | solution.py:49
  43.0 5.0 %fusion.112 = (f32[64]{0:T(128)S(1)}, s32[64]{0:T(128)S(1)}) fusion(s32[]{:T(128)S(6)} %mul.309, s32[]{:T(128)} %bitcast.11, s32[]{:T(128)} %bitcast.10, s32[]{:T(128)} %bitcast.9, s32[]{:T(128)} %bitcast.8, s32[]{:T(128)} %bitcast.7, s32[]{:T(128)} %bitcast.6, s32[]{:T(128)} %bitcast.5, s32[]{:T(128)} %bitcast.4), kind=kLoop, calls=%fused_computation.234 | loop fusion | flops 5120 | bytes 548 | tf_op jit(solution)/shard_map/convert_element_type | solution.py:31
  47.9 1.0 multiply_cosine_fusion
  49.0 0.9 maximum_maximum_fusion
  50.0 12.0 %all-gather = f32[384,576]{1,0:T(8,128)S(1)} all-gather(f32[96,576]{1,0:T(8,128)S(1)} %maximum_maximum_fusion), channel_id=2, replica_groups=mesh['ctx'=4,'req'=32] {'ctx'}, dimensions={0}, use_global_device_ids=true | all-gather | bytes 1105920 | tf_op jit(solution)/shard_map/all_gather | solution.py:175
  62.0 1.0 copy-done.3
  63.2 0.7 fusion.90
  64.2 1.2 fusion.33
  65.4 2.4 %fusion.119 = f32[8,64]{1,0:T(8,128)} fusion(bf16[256,576,1]{1,0,2:T(8,128)(2,1)} %bitcast.173, bf16[64,8,32]{2,0,1:T(8,128)(2,1)S(1)} %get-tuple-element.13, bf16[64,8,32]{2,0,1:T(8,128)(2,1)S(1)} %get-tuple-element.12, bf16[64,8,512]{2,0,1:T(8,128)(2,1)} %bitcast.171, pred[64,256]{1,0:T(8,128)(4,1)S(1)} %broadcast_compare_fusion), kind=kOutput, calls=%fused_computation.240 | convolution fusion | flops 153420032 | bytes 903168 | tf_op jit(solution)/shard_map/sub | solution.py:196
  67.8 1.0 slice_bitcast_fusion.4
  69.3 2.4 %fusion.28 = bf16[64,8,512]{2,0,1:T(8,128)(2,1)} fusion(f32[64,8]{0,1:T(8,128)} %bitcast.184, bf16[256,576]{1,0:T(8,128)(2,1)S(1)} %bitcast.174, f32[8,64,256]{2,1,0:T(8,128)} %fusion.33, pred[64,256]{1,0:T(8,128)(4,1)S(1)} %broadcast_compare_fusion), kind=kOutput, calls=%fused_computation.27 | convolution fusion | flops 135136000 | bytes 1855488 | tf_op jit(solution)/shard_map/hqk,kc->qhc/dot_general | solution.py:198
  71.7 1.8 fusion.38
  73.6 3.2 %multiply_reduce_fusion = (f32[65]{0:T(128)S(1)}, f32[65,2048]{1,0:T(8,128)S(1)}) fusion(bf16[65,1024]{1,0:T(8,128)(2,1)S(1)} %bitcast.168, bf16[1024,2048]{1,0:T(8,128)(2,1)} %param.33, bf16[1,2048]{1,0:T(2,128)(2,1)S(1)} %dynamic-slice_bitcast_fusion, bf16[64,2048]{1,0:T(8,128)(2,1)S(1)} %bitcast.175), kind=kOutput, calls=%fused_computation.55 | convolution fusion | flops 273561536 | bytes 5126404 | tf_op jit(solution)/shard_map/dot_general | solution.py:212
  77.1 0.2 fusion.43
  77.2 0.8 fusion.8
  78.0 0.5 broadcast_in_dim.160
  78.6 65.0 %all_to_all.10 = bf16[128,8,2048]{2,1,0:T(8,128)(2,1)S(1)} all-to-all(bf16[128,8,2048]{2,1,0:T(8,128)(2,1)S(1)} %bitcast.161), channel_id=1, replica_groups=mesh['ctx'=4,'req'=32] {'ctx','req'}, dimensions={0} | all-to-all | bytes 8388608 | tf_op jit(solution)/shard_map/all_to_all | solution.py:247
  143.6 2.0 copy-done.2
  145.5 4.8 %fusion.3 = f32[1024,704]{0,1:T(8,128)} fusion(bf16[128,8,2048]{2,1,0:T(8,128)(2,1)S(1)} %all_to_all.10, bf16[1,2048,704]{1,2,0:T(8,128)(2,1)S(1)} %copy-done.21), kind=kOutput, calls=%fused_computation.3 | convolution fusion | flops 2952790016 | bytes 9961472 | tf_op jit(solution)/shard_map/dot_general | solution.py:54
  150.4 11.1 %convert_bitcast_fusion = bf16[128,8,2048]{2,1,0:T(8,128)(2,1)} fusion(bf16[1,704,2048]{2,1,0:T(8,128)(2,1)S(1)} %copy-done, f32[1024,704]{0,1:T(8,128)} %fusion.3, bf16[1,2048,704]{1,2,0:T(8,128)(2,1)} %param.38, bf16[128,8,2048]{2,1,0:T(8,128)(2,1)} %copy-done.2), kind=kOutput, calls=%fused_computation.6 | convolution fusion | flops 5912002560 | bytes 17039360 | tf_op jit(solution)/shard_map/dot_general | solution.py:57
  161.5 4.8 %all-to-all-start.1 = ((bf16[128,8,2048]{2,1,0:T(8,128)(2,1)}), bf16[128,8,2048]{2,1,0:T(8,128)(2,1)}, u32[]{:S(2)}, u32[]{:S(2)}) async-start(bf16[128,8,2048]{2,1,0:T(8,128)(2,1)} %convert_bitcast_fusion), calls=%async_computation.1 | async-start | bytes 8388608 | tf_op jit(solution)/shard_map/all_to_all | solution.py:252
  166.2 1.5 fusion.42
  167.8 0.9 select_reduce_fusion
  168.7 51.8 %all-to-all-done.1 = bf16[128,8,2048]{2,1,0:T(8,128)(2,1)} async-done(((bf16[128,8,2048]{2,1,0:T(8,128)(2,1)}), bf16[128,8,2048]{2,1,0:T(8,128)(2,1)}, u32[]{:S(2)}, u32[]{:S(2)}) %all-to-all-start.1) | async-done | bytes 4194336 | tf_op jit(solution)/shard_map/all_to_all | solution.py:252
  220.5 3.7 %fusion.11 = bf16[65,2048]{1,0:T(8,128)(2,1)S(1)} fusion(f32[65,2048]{1,0:T(8,128)S(1)} %get-tuple-element.53, f32[65,512]{1,0:T(8,128)} %select_reduce_fusion, bf16[64,2,8,2048]{3,2,1,0:T(8,128)(2,1)} %bitcast.56), kind=kOutput, calls=%fused_computation.17 | convolution fusion | flops 822349824 | bytes 5126144 | tf_op jit(solution)/shard_map/dot_general | solution.py:259
  224.2 0.7 slice_bitcast_fusion.5
  224.9 0.6 slice_bitcast_fusion.8
  (83 shorter events, 2.5 us)
Async XLA Ops:
  0.6 149.7 %copy-start = (bf16[1,704,2048]{2,1,0:T(8,128)(2,1)S(1)}, bf16[1,704,2048]{2,1,0:T(8,128)(2,1)}, u32[]{:S(2)}) copy-start(bf16[1,704,2048]{2,1,0:T(8,128)(2,1)} %param.39) | copy-start | bytes 8650756
  0.6 6.4 %copy-start.17 = (bf16[4,1,576]{2,0,1:T(4,128)(2,1)S(1)}, bf16[4,1,576]{2,0,1:T(4,128)(2,1)}, u32[]{:S(2)}) copy-start(bf16[4,1,576]{2,0,1:T(4,128)(2,1)} %param.25) | copy-start | bytes 13828
  0.7 28.0 %copy-start.11 = (bf16[4,1,8,512]{3,2,1,0:T(8,128)(2,1)S(1)}, bf16[4,1,8,512]{3,2,1,0:T(8,128)(2,1)}, u32[]{:S(2)}) copy-start(bf16[4,1,8,512]{3,2,1,0:T(8,128)(2,1)} %param.26) | copy-start | bytes 98308
  0.7 27.8 %copy-start.13 = (bf16[4,1,8,64]{3,2,1,0:T(8,128)(2,1)S(1)}, bf16[4,1,8,64]{3,2,1,0:T(8,128)(2,1)}, u32[]{:S(2)}) copy-start(bf16[4,1,8,64]{3,2,1,0:T(8,128)(2,1)} %param.27) | copy-start | bytes 12292
  0.7 3.6 %copy-start.15 = (s32[4,1]{0,1:T(1,128)S(1)}, s32[4,1]{0,1:T(1,128)}, u32[]{:S(2)}) copy-start(s32[4,1]{0,1:T(1,128)} %param.29) | copy-start | bytes 52
  0.7 8.4 %copy-start.16 = (s32[4,1,8]{2,1,0:T(1,128)S(1)}, s32[4,1,8]{2,1,0:T(1,128)}, u32[]{:S(2)}) copy-start(s32[4,1,8]{2,1,0:T(1,128)} %param.30) | copy-start | bytes 388
  7.0 21.0 %copy-start.19 = (f32[32]{0:T(128)}, f32[32]{0:T(128)S(1)}, u32[]{:S(2)}) copy-start(f32[32]{0:T(128)S(1)} %multiply_power_fusion) | copy-start | bytes 388
  28.5 3.0 %copy-start.1 = (bf16[2048,576]{1,0:T(8,128)(2,1)S(1)}, bf16[2048,576]{1,0:T(8,128)(2,1)}, u32[]{:S(2)}) copy-start(bf16[2048,576]{1,0:T(8,128)(2,1)} %dynamic_update_slice.15) | copy-start | bytes 7077892
  31.5 1.2 copy-start.14
  31.5 31.5 %copy-start.9 = (bf16[1,64,8,64]{3,2,1,0:T(8,128)(2,1)S(1)}, bf16[1,64,8,64]{3,2,1,0:T(8,128)(2,1)}, u32[]{:S(2)}) copy-start(bf16[1,64,8,64]{3,2,1,0:T(8,128)(2,1)} %param.22) | copy-start | bytes 196612
  31.5 31.5 %copy-start.4 = (bf16[1,64,8,512]{3,2,1,0:T(8,128)(2,1)S(1)}, bf16[1,64,8,512]{3,2,1,0:T(8,128)(2,1)}, u32[]{:S(2)}) copy-start(bf16[1,64,8,512]{3,2,1,0:T(8,128)(2,1)} %param.21) | copy-start | bytes 1572868
  36.2 27.0 %copy-start.20 = (pred[256]{0:T(512)(128)(4,1)S(1)}, pred[256]{0:T(512)(128)(4,1)}, u32[]{:S(2)}) copy-start(pred[256]{0:T(512)(128)(4,1)} %compare_reduce_fusion) | copy-start | bytes 772
  62.0 1.0 copy-start.3
  63.0 1.2 copy-start.6
  63.2 1.0 copy-start.5
  65.4 3.9 %copy-start.7 = (bf16[4,64,576]{2,1,0:T(8,128)(2,1)S(1)}, bf16[4,64,576]{2,1,0:T(8,128)(2,1)}, u32[]{:S(2)}) copy-start(bf16[4,64,576]{2,1,0:T(8,128)(2,1)} %copy-done.6) | copy-start | bytes 884740
  69.3 4.3 %copy-start.18 = (bf16[4,1,2048]{2,0,1:T(4,128)(2,1)S(1)}, bf16[4,1,2048]{2,0,1:T(4,128)(2,1)}, u32[]{:S(2)}) copy-start(bf16[4,1,2048]{2,0,1:T(4,128)(2,1)} %param.28) | copy-start | bytes 49156
  71.7 1.9 copy-start.8
  73.5 3.3 %copy-start.10 = (s32[65,6]{0,1:T(8,128)S(1)}, s32[65,6]{0,1:T(8,128)}, u32[]{:S(2)}) copy-start(s32[65,6]{0,1:T(8,128)} %param.36) | copy-start | bytes 4684
  73.5 3.7 %copy-start.12 = (f32[2048]{0:T(1024)S(1)}, f32[2048]{0:T(1024)}, u32[]{:S(2)}) copy-start(f32[2048]{0:T(1024)} %param.34) | copy-start | bytes 24580
  78.6 67.0 %copy-start.21 = (bf16[1,2048,704]{1,2,0:T(8,128)(2,1)S(1)}, bf16[1,2048,704]{1,2,0:T(8,128)(2,1)}, u32[]{:S(2)}) copy-start(bf16[1,2048,704]{1,2,0:T(8,128)(2,1)} %param.37) | copy-start | bytes 8650756
  143.6 2.0 copy-start.2
  161.5 59.0 %all-to-all-start.1 = ((bf16[128,8,2048]{2,1,0:T(8,128)(2,1)}), bf16[128,8,2048]{2,1,0:T(8,128)(2,1)}, u32[]{:S(2)}, u32[]{:S(2)}) async-start(bf16[128,8,2048]{2,1,0:T(8,128)(2,1)} %convert_bitcast_fusion), calls=%async_computation.1 | async-start | bytes 8388608 | tf_op jit(solution)/shard_map/all_to_all | solution.py:252

commit v2 on v1

--- a/solution.py
+++ b/solution.py
@@ -1,7 +1,13 @@
+import functools
+
 import jax
 import jax.numpy as jnp
 from jax import lax
+from jax.experimental import pallas as pl
+from jax.experimental.pallas import tpu as pltpu
 from jax.sharding import PartitionSpec as P
+
+MESH = pl.DeviceIdType.MESH
 
 DC = 512
 DR = 64
@@ -69,6 +75,74 @@
     merged_total = left_total * left_factor + right_total * right_factor
     merged_accum = left_accum * left_factor[..., None] + right_accum * right_factor[..., None]
     return (new_peak, merged_total, merged_accum)
+
+
+def exchange_kernel(n_req, total, x_ref, out_ref, send_sem, recv_sem, local_sem):
+    me = lax.axis_index("ctx") * n_req + lax.axis_index("req")
+
+    def device(d):
+        return (d // n_req, d % n_req)
+
+    def outgoing(d):
+        return pltpu.make_async_remote_copy(
+            src_ref=x_ref.at[d],
+            dst_ref=out_ref.at[me],
+            send_sem=send_sem.at[d],
+            recv_sem=recv_sem.at[me],
+            device_id=device(d),
+            device_id_type=MESH,
+        )
+
+    def incoming(s):
+        return pltpu.make_async_remote_copy(
+            src_ref=x_ref.at[me],
+            dst_ref=out_ref.at[s],
+            send_sem=send_sem.at[s],
+            recv_sem=recv_sem.at[s],
+            device_id=device(s),
+            device_id_type=MESH,
+        )
+
+    barrier = pltpu.get_barrier_semaphore()
+
+    def greet(k, carry):
+        d = lax.rem(me + k, total)
+        pl.semaphore_signal(barrier, inc=1, device_id=device(d), device_id_type=MESH)
+        return carry
+
+    lax.fori_loop(1, total, greet, 0)
+    pl.semaphore_wait(barrier, total - 1)
+    local = pltpu.make_async_copy(x_ref.at[me], out_ref.at[me], local_sem)
+    local.start()
+
+    def send(k, carry):
+        outgoing(lax.rem(me + k, total)).start()
+        return carry
+
+    lax.fori_loop(1, total, send, 0)
+
+    def finish(k, carry):
+        outgoing(lax.rem(me + k, total)).wait_send()
+        incoming(lax.rem(me + total - k, total)).wait_recv()
+        return carry
+
+    lax.fori_loop(1, total, finish, 0)
+    local.wait()
+
+
+def exchange(x, n_req, total, collective_id):
+    return pl.pallas_call(
+        functools.partial(exchange_kernel, n_req, total),
+        out_shape=jax.ShapeDtypeStruct(x.shape, x.dtype),
+        in_specs=[pl.BlockSpec(memory_space=pl.ANY)],
+        out_specs=pl.BlockSpec(memory_space=pl.ANY),
+        scratch_shapes=[
+            pltpu.SemaphoreType.DMA((total,)),
+            pltpu.SemaphoreType.DMA((total,)),
+            pltpu.SemaphoreType.DMA(()),
+        ],
+        compiler_params=pltpu.CompilerParams(collective_id=collective_id, has_side_effects=True),
+    )(x)
 
 
 def body(
@@ -243,15 +317,16 @@
     doubled = jnp.broadcast_to(outgoing[:, None], (expert_count, 2, capacity, width)).reshape(
         devices, capacity, width
     )
+    req_count = lax.axis_size("req")
     partial_out = expert_half(
-        lax.all_to_all(doubled, ("ctx", "req"), split_axis=0, concat_axis=0, tiled=True),
+        exchange(doubled, req_count, devices, 0),
         w_gate[0],
         w_up[0],
         w_down[0],
     )
-    returned = lax.all_to_all(
-        partial_out, ("ctx", "req"), split_axis=0, concat_axis=0, tiled=True
-    ).reshape(expert_count, 2, capacity, width)
+    returned = exchange(partial_out, req_count, devices, 1).reshape(
+        expert_count, 2, capacity, width
+    )
     results = (returned[:, 0].astype(jnp.float32) + returned[:, 1].astype(jnp.float32)).astype(
         jnp.bfloat16
     ).reshape(expert_count * capacity, width)

time: 227 us -> 261 us (1.15)
  the two profiles are of different devices: /device:TPU:8 before, /device:TPU:29 now
where the time goes in v2:
time: 261 us; the launch traced here: 260 us
  Pallas kernels  153 us (59%)
  matrix products  39.5 us (15%)
  local copies, waits for them, and re-layouts  22.8 us (9%)
  other arithmetic  17.8 us (7%)
  between operations  14 us (5%)
  blocking collectives  12.7 us (5%)
    pallas_call x2, Pallas kernels, exchange(): pl.pallas_call(functools.partial(exchange_kernel, n_req, total), out_shap...  153 us
    all_gather x1, blocking collectives, body(): gathered = lax.all_gather(packed, 'ctx')  12.7 us
    dot_general x1, matrix products, expert_half(): jnp.dot(hidden, down_part, preferred_element_type=jnp.float32)  11.2 us
    dot_general x1, matrix products, expert_half(): gate_out = jnp.dot(flat_rows, gate_part, preferred_element_type=jnp.float32)  7.91 us
    unnamed x43, local copies, waits for them, and re-layouts  5.64 us
    dynamic_update_slice x4, local copies, waits for them, and re-layouts, body(): flat_pool = lax.dynamic_update_slice_in_dim(flat_pool, row, spot, 0)  5.3 us

profile of v2, /device:TPU:29, one launch (start us, length us, event | category | flops | bytes accessed | tf_op | source)
XLA Modules:
  0.0 259.6 jit_solution(5825601134270590226)
XLA Ops:
  0.7 3.6 %copy.76 = bf16[32,64,576]{2,1,0:T(8,128)(2,1)} copy(bf16[32,64,576]{2,1,0:T(8,128)(2,1)} %param.31) | data formatting | bytes 4718592
  4.3 0.7 fusion.115
  7.0 0.2 select_reduce_fusion.5
  7.3 0.6 fusion.116
  8.6 0.7 fusion.117
  10.2 0.7 broadcast_select_fusion.3
  10.9 1.3 dynamic_update_slice.12
  15.3 0.7 broadcast_select_fusion.2
  16.0 1.3 dynamic_update_slice.13
  20.5 0.7 broadcast_select_fusion.1
  21.3 1.3 dynamic_update_slice.14
  25.9 0.7 broadcast_select_fusion
  26.6 1.3 dynamic_update_slice.15
  28.7 2.8 %fusion.118 = (f32[4,8]{1,0:T(4,128)S(1)}, f32[4,8,2048]{2,1,0:T(8,128)S(1)}) fusion(bf16[2048,576]{1,0:T(8,128)(2,1)} %dynamic_update_slice.15, bf16[4,8,32]{2,1,0:T(8,128)(2,1)S(1)} %get-tuple-element.17, bf16[4,8,32]{2,1,0:T(8,128)(2,1)S(1)} %get-tuple-element.16, bf16[4,8,512]{2,1,0:T(8,128)(2,1)S(1)} %bitcast.179, pred[4,2048]{1,0:T(4,128)(4,1)S(1)} %fusion.73), kind=kOutput, calls=%fused_computation.239 | convolution fusion | flops 75804640 | bytes 2666624 | tf_op jit(solution)/shard_map/rhd,kd->rhk/dot_general | solution.py:225
  31.5 1.1 fusion.39
  32.7 0.8 fusion.57
  33.5 0.8 reshape.786
  34.2 1.3 reshape.785
  35.6 1.6 fusion.114
  37.2 5.0 %fusion.112 = (f32[64]{0:T(128)S(1)}, s32[64]{0:T(128)S(1)}) fusion(s32[]{:T(128)S(6)} %mul.309, s32[]{:T(128)} %bitcast.11, s32[]{:T(128)} %bitcast.10, s32[]{:T(128)} %bitcast.9, s32[]{:T(128)} %bitcast.8, s32[]{:T(128)} %bitcast.7, s32[]{:T(128)} %bitcast.6, s32[]{:T(128)} %bitcast.5, s32[]{:T(128)} %bitcast.4), kind=kLoop, calls=%fused_computation.234 | loop fusion | flops 5120 | bytes 548 | tf_op jit(solution)/shard_map/convert_element_type | solution.py:37
  42.2 1.0 multiply_cosine_fusion
  43.2 0.8 slice.178
  44.2 0.9 maximum_maximum_fusion
  45.1 12.7 %all-gather = f32[384,576]{1,0:T(8,128)S(1)} all-gather(f32[96,576]{1,0:T(8,128)S(1)} %maximum_maximum_fusion), channel_id=2, replica_groups=mesh['ctx'=4,'req'=32] {'ctx'}, dimensions={0}, use_global_device_ids=true | all-gather | bytes 1105920 | tf_op jit(solution)/shard_map/all_gather | solution.py:249
  57.8 1.0 copy-done.2
  59.0 4.4 %compare_select_fusion.1 = s32[256,1]{0,1:T(1,128)S(1)} fusion(s32[]{:T(128)} %bitcast.5, s32[]{:T(128)} %bitcast.6, s32[]{:T(128)} %bitcast.7, s32[]{:T(128)} %bitcast.8, s32[]{:T(128)} %bitcast.9, s32[]{:T(128)} %bitcast.11, s32[]{:T(128)} %bitcast.10), kind=kLoop, calls=%fused_computation.135 | loop fusion | flops 11264 | bytes 1052 | tf_op jit(solution)/shard_map/gather | solution.py:55
  63.4 0.7 fusion.90
  64.2 0.2 copy.69
  64.4 0.8 copy-done.4
  65.1 1.2 fusion.33
  66.4 1.8 fusion.119
  68.2 2.4 fusion.28
  70.6 1.0 slice_bitcast_fusion.4
  71.7 0.2 dynamic-slice_reduce_fusion
  72.1 1.7 fusion.38
  74.0 3.2 %multiply_reduce_fusion = (f32[65]{0:T(128)S(1)}, f32[65,2048]{1,0:T(8,128)S(1)}) fusion(bf16[65,1024]{1,0:T(8,128)(2,1)S(1)} %bitcast.169, bf16[1024,2048]{1,0:T(8,128)(2,1)} %param.33, bf16[1,2048]{1,0:T(2,128)(2,1)S(1)} %dynamic-slice_bitcast_fusion, bf16[64,2048]{1,0:T(8,128)(2,1)} %bitcast.176), kind=kOutput, calls=%fused_computation.55 | convolution fusion | flops 273561536 | bytes 5126404 | tf_op jit(solution)/shard_map/dot_general | solution.py:286
  77.5 0.2 fusion.43
  77.7 0.8 fusion.8
  78.5 2.5 broadcast_in_dim.160
  80.9 73.0 %shard_map.211 = bf16[128,8,2048]{2,1,0:T(8,128)(2,1)} custom-call(bf16[128,8,2048]{2,1,0:T(8,128)(2,1)} %bitcast.161), custom_call_target="tpu_custom_call" | custom-call | tf_op jit(solution)/shard_map/pallas_call | solution.py:134
  154.0 7.9 %fusion.3 = f32[1024,704]{0,1:T(8,128)} fusion(bf16[128,8,2048]{2,1,0:T(8,128)(2,1)} %shard_map.211, bf16[1,2048,704]{1,2,0:T(8,128)(2,1)} %param.37), kind=kOutput, calls=%fused_computation.3 | convolution fusion | flops 2952790016 | bytes 9961472 | tf_op jit(solution)/shard_map/dot_general | solution.py:60
  161.9 11.2 %convert_bitcast_fusion.x_ref = bf16[128,8,2048]{2,1,0:T(8,128)(2,1)} fusion(bf16[1,704,2048]{2,1,0:T(8,128)(2,1)S(1)} %copy-done, f32[1024,704]{0,1:T(8,128)} %fusion.3, bf16[1,2048,704]{1,2,0:T(8,128)(2,1)} %param.38, bf16[128,8,2048]{2,1,0:T(8,128)(2,1)} %shard_map.211), kind=kOutput, calls=%fused_computation.6 | convolution fusion | flops 5912002560 | bytes 17039360 | tf_op jit(solution)/shard_map/dot_general | solution.py:63
  173.1 79.8 %shard_map.212 = bf16[128,8,2048]{2,1,0:T(8,128)(2,1)} custom-call(bf16[128,8,2048]{2,1,0:T(8,128)(2,1)} %convert_bitcast_fusion.x_ref), custom_call_target="tpu_custom_call" | custom-call | tf_op jit(solution)/shard_map/pallas_call | solution.py:134
  252.9 1.5 fusion.42
  254.5 0.2 select_reduce_fusion
  254.7 3.6 %fusion.11 = bf16[65,2048]{1,0:T(8,128)(2,1)S(1)} fusion(f32[65,2048]{1,0:T(8,128)S(1)} %get-tuple-element.53, f32[65,512]{1,0:T(8,128)S(1)} %select_reduce_fusion, bf16[64,2,8,2048]{3,2,1,0:T(8,128)(2,1)} %bitcast.165), kind=kOutput, calls=%fused_computation.17 | convolution fusion | flops 822349824 | bytes 5126144 | tf_op jit(solution)/shard_map/dot_general | solution.py:334
  258.3 0.7 slice_bitcast_fusion.5
  259.0 0.6 slice_bitcast_fusion.8
  (76 shorter events, 2.2 us)
Async XLA Ops:
  0.6 161.3 %copy-start = (bf16[1,704,2048]{2,1,0:T(8,128)(2,1)S(1)}, bf16[1,704,2048]{2,1,0:T(8,128)(2,1)}, u32[]{:S(2)}) copy-start(bf16[1,704,2048]{2,1,0:T(8,128)(2,1)} %param.39) | copy-start | bytes 8650756
  0.6 9.3 %copy-start.16 = (bf16[4,1,576]{2,0,1:T(4,128)(2,1)S(1)}, bf16[4,1,576]{2,0,1:T(4,128)(2,1)}, u32[]{:S(2)}) copy-start(bf16[4,1,576]{2,0,1:T(4,128)(2,1)} %param.25) | copy-start | bytes 13828
  0.7 28.0 %copy-start.10 = (bf16[4,1,8,512]{3,2,1,0:T(8,128)(2,1)S(1)}, bf16[4,1,8,512]{3,2,1,0:T(8,128)(2,1)}, u32[]{:S(2)}) copy-start(bf16[4,1,8,512]{3,2,1,0:T(8,128)(2,1)} %param.26) | copy-start | bytes 98308
  0.7 27.9 %copy-start.12 = (bf16[4,1,8,64]{3,2,1,0:T(8,128)(2,1)S(1)}, bf16[4,1,8,64]{3,2,1,0:T(8,128)(2,1)}, u32[]{:S(2)}) copy-start(bf16[4,1,8,64]{3,2,1,0:T(8,128)(2,1)} %param.27) | copy-start | bytes 12292
  0.7 3.6 %copy-start.14 = (s32[4,1]{0,1:T(1,128)S(1)}, s32[4,1]{0,1:T(1,128)}, u32[]{:S(2)}) copy-start(s32[4,1]{0,1:T(1,128)} %param.29) | copy-start | bytes 52
  0.7 6.4 %copy-start.15 = (s32[4,1,8]{2,1,0:T(1,128)S(1)}, s32[4,1,8]{2,1,0:T(1,128)}, u32[]{:S(2)}) copy-start(s32[4,1,8]{2,1,0:T(1,128)} %param.30) | copy-start | bytes 388
  9.9 18.0 %copy-start.18 = (f32[32]{0:T(128)}, f32[32]{0:T(128)S(1)}, u32[]{:S(2)}) copy-start(f32[32]{0:T(128)S(1)} %multiply_power_fusion) | copy-start | bytes 388
  28.5 3.0 %copy-start.1 = (bf16[2048,576]{1,0:T(8,128)(2,1)S(1)}, bf16[2048,576]{1,0:T(8,128)(2,1)}, u32[]{:S(2)}) copy-start(bf16[2048,576]{1,0:T(8,128)(2,1)} %dynamic_update_slice.15) | copy-start | bytes 7077892
  31.5 1.2 copy-start.13
  31.5 27.3 %copy-start.7 = (bf16[1,64,8,64]{3,2,1,0:T(8,128)(2,1)S(1)}, bf16[1,64,8,64]{3,2,1,0:T(8,128)(2,1)}, u32[]{:S(2)}) copy-start(bf16[1,64,8,64]{3,2,1,0:T(8,128)(2,1)} %param.22) | copy-start | bytes 196612
  31.5 32.6 %copy-start.3 = (bf16[1,64,8,512]{3,2,1,0:T(8,128)(2,1)S(1)}, bf16[1,64,8,512]{3,2,1,0:T(8,128)(2,1)}, u32[]{:S(2)}) copy-start(bf16[1,64,8,512]{3,2,1,0:T(8,128)(2,1)} %param.21) | copy-start | bytes 1572868
  57.8 1.0 copy-start.2
  58.8 5.5 %copy-start.5 = (bf16[4,64,576]{2,1,0:T(8,128)(2,1)}, bf16[4,64,576]{2,1,0:T(8,128)(2,1)S(1)}, u32[]{:S(2)}) copy-start(bf16[4,64,576]{2,1,0:T(8,128)(2,1)S(1)} %slice.237) | copy-start | bytes 884740
  59.0 5.4 %copy-start.8 = (bf16[64,8,32]{2,0,1:T(8,128)(2,1)}, bf16[64,8,32]{2,0,1:T(8,128)(2,1)S(1)}, u32[]{:S(2)}) copy-start(bf16[64,8,32]{2,0,1:T(8,128)(2,1)S(1)} %get-tuple-element.13) | copy-start | bytes 98308
  64.3 0.8 copy-start.4
  66.4 1.8 copy-start.6
  70.6 3.4 %copy-start.17 = (bf16[4,1,2048]{2,0,1:T(4,128)(2,1)S(1)}, bf16[4,1,2048]{2,0,1:T(4,128)(2,1)}, u32[]{:S(2)}) copy-start(bf16[4,1,2048]{2,0,1:T(4,128)(2,1)} %param.28) | copy-start | bytes 49156
  73.9 3.3 %copy-start.9 = (s32[65,6]{0,1:T(8,128)S(1)}, s32[65,6]{0,1:T(8,128)}, u32[]{:S(2)}) copy-start(s32[65,6]{0,1:T(8,128)} %param.36) | copy-start | bytes 4684
  73.9 3.7 %copy-start.11 = (f32[2048]{0:T(1024)S(1)}, f32[2048]{0:T(1024)}, u32[]{:S(2)}) copy-start(f32[2048]{0:T(1024)} %param.34) | copy-start | bytes 24580

commit v3 on v2

--- a/solution.py
+++ b/solution.py
@@ -49,10 +49,11 @@
 
 
 def block_position(block_order, global_rows, shard_rows):
-    shard_id = global_rows // shard_rows
-    within = global_rows % shard_rows
     half_rows = shard_rows // 2
-    return block_order[2 * shard_id + within // half_rows] * half_rows + within % half_rows
+    block = global_rows // half_rows
+    hit = block[:, None] == jnp.arange(block_order.shape[0])[None, :]
+    logical = jnp.sum(jnp.where(hit, block_order[None, :], 0), axis=1)
+    return logical * half_rows + global_rows % half_rows
 
 
 def expert_half(inputs, gate_part, up_part, down_part):
@@ -196,18 +197,20 @@
     page_index = lengths // page_rows
     owner_ctx = page_index // pages_dev
     page_hit = tables[:, :, None] == jnp.arange(slot_count)[None, None, :]
-    slot_of = jnp.sum(
-        jnp.where((jnp.arange(pages_dev)[None, :] == (page_index % pages_dev)[:, None])[:, :, None],
-                  page_hit, False).astype(jnp.int32) * jnp.arange(slot_count)[None, None, :],
-        axis=(1, 2),
-    )
-    flat_pool = cache_pool.reshape(slot_count * page_rows, row_width)
-    for request in range(request_count):
-        owned = owner_ctx[request] == ctx_index
-        spot = jnp.where(owned, slot_of[request] * page_rows + lengths[request] % page_rows, 0)
-        old_row = lax.dynamic_slice_in_dim(flat_pool, spot, 1, 0)
-        row = jnp.where(owned, new_rows[request][None], old_row)
-        flat_pool = lax.dynamic_update_slice_in_dim(flat_pool, row, spot, 0)
+    wanted = jnp.arange(pages_dev)[None, :] == (page_index % pages_dev)[:, None]
+    slot_of = jnp.sum(jnp.where(wanted, tables, 0), axis=1)
+    target = jnp.where(
+        owner_ctx == ctx_index, slot_of * page_rows + lengths % page_rows, slot_count * page_rows
+    )
+    row_hit = jnp.arange(slot_count * page_rows)[:, None] == target[None, :]
+    written = jnp.dot(
+        row_hit.astype(jnp.bfloat16), new_rows, preferred_element_type=jnp.float32
+    ).astype(jnp.bfloat16)
+    flat_pool = jnp.where(
+        jnp.any(row_hit, axis=1)[:, None],
+        written,
+        cache_pool.reshape(slot_count * page_rows, row_width),
+    )
     page_valid = jnp.any(page_hit, axis=1)
     page_logical = jnp.sum(page_hit.astype(jnp.int32) * jnp.arange(pages_dev)[None, :, None], axis=1)
     page_start = (ctx_index * pages_dev + page_logical) * page_rows
@@ -317,16 +320,15 @@
     doubled = jnp.broadcast_to(outgoing[:, None], (expert_count, 2, capacity, width)).reshape(
         devices, capacity, width
     )
-    req_count = lax.axis_size("req")
     partial_out = expert_half(
-        exchange(doubled, req_count, devices, 0),
+        lax.all_to_all(doubled, ("ctx", "req"), split_axis=0, concat_axis=0, tiled=True),
         w_gate[0],
         w_up[0],
         w_down[0],
     )
-    returned = exchange(partial_out, req_count, devices, 1).reshape(
-        expert_count, 2, capacity, width
-    )
+    returned = lax.all_to_all(
+        partial_out, ("ctx", "req"), split_axis=0, concat_axis=0, tiled=True
+    ).reshape(expert_count, 2, capacity, width)
     results = (returned[:, 0].astype(jnp.float32) + returned[:, 1].astype(jnp.float32)).astype(
         jnp.bfloat16
     ).reshape(expert_count * capacity, width)

time: 261 us -> 200 us (0.77)
  the two profiles are of different devices: /device:TPU:29 before, /device:TPU:8 now
where the time goes in v3:
time: 200 us; the launch traced here: 199 us
  blocking collectives  77 us (38%)
  waiting for transfers between devices  47.5 us (24%)
  matrix products  37.4 us (19%)
  local copies, waits for them, and re-layouts  21.2 us (11%)
  other arithmetic  10.4 us (5%)
  starting transfers between devices  4.76 us (2%)
    all_to_all x1, blocking collectives, body(): lax.all_to_all(doubled, ('ctx', 'req'), split_axis=0, concat_axis=0, tile...  65 us
    all_to_all x1, waiting for transfers between devices, body(): lax.all_to_all(partial_out, ('ctx', 'req'), split_axis=0, concat_axis=0,...  47.5 us
    all_gather x1, blocking collectives, body(): gathered = lax.all_gather(packed, 'ctx')  12 us
    dot_general x1, matrix products, expert_half(): jnp.dot(hidden, down_part, preferred_element_type=jnp.float32)  11.1 us
    dot_general x1, matrix products, expert_half(): gate_out = jnp.dot(flat_rows, gate_part, preferred_element_type=jnp.float32)  4.82 us
    all_to_all x1, starting transfers between devices, body(): lax.all_to_all(partial_out, ('ctx', 'req'), split_axis=0, concat_axis=0,...  4.76 us
    unnamed x46, local copies, waits for them, and re-layouts  4.66 us
    select_n x1, local copies, waits for them, and re-layouts, body(): jnp.where(jnp.any(row_hit, axis=1)[:, None], written, cache_pool.reshape(...  4.33 us
  transfers between devices with their start and end apart: 1, of which 1 were waited for; matrix products, arithmetic and copies ran while one was open for 3% of the time, Pallas kernels for 0%

profile of v3, /device:TPU:8, one launch (start us, length us, event | category | flops | bytes accessed | tf_op | source)
XLA Modules:
  0.0 199.3 jit_solution(16934485441668844071)
XLA Ops:
  0.7 0.8 slice_bitcast_fusion.10
  1.5 0.7 slice_bitcast_fusion.9
  2.3 0.8 select_reduce_fusion.4
  3.0 0.8 fusion.84
  3.8 0.7 convert_bitcast_fusion.1
  4.5 0.9 select_reduce_fusion.7
  5.4 0.7 compare_select_fusion.2
  6.2 4.3 %copy.61 = bf16[2048,576]{0,1:T(8,128)(2,1)} copy(bf16[2048,576]{1,0:T(8,128)(2,1)} %bitcast.127) | data formatting | bytes 4718592 | tf_op jit(solution)/shard_map/reshape | solution.py:212
  11.2 2.5 %fusion.8 = bf16[2048,576]{0,1:T(8,128)(2,1)S(1)} fusion(bf16[2048,576]{0,1:T(8,128)(2,1)} %copy.61, pred[2048]{0:T(1024)(128)(4,1)S(1)} %fusion.74, s32[4]{0:T(128)S(1)} %compare_select_fusion.2, bf16[4,32]{1,0:T(4,128)(2,1)S(1)} %get-tuple-element.27, bf16[4,32]{1,0:T(4,128)(2,1)S(1)} %get-tuple-element.28, bf16[4,512]{1,0:T(4,128)(2,1)S(1)} %slice_bitcast_fusion.9), kind=kOutput, calls=%fused_computation.13 | convolution fusion | flops 11818496 | bytes 4725264 | tf_op jit(solution)/shard_map/dot_general | solution.py:206
  13.8 0.6 fusion.118
  14.4 0.9 copy-done.1
  15.3 1.4 fusion.40
  16.6 0.8 fusion.58
  17.4 0.8 reshape.511
  18.2 0.6 and_select_fusion.1
  18.8 1.4 reshape.512
  20.1 0.8 select_reduce_fusion.6
  21.0 0.8 slice.92
  21.8 1.0 multiply_cosine_fusion
  22.9 0.9 maximum_maximum_fusion
  23.8 12.0 %all-gather = f32[384,576]{1,0:T(8,128)S(1)} all-gather(f32[96,576]{1,0:T(8,128)S(1)} %maximum_maximum_fusion), channel_id=2, replica_groups=mesh['ctx'=4,'req'=32] {'ctx'}, dimensions={0}, use_global_device_ids=true | all-gather | bytes 1105920 | tf_op jit(solution)/shard_map/all_gather | solution.py:252
  35.9 0.9 copy-done.3
  37.0 0.2 copy.77
  37.3 0.1 fusion.54
  37.4 0.2 copy-done.6
  37.6 0.4 copy-done.5
  38.0 1.2 fusion.34
  39.2 2.4 %fusion.119 = f32[8,64]{1,0:T(8,128)} fusion(bf16[256,576,1]{1,0,2:T(8,128)(2,1)} %bitcast.135, bf16[64,8,32]{2,0,1:T(8,128)(2,1)S(1)} %get-tuple-element.14, bf16[64,8,32]{2,0,1:T(8,128)(2,1)S(1)} %get-tuple-element.13, bf16[64,8,512]{2,0,1:T(8,128)(2,1)} %bitcast.133, pred[64,256]{1,0:T(8,128)(4,1)S(1)} %broadcast_compare_fusion), kind=kOutput, calls=%fused_computation.209 | convolution fusion | flops 153420032 | bytes 903168 | tf_op jit(solution)/shard_map/sub | solution.py:273
  41.5 1.0 slice_bitcast_fusion.4
  42.7 0.2 dynamic-slice_reduce_fusion
  43.1 2.4 %fusion.29 = bf16[64,8,512]{2,0,1:T(8,128)(2,1)} fusion(f32[64,8]{0,1:T(8,128)} %bitcast.146, bf16[256,576]{1,0:T(8,128)(2,1)S(1)} %bitcast.136, f32[8,64,256]{2,1,0:T(8,128)} %fusion.34, pred[64,256]{1,0:T(8,128)(4,1)S(1)} %broadcast_compare_fusion), kind=kOutput, calls=%fused_computation.29 | convolution fusion | flops 135136000 | bytes 1855488 | tf_op jit(solution)/shard_map/hqk,kc->qhc/dot_general | solution.py:275
  45.4 1.8 fusion.39
  47.4 3.2 %multiply_reduce_fusion = (f32[65]{0:T(128)S(1)}, f32[65,2048]{1,0:T(8,128)S(1)}) fusion(bf16[65,1024]{1,0:T(8,128)(2,1)S(1)} %bitcast.130, bf16[1024,2048]{1,0:T(8,128)(2,1)} %param.33, bf16[1,2048]{1,0:T(2,128)(2,1)S(1)} %dynamic-slice_bitcast_fusion, bf16[64,2048]{1,0:T(8,128)(2,1)S(1)} %bitcast.137), kind=kOutput, calls=%fused_computation.57 | convolution fusion | flops 273561536 | bytes 5126404 | tf_op jit(solution)/shard_map/dot_general | solution.py:289
  50.8 0.2 fusion.44
  51.0 0.8 fusion.9
  51.8 0.5 broadcast_in_dim.198
  52.4 65.0 %all_to_all.10 = bf16[128,8,2048]{2,1,0:T(8,128)(2,1)S(1)} all-to-all(bf16[128,8,2048]{2,1,0:T(8,128)(2,1)S(1)} %bitcast.124), channel_id=1, replica_groups=mesh['ctx'=4,'req'=32] {'ctx','req'}, dimensions={0} | all-to-all | bytes 8388608 | tf_op jit(solution)/shard_map/all_to_all | solution.py:324
  117.4 2.0 copy-done.2
  119.3 4.8 %fusion.3 = f32[1024,704]{0,1:T(8,128)} fusion(bf16[128,8,2048]{2,1,0:T(8,128)(2,1)S(1)} %all_to_all.10, bf16[1,2048,704]{1,2,0:T(8,128)(2,1)S(1)} %copy-done.20), kind=kOutput, calls=%fused_computation.3 | convolution fusion | flops 2952790016 | bytes 9961472 | tf_op jit(solution)/shard_map/dot_general | solution.py:61
  124.1 11.1 %convert_bitcast_fusion = bf16[128,8,2048]{2,1,0:T(8,128)(2,1)} fusion(bf16[1,704,2048]{2,1,0:T(8,128)(2,1)S(1)} %copy-done, f32[1024,704]{0,1:T(8,128)} %fusion.3, bf16[1,2048,704]{1,2,0:T(8,128)(2,1)} %param.38, bf16[128,8,2048]{2,1,0:T(8,128)(2,1)} %copy-done.2), kind=kOutput, calls=%fused_computation.6 | convolution fusion | flops 5912002560 | bytes 17039360 | tf_op jit(solution)/shard_map/dot_general | solution.py:64
  135.3 4.8 %all-to-all-start.1 = ((bf16[128,8,2048]{2,1,0:T(8,128)(2,1)}), bf16[128,8,2048]{2,1,0:T(8,128)(2,1)}, u32[]{:S(2)}, u32[]{:S(2)}) async-start(bf16[128,8,2048]{2,1,0:T(8,128)(2,1)} %convert_bitcast_fusion), calls=%async_computation.1 | async-start | bytes 8388608 | tf_op jit(solution)/shard_map/all_to_all | solution.py:329
  140.0 4.3 %copy.69 = bf16[2048,576]{1,0:T(8,128)(2,1)} copy(bf16[2048,576]{0,1:T(8,128)(2,1)} %copy-done.1) | data formatting | bytes 4718592 | tf_op jit(solution)/shard_map/jit(_where)/select_n | solution.py:209
  144.4 1.5 fusion.43
  146.0 0.9 select_reduce_fusion
  146.8 47.5 %all-to-all-done.1 = bf16[128,8,2048]{2,1,0:T(8,128)(2,1)} async-done(((bf16[128,8,2048]{2,1,0:T(8,128)(2,1)}), bf16[128,8,2048]{2,1,0:T(8,128)(2,1)}, u32[]{:S(2)}, u32[]{:S(2)}) %all-to-all-start.1) | async-done | bytes 4194336 | tf_op jit(solution)/shard_map/all_to_all | solution.py:329
  194.3 3.7 %fusion.12 = bf16[65,2048]{1,0:T(8,128)(2,1)S(1)} fusion(f32[65,2048]{1,0:T(8,128)S(1)} %get-tuple-element.34, f32[65,512]{1,0:T(8,128)} %select_reduce_fusion, bf16[64,2,8,2048]{3,2,1,0:T(8,128)(2,1)} %bitcast.33), kind=kOutput, calls=%fused_computation.19 | convolution fusion | flops 822349824 | bytes 5126144 | tf_op jit(solution)/shard_map/dot_general | solution.py:336
  197.9 0.7 slice_bitcast_fusion.5
  198.7 0.6 slice_bitcast_fusion.8
  (73 shorter events, 1.9 us)
Async XLA Ops:
  0.6 123.5 %copy-start = (bf16[1,704,2048]{2,1,0:T(8,128)(2,1)S(1)}, bf16[1,704,2048]{2,1,0:T(8,128)(2,1)}, u32[]{:S(2)}) copy-start(bf16[1,704,2048]{2,1,0:T(8,128)(2,1)} %param.39) | copy-start | bytes 8650756
  0.6 10.5 %copy-start.17 = (s32[4,1]{0,1:T(1,128)S(1)}, s32[4,1]{0,1:T(1,128)}, u32[]{:S(2)}) copy-start(s32[4,1]{0,1:T(1,128)} %param.29) | copy-start | bytes 52
  0.7 10.4 %copy-start.13 = (bf16[4,1,8,64]{3,2,1,0:T(8,128)(2,1)S(1)}, bf16[4,1,8,64]{3,2,1,0:T(8,128)(2,1)}, u32[]{:S(2)}) copy-start(bf16[4,1,8,64]{3,2,1,0:T(8,128)(2,1)} %param.27) | copy-start | bytes 12292
  0.7 13.1 %copy-start.16 = (f32[32]{0:T(128)}, f32[32]{0:T(128)S(1)}, u32[]{:S(2)}) copy-start(f32[32]{0:T(128)S(1)} %multiply_power_fusion) | copy-start | bytes 388
  10.5 3.3 %copy-start.11 = (bf16[4,1,8,512]{3,2,1,0:T(8,128)(2,1)S(1)}, bf16[4,1,8,512]{3,2,1,0:T(8,128)(2,1)}, u32[]{:S(2)}) copy-start(bf16[4,1,8,512]{3,2,1,0:T(8,128)(2,1)} %param.26) | copy-start | bytes 98308
  13.8 1.5 copy-start.1
  14.4 2.3 %copy-start.14 = (f32[4,8]{1,0:T(4,128)}, f32[4,8]{1,0:T(4,128)S(1)}, u32[]{:S(2)}) copy-start(f32[4,8]{1,0:T(4,128)S(1)} %get-tuple-element.31) | copy-start | bytes 388
  14.4 22.5 %copy-start.9 = (bf16[1,64,8,64]{3,2,1,0:T(8,128)(2,1)S(1)}, bf16[1,64,8,64]{3,2,1,0:T(8,128)(2,1)}, u32[]{:S(2)}) copy-start(bf16[1,64,8,64]{3,2,1,0:T(8,128)(2,1)} %param.22) | copy-start | bytes 196612
  15.3 21.7 %copy-start.4 = (bf16[1,64,8,512]{3,2,1,0:T(8,128)(2,1)S(1)}, bf16[1,64,8,512]{3,2,1,0:T(8,128)(2,1)}, u32[]{:S(2)}) copy-start(bf16[1,64,8,512]{3,2,1,0:T(8,128)(2,1)} %param.21) | copy-start | bytes 1572868
  20.1 16.8 %copy-start.18 = (s32[256]{0:T(256)S(1)}, s32[256]{0:T(256)}, u32[]{:S(2)}) copy-start(s32[256]{0:T(256)} %and_select_fusion.1) | copy-start | bytes 3076
  20.1 16.8 %copy-start.19 = (s32[8]{0:T(128)S(1)}, s32[8]{0:T(128)}, u32[]{:S(2)}) copy-start(s32[8]{0:T(128)} %param.24) | copy-start | bytes 100
  35.9 0.9 copy-start.3
  36.9 0.7 copy-start.6
  37.2 0.8 copy-start.5
  39.2 3.9 %copy-start.7 = (bf16[4,64,576]{2,1,0:T(8,128)(2,1)S(1)}, bf16[4,64,576]{2,1,0:T(8,128)(2,1)}, u32[]{:S(2)}) copy-start(bf16[4,64,576]{2,1,0:T(8,128)(2,1)} %copy-done.6) | copy-start | bytes 884740
  43.1 4.3 %copy-start.15 = (bf16[4,1,2048]{2,0,1:T(4,128)(2,1)S(1)}, bf16[4,1,2048]{2,0,1:T(4,128)(2,1)}, u32[]{:S(2)}) copy-start(bf16[4,1,2048]{2,0,1:T(4,128)(2,1)} %param.28) | copy-start | bytes 49156
  45.4 1.9 copy-start.8
  47.2 3.3 %copy-start.10 = (s32[65,6]{0,1:T(8,128)S(1)}, s32[65,6]{0,1:T(8,128)}, u32[]{:S(2)}) copy-start(s32[65,6]{0,1:T(8,128)} %param.36) | copy-start | bytes 4684
  47.3 3.7 %copy-start.12 = (f32[2048]{0:T(1024)S(1)}, f32[2048]{0:T(1024)}, u32[]{:S(2)}) copy-start(f32[2048]{0:T(1024)} %param.34) | copy-start | bytes 24580
  52.4 67.0 %copy-start.20 = (bf16[1,2048,704]{1,2,0:T(8,128)(2,1)S(1)}, bf16[1,2048,704]{1,2,0:T(8,128)(2,1)}, u32[]{:S(2)}) copy-start(bf16[1,2048,704]{1,2,0:T(8,128)(2,1)} %param.37) | copy-start | bytes 8650756
  117.3 2.0 copy-start.2
  135.3 59.0 %all-to-all-start.1 = ((bf16[128,8,2048]{2,1,0:T(8,128)(2,1)}), bf16[128,8,2048]{2,1,0:T(8,128)(2,1)}, u32[]{:S(2)}, u32[]{:S(2)}) async-start(bf16[128,8,2048]{2,1,0:T(8,128)(2,1)} %convert_bitcast_fusion), calls=%async_computation.1 | async-start | bytes 8388608 | tf_op jit(solution)/shard_map/all_to_all | solution.py:329

commit v4 on v3

--- a/solution.py
+++ b/solution.py
@@ -317,21 +317,29 @@
     outgoing = lax.dot_general(
         dispatch, normed, (((0,), (0,)), ((), ())), preferred_element_type=jnp.float32
     ).astype(jnp.bfloat16).reshape(expert_count, capacity, width)
-    doubled = jnp.broadcast_to(outgoing[:, None], (expert_count, 2, capacity, width)).reshape(
-        devices, capacity, width
-    )
-    partial_out = expert_half(
-        lax.all_to_all(doubled, ("ctx", "req"), split_axis=0, concat_axis=0, tiled=True),
-        w_gate[0],
-        w_up[0],
-        w_down[0],
-    )
-    returned = lax.all_to_all(
-        partial_out, ("ctx", "req"), split_axis=0, concat_axis=0, tiled=True
-    ).reshape(expert_count, 2, capacity, width)
-    results = (returned[:, 0].astype(jnp.float32) + returned[:, 1].astype(jnp.float32)).astype(
-        jnp.bfloat16
-    ).reshape(expert_count * capacity, width)
+    chunks = 2
+    piece = capacity // chunks
+    pieces = []
+    for chunk in range(chunks):
+        part = outgoing[:, chunk * piece:(chunk + 1) * piece]
+        doubled = jnp.broadcast_to(part[:, None], (expert_count, 2, piece, width)).reshape(
+            devices, piece, width
+        )
+        partial_out = expert_half(
+            lax.all_to_all(doubled, ("ctx", "req"), split_axis=0, concat_axis=0, tiled=True),
+            w_gate[0],
+            w_up[0],
+            w_down[0],
+        )
+        returned = lax.all_to_all(
+            partial_out, ("ctx", "req"), split_axis=0, concat_axis=0, tiled=True
+        ).reshape(expert_count, 2, piece, width)
+        pieces.append(
+            (returned[:, 0].astype(jnp.float32) + returned[:, 1].astype(jnp.float32)).astype(
+                jnp.bfloat16
+            )
+        )
+    results = jnp.concatenate(pieces, axis=1).reshape(expert_count * capacity, width)
     combine = jnp.sum(jnp.where(slot_hit, mixing[:, :, None], 0.0), axis=1)
     moe = jnp.dot(combine, results.astype(jnp.float32), precision=lax.Precision.HIGHEST)
     final = (hidden_state + moe).astype(jnp.bfloat16)

time: 200 us -> 211 us (1.055); the launches traced: 199 us -> 207 us
  blocking collectives: 77 us -> 50.4 us
  local copies, waits for them, and re-layouts: 21.2 us -> 38.9 us
  starting transfers between devices: 4.76 us -> 20 us
  waiting for transfers between devices: 47.5 us -> 34.7 us
  matrix products: 37.4 us -> 45.6 us
  other arithmetic: 10.4 us -> 16.3 us
    all_to_all x1, blocking collectives: 65 us -> 38.3 us  [body(): lax.all_to_all(doubled, ('ctx', 'req'), split_axis=0, concat_axis=0, tile...]
    all_to_all x1 -> x2, waiting for transfers between devices: 47.5 us -> 26.7 us  [body(): lax.all_to_all(partial_out, ('ctx', 'req'), split_axis=0, concat_axis=0,...]
    reshape x0 -> x4, local copies, waits for them, and re-layouts: none -> 16.2 us  [the longest x2 8.26 us: expert_half(): return partial_out.reshape(inputs.shape)]
    all_to_all x1 -> x2, starting transfers between devices: 4.76 us -> 13.3 us  [body(): lax.all_to_all(partial_out, ('ctx', 'req'), split_axis=0, concat_axis=0,...]
    all_to_all x0 -> x1, waiting for transfers between devices: none -> 7.93 us  [body(): lax.all_to_all(doubled, ('ctx', 'req'), split_axis=0, concat_axis=0, tile...]
    all_to_all x0 -> x1, starting transfers between devices: none -> 6.68 us  [body(): lax.all_to_all(doubled, ('ctx', 'req'), split_axis=0, concat_axis=0, tile...]
    convert_element_type x0 -> x2, other arithmetic: none -> 5.97 us  [body(): (returned[:, 0].astype(jnp.float32) + returned[:, 1].astype(jnp.float32))...]
    dot_general x1 -> x2, matrix products: 4.82 us -> 10.5 us  [expert_half(): gate_out = jnp.dot(flat_rows, gate_part, preferred_element_type=jnp.float32)]
  transfers between devices with their start and end apart: 1 -> 3, of which waited for: 1 -> 3; matrix products, arithmetic and copies ran while one was open for 3% -> 25% of each run, Pallas kernels for 0% -> 0%
where the time goes in v4:
time: 211 us; the launch traced here: 207 us
  blocking collectives  50.4 us (24%)
  matrix products  45.6 us (22%)
  local copies, waits for them, and re-layouts  38.9 us (18%)
  waiting for transfers between devices  34.7 us (16%)
  starting transfers between devices  20 us (9%)
  other arithmetic  16.3 us (8%)
    all_to_all x1, blocking collectives, body(): lax.all_to_all(doubled, ('ctx', 'req'), split_axis=0, concat_axis=0, tile...  38.3 us
    all_to_all x2, waiting for transfers between devices, body(): lax.all_to_all(partial_out, ('ctx', 'req'), split_axis=0, concat_axis=0,...  26.7 us
    dot_general x2, matrix products, expert_half(): jnp.dot(hidden, down_part, preferred_element_type=jnp.float32)  15.4 us
    all_to_all x2, starting transfers between devices, body(): lax.all_to_all(partial_out, ('ctx', 'req'), split_axis=0, concat_axis=0,...  13.3 us
    all_gather x1, blocking collectives, body(): gathered = lax.all_gather(packed, 'ctx')  12 us
    dot_general x2, matrix products, expert_half(): gate_out = jnp.dot(flat_rows, gate_part, preferred_element_type=jnp.float32)  10.5 us
    reshape x2, local copies, waits for them, and re-layouts, expert_half(): return partial_out.reshape(inputs.shape)  8.26 us
    all_to_all x1, waiting for transfers between devices, body(): lax.all_to_all(doubled, ('ctx', 'req'), split_axis=0, concat_axis=0, tile...  7.93 us
  transfers between devices with their start and end apart: 3, of which 3 were waited for; matrix products, arithmetic and copies ran while one was open for 25% of the time, Pallas kernels for 0%

profile of v4, /device:TPU:8, one launch (start us, length us, event | category | flops | bytes accessed | tf_op | source)
XLA Modules:
  0.0 206.9 jit_solution(621916525632490257)
XLA Ops:
  0.7 0.8 slice_bitcast_fusion.12
  2.2 0.8 select_reduce_fusion.4
  3.0 0.8 fusion.97
  3.7 0.7 convert_bitcast_fusion
  4.5 0.9 select_reduce_fusion.7
  6.2 4.3 %copy.67 = bf16[2048,576]{0,1:T(8,128)(2,1)} copy(bf16[2048,576]{1,0:T(8,128)(2,1)} %bitcast.149) | data formatting | bytes 4718592 | tf_op jit(solution)/shard_map/reshape | solution.py:212
  11.2 2.5 %fusion.11 = bf16[2048,576]{0,1:T(8,128)(2,1)S(1)} fusion(bf16[2048,576]{0,1:T(8,128)(2,1)} %copy.67, pred[2048]{0:T(1024)(128)(4,1)S(1)} %fusion.87, s32[4]{0:T(128)S(1)} %compare_select_fusion.2, bf16[4,32]{1,0:T(4,128)(2,1)S(1)} %get-tuple-element.29, bf16[4,32]{1,0:T(4,128)(2,1)S(1)} %get-tuple-element.30, bf16[4,512]{1,0:T(4,128)(2,1)S(1)} %slice_bitcast_fusion.11), kind=kOutput, calls=%fused_computation.15 | convolution fusion | flops 11818496 | bytes 4725264 | tf_op jit(solution)/shard_map/dot_general | solution.py:206
  14.4 1.4 fusion.45
  15.8 0.8 fusion.71
  16.5 0.8 reshape.537
  17.8 1.4 reshape.538
  19.2 0.8 select_reduce_fusion.6
  20.0 0.8 slice.108
  20.9 1.0 multiply_cosine_fusion
  21.9 0.9 maximum_maximum_fusion
  22.9 12.0 %all-gather = f32[384,576]{1,0:T(8,128)S(1)} all-gather(f32[96,576]{1,0:T(8,128)S(1)} %maximum_maximum_fusion), channel_id=2, replica_groups=mesh['ctx'=4,'req'=32] {'ctx'}, dimensions={0}, use_global_device_ids=true | all-gather | bytes 1105920 | tf_op jit(solution)/shard_map/all_gather | solution.py:252
  34.9 0.9 copy-done.2
  37.0 1.2 fusion.43
  38.3 2.4 %fusion.135 = f32[8,64]{1,0:T(8,128)} fusion(bf16[256,576,1]{1,0,2:T(8,128)(2,1)} %bitcast.157, bf16[64,8,32]{2,0,1:T(8,128)(2,1)S(1)} %get-tuple-element.16, bf16[64,8,32]{2,0,1:T(8,128)(2,1)S(1)} %get-tuple-element.15, bf16[64,8,512]{2,0,1:T(8,128)(2,1)} %bitcast.155, pred[64,256]{1,0:T(8,128)(4,1)S(1)} %broadcast_compare_fusion), kind=kOutput, calls=%fused_computation.226 | convolution fusion | flops 153420032 | bytes 903168 | tf_op jit(solution)/shard_map/sub | solution.py:273
  40.6 1.0 slice_bitcast_fusion.6
  42.1 2.4 %fusion.38 = bf16[64,8,512]{2,0,1:T(8,128)(2,1)} fusion(f32[64,8]{0,1:T(8,128)} %bitcast.168, bf16[256,576]{1,0:T(8,128)(2,1)S(1)} %bitcast.158, f32[8,64,256]{2,1,0:T(8,128)} %fusion.43, pred[64,256]{1,0:T(8,128)(4,1)S(1)} %broadcast_compare_fusion), kind=kOutput, calls=%fused_computation.37 | convolution fusion | flops 135136000 | bytes 1855488 | tf_op jit(solution)/shard_map/hqk,kc->qhc/dot_general | solution.py:275
  44.5 1.8 fusion.44
  46.4 3.2 %multiply_reduce_fusion = (f32[65]{0:T(128)S(1)}, f32[65,2048]{1,0:T(8,128)S(1)}) fusion(bf16[65,1024]{1,0:T(8,128)(2,1)S(1)} %bitcast.152, bf16[1024,2048]{1,0:T(8,128)(2,1)} %param.33, bf16[1,2048]{1,0:T(2,128)(2,1)S(1)} %dynamic-slice_bitcast_fusion, bf16[64,2048]{1,0:T(8,128)(2,1)S(1)} %bitcast.159), kind=kOutput, calls=%fused_computation.71 | convolution fusion | flops 273561536 | bytes 5126404 | tf_op jit(solution)/shard_map/dot_general | solution.py:289
  50.1 0.8 fusion.12
  50.9 1.1 fusion.133
  52.0 1.2 broadcast_in_dim.202
  53.3 38.3 %all_to_all.20 = bf16[128,4,2048]{2,1,0:T(4,128)(2,1)} all-to-all(bf16[128,4,2048]{2,1,0:T(4,128)(2,1)S(1)} %bitcast.146), channel_id=1, replica_groups=mesh['ctx'=4,'req'=32] {'ctx','req'}, dimensions={0} | all-to-all | bytes 4194304 | tf_op jit(solution)/shard_map/all_to_all | solution.py:329
  91.6 2.6 %broadcast_in_dim.203 = bf16[64,2,4,2048]{3,2,1,0:T(4,128)(2,1)} broadcast(bf16[64,4,2048]{2,1,0:T(4,128)(2,1)S(1)} %get-tuple-element.14), dimensions={0,2,3} | broadcast | bytes 3145728 | tf_op jit(solution)/shard_map/broadcast_in_dim | solution.py:325
  94.2 6.7 %all-to-all-start.2 = ((bf16[128,4,2048]{2,1,0:T(4,128)(2,1)}), bf16[128,4,2048]{2,1,0:T(4,128)(2,1)}, u32[]{:S(2)}, u32[]{:S(2)}) async-start(bf16[128,4,2048]{2,1,0:T(4,128)(2,1)} %bitcast.145), calls=%async_computation.2 | async-start | bytes 4194304 | tf_op jit(solution)/shard_map/all_to_all | solution.py:329
  100.9 4.0 %reshape.523 = bf16[512,2048]{1,0:T(8,128)(2,1)} reshape(bf16[128,4,2048]{2,1,0:T(4,128)(2,1)} %all_to_all.20) | data formatting | bytes 4194304 | tf_op jit(solution)/shard_map/reshape | solution.py:60
  104.8 5.2 %fusion.9 = f32[512,704]{0,1:T(8,128)} fusion(bf16[512,2048]{1,0:T(8,128)(2,1)} %reshape.523, bf16[1,2048,704]{1,2,0:T(8,128)(2,1)} %param.37), kind=kOutput, calls=%fused_computation.13 | convolution fusion | flops 1476395008 | bytes 6422528 | tf_op jit(solution)/shard_map/dot_general | solution.py:61
  110.0 7.7 %convolution_convert_fusion.2 = bf16[512,2048]{1,0:T(8,128)(2,1)} fusion(bf16[1,704,2048]{2,1,0:T(8,128)(2,1)S(1)} %copy-done, bf16[512,2048]{1,0:T(8,128)(2,1)} %reshape.523, bf16[1,2048,704]{1,2,0:T(8,128)(2,1)} %param.38, f32[512,704]{0,1:T(8,128)} %fusion.9), kind=kOutput, calls=%fused_computation.3 | convolution fusion | flops 2956001280 | bytes 11403264 | tf_op jit(solution)/shard_map/dot_general | solution.py:64
  117.7 4.2 %reshape.524 = bf16[128,4,2048]{2,1,0:T(4,128)(2,1)} reshape(bf16[512,2048]{1,0:T(8,128)(2,1)} %convolution_convert_fusion.2) | data formatting | bytes 4194304 | tf_op jit(solution)/shard_map/reshape | solution.py:67
  121.9 7.9 %all-to-all-done.2 = bf16[128,4,2048]{2,1,0:T(4,128)(2,1)} async-done(((bf16[128,4,2048]{2,1,0:T(4,128)(2,1)}), bf16[128,4,2048]{2,1,0:T(4,128)(2,1)}, u32[]{:S(2)}, u32[]{:S(2)}) %all-to-all-start.2) | async-done | bytes 2097184 | tf_op jit(solution)/shard_map/all_to_all | solution.py:329
  129.8 6.7 %all-to-all-start.1 = ((bf16[128,4,2048]{2,1,0:T(4,128)(2,1)}), bf16[128,4,2048]{2,1,0:T(4,128)(2,1)}, u32[]{:S(2)}, u32[]{:S(2)}) async-start(bf16[128,4,2048]{2,1,0:T(4,128)(2,1)} %reshape.524), calls=%async_computation.1 | async-start | bytes 4194304 | tf_op jit(solution)/shard_map/all_to_all | solution.py:334
  136.5 3.9 %reshape.527 = bf16[512,2048]{1,0:T(8,128)(2,1)} reshape(bf16[128,4,2048]{2,1,0:T(4,128)(2,1)} %all-to-all-done.2) | data formatting | bytes 4194304 | tf_op jit(solution)/shard_map/reshape | solution.py:60
  140.4 5.3 %fusion.7 = f32[512,704]{0,1:T(8,128)} fusion(bf16[512,2048]{1,0:T(8,128)(2,1)} %reshape.527, bf16[1,2048,704]{1,2,0:T(8,128)(2,1)} %param.37), kind=kOutput, calls=%fused_computation.11 | convolution fusion | flops 1476395008 | bytes 6422528 | tf_op jit(solution)/shard_map/dot_general | solution.py:61
  145.7 7.7 %convolution_convert_fusion.1 = bf16[512,2048]{1,0:T(8,128)(2,1)} fusion(bf16[1,704,2048]{2,1,0:T(8,128)(2,1)S(1)} %copy-done, bf16[512,2048]{1,0:T(8,128)(2,1)} %reshape.527, bf16[1,2048,704]{1,2,0:T(8,128)(2,1)} %param.38, f32[512,704]{0,1:T(8,128)} %fusion.7), kind=kOutput, calls=%fused_computation.2 | convolution fusion | flops 2956001280 | bytes 11403264 | tf_op jit(solution)/shard_map/dot_general | solution.py:64
  153.4 4.1 %reshape.528 = bf16[128,4,2048]{2,1,0:T(4,128)(2,1)} reshape(bf16[512,2048]{1,0:T(8,128)(2,1)} %convolution_convert_fusion.1) | data formatting | bytes 4194304 | tf_op jit(solution)/shard_map/reshape | solution.py:67
  157.5 8.0 %all-to-all-done.1 = bf16[128,4,2048]{2,1,0:T(4,128)(2,1)} async-done(((bf16[128,4,2048]{2,1,0:T(4,128)(2,1)}), bf16[128,4,2048]{2,1,0:T(4,128)(2,1)}, u32[]{:S(2)}, u32[]{:S(2)}) %all-to-all-start.1) | async-done | bytes 2097184 | tf_op jit(solution)/shard_map/all_to_all | solution.py:334
  165.5 6.7 %all-to-all-start.3 = ((bf16[128,4,2048]{2,1,0:T(4,128)(2,1)}), bf16[128,4,2048]{2,1,0:T(4,128)(2,1)}, u32[]{:S(2)}, u32[]{:S(2)}) async-start(bf16[128,4,2048]{2,1,0:T(4,128)(2,1)} %reshape.528), calls=%async_computation.3 | async-start | bytes 4194304 | tf_op jit(solution)/shard_map/all_to_all | solution.py:334
  172.1 4.3 %copy.77 = bf16[2048,576]{1,0:T(8,128)(2,1)} copy(bf16[2048,576]{0,1:T(8,128)(2,1)} %copy-done.1) | data formatting | bytes 4718592 | tf_op jit(solution)/shard_map/jit(_where)/select_n | solution.py:209
  176.5 1.5 fusion.48
  178.1 0.9 select_reduce_fusion
  178.9 3.4 %fusion.49 = bf16[64,4,2048]{2,1,0:T(4,128)(2,1)} fusion(bf16[64,2,4,2048]{3,2,1,0:T(4,128)(2,1)} %bitcast.31), kind=kLoop, calls=%fused_computation.52 | loop fusion | flops 2097152 | bytes 3145728 | tf_op jit(solution)/shard_map/convert_element_type | solution.py:338
  182.4 18.8 %all-to-all-done.3 = bf16[128,4,2048]{2,1,0:T(4,128)(2,1)} async-done(((bf16[128,4,2048]{2,1,0:T(4,128)(2,1)}), bf16[128,4,2048]{2,1,0:T(4,128)(2,1)}, u32[]{:S(2)}, u32[]{:S(2)}) %all-to-all-start.3) | async-done | bytes 2097184 | tf_op jit(solution)/shard_map/all_to_all | solution.py:334
  201.1 2.5 %fusion.50 = bf16[64,4,2048]{2,1,0:T(4,128)(2,1)S(1)} fusion(bf16[64,2,4,2048]{3,2,1,0:T(4,128)(2,1)} %bitcast.34), kind=kLoop, calls=%fused_computation.53 | loop fusion | flops 2097152 | bytes 3145728 | tf_op jit(solution)/shard_map/convert_element_type | solution.py:338
  203.7 1.9 fusion.15
  (87 shorter events, 7.0 us)
Async XLA Ops:
  0.6 109.4 %copy-start = (bf16[1,704,2048]{2,1,0:T(8,128)(2,1)S(1)}, bf16[1,704,2048]{2,1,0:T(8,128)(2,1)}, u32[]{:S(2)}) copy-start(bf16[1,704,2048]{2,1,0:T(8,128)(2,1)} %param.39) | copy-start | bytes 8650756
  0.7 10.3 %copy-start.17 = (f32[32]{0:T(128)}, f32[32]{0:T(128)S(1)}, u32[]{:S(2)}) copy-start(f32[32]{0:T(128)S(1)} %multiply_power_fusion) | copy-start | bytes 388
  6.1 4.9 %copy-start.14 = (bf16[4,1,8,64]{3,2,1,0:T(8,128)(2,1)S(1)}, bf16[4,1,8,64]{3,2,1,0:T(8,128)(2,1)}, u32[]{:S(2)}) copy-start(bf16[4,1,8,64]{3,2,1,0:T(8,128)(2,1)} %param.27) | copy-start | bytes 12292
  6.1 5.0 %copy-start.18 = (s32[4,1]{0,1:T(1,128)S(1)}, s32[4,1]{0,1:T(1,128)}, u32[]{:S(2)}) copy-start(s32[4,1]{0,1:T(1,128)} %param.29) | copy-start | bytes 52
  11.2 2.5 %copy-start.12 = (bf16[4,1,8,512]{3,2,1,0:T(8,128)(2,1)S(1)}, bf16[4,1,8,512]{3,2,1,0:T(8,128)(2,1)}, u32[]{:S(2)}) copy-start(bf16[4,1,8,512]{3,2,1,0:T(8,128)(2,1)} %param.26) | copy-start | bytes 98308
  13.7 2.0 copy-start.1
  14.4 1.4 copy-start.15
  15.7 20.1 %copy-start.10 = (bf16[1,64,8,64]{3,2,1,0:T(8,128)(2,1)S(1)}, bf16[1,64,8,64]{3,2,1,0:T(8,128)(2,1)}, u32[]{:S(2)}) copy-start(bf16[1,64,8,64]{3,2,1,0:T(8,128)(2,1)} %param.22) | copy-start | bytes 196612
  15.7 20.3 %copy-start.4 = (bf16[1,64,8,512]{3,2,1,0:T(8,128)(2,1)S(1)}, bf16[1,64,8,512]{3,2,1,0:T(8,128)(2,1)}, u32[]{:S(2)}) copy-start(bf16[1,64,8,512]{3,2,1,0:T(8,128)(2,1)} %param.21) | copy-start | bytes 1572868
  19.2 16.8 %copy-start.19 = (s32[256]{0:T(256)S(1)}, s32[256]{0:T(256)}, u32[]{:S(2)}) copy-start(s32[256]{0:T(256)} %and_select_fusion.1) | copy-start | bytes 3076
  19.2 16.8 %copy-start.20 = (s32[8]{0:T(128)S(1)}, s32[8]{0:T(128)}, u32[]{:S(2)}) copy-start(s32[8]{0:T(128)} %param.24) | copy-start | bytes 100
  34.9 0.9 copy-start.2
  35.9 0.7 copy-start.6
  36.2 0.8 copy-start.5
  38.3 3.9 %copy-start.7 = (bf16[4,64,576]{2,1,0:T(8,128)(2,1)S(1)}, bf16[4,64,576]{2,1,0:T(8,128)(2,1)}, u32[]{:S(2)}) copy-start(bf16[4,64,576]{2,1,0:T(8,128)(2,1)} %copy-done.6) | copy-start | bytes 884740
  44.5 1.9 copy-start.16
  44.5 1.9 copy-start.8
  46.4 3.2 %copy-start.11 = (s32[65,6]{0,1:T(8,128)S(1)}, s32[65,6]{0,1:T(8,128)}, u32[]{:S(2)}) copy-start(s32[65,6]{0,1:T(8,128)} %param.36) | copy-start | bytes 4684
  46.4 3.7 %copy-start.13 = (f32[2048]{0:T(1024)S(1)}, f32[2048]{0:T(1024)}, u32[]{:S(2)}) copy-start(f32[2048]{0:T(1024)} %param.34) | copy-start | bytes 24580
  94.2 35.7 %all-to-all-start.2 = ((bf16[128,4,2048]{2,1,0:T(4,128)(2,1)}), bf16[128,4,2048]{2,1,0:T(4,128)(2,1)}, u32[]{:S(2)}, u32[]{:S(2)}) async-start(bf16[128,4,2048]{2,1,0:T(4,128)(2,1)} %bitcast.145), calls=%async_computation.2 | async-start | bytes 4194304 | tf_op jit(solution)/shard_map/all_to_all | solution.py:329
  129.8 35.6 %all-to-all-start.1 = ((bf16[128,4,2048]{2,1,0:T(4,128)(2,1)}), bf16[128,4,2048]{2,1,0:T(4,128)(2,1)}, u32[]{:S(2)}, u32[]{:S(2)}) async-start(bf16[128,4,2048]{2,1,0:T(4,128)(2,1)} %reshape.524), calls=%async_computation.1 | async-start | bytes 4194304 | tf_op jit(solution)/shard_map/all_to_all | solution.py:334
  165.5 35.6 %all-to-all-start.3 = ((bf16[128,4,2048]{2,1,0:T(4,128)(2,1)}), bf16[128,4,2048]{2,1,0:T(4,128)(2,1)}, u32[]{:S(2)}, u32[]{:S(2)}) async-start(bf16[128,4,2048]{2,1,0:T(4,128)(2,1)} %reshape.528), calls=%async_computation.3 | async-start | bytes 4194304 | tf_op jit(solution)/shard_map/all_to_all | solution.py:334
  201.1 2.5 %copy-start.3 = (bf16[64,4,2048]{2,1,0:T(4,128)(2,1)S(1)}, bf16[64,4,2048]{2,1,0:T(4,128)(2,1)}, u32[]{:S(2)}) copy-start(bf16[64,4,2048]{2,1,0:T(4,128)(2,1)} %fusion.49) | copy-start | bytes 3145732
  201.1 2.6 %copy-start.9 = (f32[65,512]{1,0:T(8,128)S(1)}, f32[65,512]{1,0:T(8,128)}, u32[]{:S(2)}) copy-start(f32[65,512]{1,0:T(8,128)} %select_reduce_fusion) | copy-start | bytes 399364

commit v5 on v3

--- a/solution.py
+++ b/solution.py
@@ -144,6 +144,68 @@
         ],
         compiler_params=pltpu.CompilerParams(collective_id=collective_id, has_side_effects=True),
     )(x)
+
+
+def context_kernel(n_ctx, keys_ref, parts_ref, keys_out, parts_out, sems):
+    me = lax.axis_index("ctx")
+    row = lax.axis_index("req")
+    barrier = pltpu.get_barrier_semaphore()
+    for step in range(1, n_ctx):
+        other = lax.rem(me + step, n_ctx)
+        pl.semaphore_signal(barrier, inc=1, device_id=(other, row), device_id_type=MESH)
+    pl.semaphore_wait(barrier, n_ctx - 1)
+
+    def key_copy(source, target):
+        return pltpu.make_async_remote_copy(
+            src_ref=keys_ref,
+            dst_ref=keys_out.at[source],
+            send_sem=sems.at[0, target],
+            recv_sem=sems.at[1, source],
+            device_id=(target, row),
+            device_id_type=MESH,
+        )
+
+    def part_copy(source, target):
+        return pltpu.make_async_remote_copy(
+            src_ref=parts_ref.at[target],
+            dst_ref=parts_out.at[source],
+            send_sem=sems.at[2, target],
+            recv_sem=sems.at[3, source],
+            device_id=(target, row),
+            device_id_type=MESH,
+        )
+
+    own_keys = pltpu.make_async_copy(keys_ref, keys_out.at[me], sems.at[4, 0])
+    own_parts = pltpu.make_async_copy(parts_ref.at[me], parts_out.at[me], sems.at[4, 1])
+    own_keys.start()
+    own_parts.start()
+    for step in range(1, n_ctx):
+        other = lax.rem(me + step, n_ctx)
+        key_copy(me, other).start()
+        part_copy(me, other).start()
+    for step in range(1, n_ctx):
+        other = lax.rem(me + step, n_ctx)
+        source = lax.rem(me + n_ctx - step, n_ctx)
+        key_copy(me, other).wait_send()
+        part_copy(me, other).wait_send()
+        key_copy(source, me).wait_recv()
+        part_copy(source, me).wait_recv()
+    own_keys.wait()
+    own_parts.wait()
+
+
+def context_exchange(keys, parts, n_ctx):
+    return pl.pallas_call(
+        functools.partial(context_kernel, n_ctx),
+        out_shape=(
+            jax.ShapeDtypeStruct((n_ctx,) + keys.shape, keys.dtype),
+            jax.ShapeDtypeStruct(parts.shape, parts.dtype),
+        ),
+        in_specs=[pl.BlockSpec(memory_space=pl.ANY)] * 2,
+        out_specs=(pl.BlockSpec(memory_space=pl.ANY), pl.BlockSpec(memory_space=pl.ANY)),
+        scratch_shapes=[pltpu.SemaphoreType.DMA((5, n_ctx))],
+        compiler_params=pltpu.CompilerParams(collective_id=2, has_side_effects=True),
+    )(keys, parts)
 
 
 def body(
@@ -239,21 +301,20 @@
         preferred_element_type=jnp.float32,
     )
 
+    dec_share = request_count // ctx_count
+    part_width = 128 * ((DC + 2 + 127) // 128)
     dec_block = jnp.concatenate(
         [
-            local_accum.reshape(request_count * head_count, DC),
-            local_peak.reshape(-1, 1),
-            local_total.reshape(-1, 1),
-            jnp.zeros((request_count * head_count, row_width - DC - 2), jnp.float32),
+            local_accum,
+            local_peak[..., None],
+            local_total[..., None],
+            jnp.zeros((request_count, head_count, part_width - DC - 2), jnp.float32),
         ],
-        axis=1,
-    )
-    packed = jnp.concatenate([stored.astype(jnp.float32), dec_block], axis=0)
-    gathered = lax.all_gather(packed, "ctx")
-    moving = gathered[:, :shard_rows].reshape(ctx_count * shard_rows, row_width).astype(jnp.bfloat16)
-    dec_parts = gathered[:, shard_rows:].reshape(ctx_count, request_count, head_count, row_width)
-    dec_share = request_count // ctx_count
-    own_parts = lax.dynamic_slice_in_dim(dec_parts, ctx_index * dec_share, dec_share, 1)
+        axis=2,
+    ).reshape(ctx_count, dec_share * head_count, part_width)
+    keys_all, own_parts = context_exchange(stored, dec_block, ctx_count)
+    moving = keys_all.reshape(ctx_count * shard_rows, row_width)
+    own_parts = own_parts.reshape(ctx_count, dec_share, head_count, part_width)
     part_accum = own_parts[..., :DC]
     part_peak = own_parts[..., DC]
     part_total = own_parts[..., DC + 1]

time: 200 us -> 200 us (level)
  blocking collectives: 77 us -> 65.9 us
  Pallas kernels: 0 us -> 9.2 us
  other arithmetic: 10.4 us -> 13.4 us
  local copies, waits for them, and re-layouts: 21.2 us -> 18.7 us
    all_gather x1 -> x0, blocking collectives: 12 us -> none  [body(): gathered = lax.all_gather(packed, 'ctx')]
    pallas_call x0 -> x1, Pallas kernels: none -> 9.2 us  [context_exchange(): pl.pallas_call(functools.partial(context_kernel, n_ctx), out_shape=(jax.S...]
    reshape x3 -> x0, local copies, waits for them, and re-layouts: 3.12 us -> none  [the longest x1 1.37 us: body(): local_total.reshape(-1, 1)]
    unnamed x46 -> x40, local copies, waits for them, and re-layouts: 4.66 us -> 5.31 us
where the time goes in v5:
time: 200 us; the launch traced here: 199 us
  blocking collectives  65.9 us (33%)
  waiting for transfers between devices  47.5 us (24%)
  matrix products  39 us (20%)
  local copies, waits for them, and re-layouts  18.7 us (9%)
  other arithmetic  13.4 us (7%)
  Pallas kernels  9.2 us (5%)
  starting transfers between devices  4.76 us (2%)
    all_to_all x1, blocking collectives, body(): lax.all_to_all(doubled, ('ctx', 'req'), split_axis=0, concat_axis=0, tile...  65.9 us
    all_to_all x1, waiting for transfers between devices, body(): lax.all_to_all(partial_out, ('ctx', 'req'), split_axis=0, concat_axis=0,...  47.5 us
    dot_general x1, matrix products, expert_half(): jnp.dot(hidden, down_part, preferred_element_type=jnp.float32)  11.1 us
    pallas_call x1, Pallas kernels, context_exchange(): pl.pallas_call(functools.partial(context_kernel, n_ctx), out_shape=(jax.S...  9.2 us
    unnamed x40, local copies, waits for them, and re-layouts  5.31 us
    dot_general x1, matrix products, expert_half(): gate_out = jnp.dot(flat_rows, gate_part, preferred_element_type=jnp.float32)  4.82 us
    all_to_all x1, starting transfers between devices, body(): lax.all_to_all(partial_out, ('ctx', 'req'), split_axis=0, concat_axis=0,...  4.76 us
    select_n x1, local copies, waits for them, and re-layouts, body(): jnp.where(jnp.any(row_hit, axis=1)[:, None], written, cache_pool.reshape(...  4.33 us
  transfers between devices with their start and end apart: 1, of which 1 were waited for; matrix products, arithmetic and copies ran while one was open for 3% of the time, Pallas kernels for 0%

profile of v5, /device:TPU:8, one launch (start us, length us, event | category | flops | bytes accessed | tf_op | source)
XLA Modules:
  0.0 199.4 jit_solution(14206466025929796162)
XLA Ops:
  0.7 0.8 slice_bitcast_fusion.7
  1.5 0.7 slice_bitcast_fusion.6
  2.3 0.8 select_reduce_fusion.4
  3.0 0.8 fusion.83
  3.8 0.7 convert_bitcast_fusion.1
  4.5 0.9 select_reduce_fusion.7
  5.4 0.7 compare_select_fusion.2
  6.2 4.3 %copy.48 = bf16[2048,576]{0,1:T(8,128)(2,1)} copy(bf16[2048,576]{1,0:T(8,128)(2,1)} %bitcast.121) | data formatting | bytes 4718592 | tf_op jit(solution)/shard_map/reshape | solution.py:274
  11.3 2.5 %fusion.8 = bf16[2048,576]{0,1:T(8,128)(2,1)S(1)} fusion(bf16[2048,576]{0,1:T(8,128)(2,1)} %copy.48, pred[2048]{0:T(1024)(128)(4,1)S(1)} %fusion.73, s32[4]{0:T(128)S(1)} %compare_select_fusion.2, bf16[4,32]{1,0:T(4,128)(2,1)S(1)} %get-tuple-element.31, bf16[4,32]{1,0:T(4,128)(2,1)S(1)} %get-tuple-element.32, bf16[4,512]{1,0:T(4,128)(2,1)S(1)} %slice_bitcast_fusion.6), kind=kOutput, calls=%fused_computation.13 | convolution fusion | flops 11818496 | bytes 4725264 | tf_op jit(solution)/shard_map/dot_general | solution.py:268
  13.8 1.7 fusion.117
  15.5 1.4 fusion.23
  16.8 0.2 fusion.57
  17.0 0.6 and_select_fusion.1
  17.7 0.7 copy.50
  18.5 0.6 fusion.115
  19.1 0.8 multiply_cosine_fusion
  19.9 0.9 copy.65
  20.8 0.8 select_reduce_fusion.5
  21.6 0.6 fusion.98
  22.2 0.9 copy.64
  23.2 0.7 pad_maximum_fusion.keys_ref
  23.9 1.6 maximum_maximum_fusion.parts_ref
  25.5 9.2 %shard_map.211 = (bf16[4,64,576]{2,1,0:T(8,128)(2,1)}, f32[4,8,640]{2,1,0:T(8,128)}) custom-call(bf16[64,576]{1,0:T(8,128)(2,1)} %pad_maximum_fusion.keys_ref, f32[4,8,640]{2,1,0:T(8,128)} %maximum_maximum_fusion.parts_ref), custom_call_target="tpu_custom_call" | custom-call | tf_op jit(solution)/shard_map/pallas_call | solution.py:198
  34.7 0.8 broadcast_compare_fusion
  35.4 0.9 fusion.53
  36.4 0.6 copy-done.6
  37.1 2.4 %fusion.34 = f32[8,64,256]{2,1,0:T(8,128)} fusion(bf16[256,576,1]{1,0,2:T(8,128)(2,1)} %bitcast.142, bf16[64,8,32]{2,0,1:T(8,128)(2,1)S(1)} %get-tuple-element.18, bf16[64,8,32]{2,0,1:T(8,128)(2,1)S(1)} %get-tuple-element.17, bf16[64,8,512]{2,0,1:T(8,128)(2,1)} %bitcast.126, pred[64,256]{1,0:T(8,128)(4,1)S(1)} %broadcast_compare_fusion), kind=kOutput, calls=%fused_computation.35 | convolution fusion | flops 153026560 | bytes 1425408 | tf_op jit(solution)/shard_map/qhd,kd->hqk/dot_general | solution.py:329
  39.5 1.6 fusion.118
  41.2 0.2 slice_reduce_fusion
  41.6 2.4 %fusion.29 = bf16[64,8,512]{2,0,1:T(8,128)(2,1)} fusion(f32[64,8]{0,1:T(8,128)S(1)} %bitcast.145, bf16[256,576]{1,0:T(8,128)(2,1)} %bitcast.144, f32[8,64,256]{2,1,0:T(8,128)} %fusion.34, pred[64,256]{1,0:T(8,128)(4,1)S(1)} %broadcast_compare_fusion), kind=kOutput, calls=%fused_computation.29 | convolution fusion | flops 135136000 | bytes 1853440 | tf_op jit(solution)/shard_map/hqk,kc->qhc/dot_general | solution.py:336
  44.1 1.7 fusion.39
  45.9 0.7 copy.61
  46.6 3.2 %multiply_reduce_fusion = (f32[65]{0:T(128)S(1)}, f32[65,2048]{1,0:T(8,128)S(1)}) fusion(bf16[65,1024]{1,0:T(8,128)(2,1)} %bitcast.124, bf16[1024,2048]{1,0:T(8,128)(2,1)} %param.33, bf16[1,2048]{1,0:T(2,128)(2,1)S(1)} %dynamic-slice_bitcast_fusion, bf16[64,2048]{1,0:T(8,128)(2,1)} %bitcast.128), kind=kOutput, calls=%fused_computation.55 | convolution fusion | flops 273561536 | bytes 5126404 | tf_op jit(solution)/shard_map/dot_general | solution.py:350
  50.1 0.2 fusion.43
  50.3 0.8 fusion.9
  51.1 0.5 broadcast_in_dim.206
  51.6 65.9 %all_to_all.10 = bf16[128,8,2048]{2,1,0:T(8,128)(2,1)S(1)} all-to-all(bf16[128,8,2048]{2,1,0:T(8,128)(2,1)S(1)} %bitcast.120), channel_id=1, replica_groups=mesh['ctx'=4,'req'=32] {'ctx','req'}, dimensions={0} | all-to-all | bytes 8388608 | tf_op jit(solution)/shard_map/all_to_all | solution.py:385
  117.5 2.0 copy-done.2
  119.5 4.8 %fusion.3 = f32[1024,704]{0,1:T(8,128)} fusion(bf16[128,8,2048]{2,1,0:T(8,128)(2,1)S(1)} %all_to_all.10, bf16[1,2048,704]{1,2,0:T(8,128)(2,1)S(1)} %copy-done.17), kind=kOutput, calls=%fused_computation.3 | convolution fusion | flops 2952790016 | bytes 9961472 | tf_op jit(solution)/shard_map/dot_general | solution.py:61
  124.3 11.1 %convert_bitcast_fusion = bf16[128,8,2048]{2,1,0:T(8,128)(2,1)} fusion(bf16[1,704,2048]{2,1,0:T(8,128)(2,1)S(1)} %copy-done, f32[1024,704]{0,1:T(8,128)} %fusion.3, bf16[1,2048,704]{1,2,0:T(8,128)(2,1)} %param.38, bf16[128,8,2048]{2,1,0:T(8,128)(2,1)} %copy-done.2), kind=kOutput, calls=%fused_computation.6 | convolution fusion | flops 5912002560 | bytes 17039360 | tf_op jit(solution)/shard_map/dot_general | solution.py:64
  135.4 4.8 %all-to-all-start.1 = ((bf16[128,8,2048]{2,1,0:T(8,128)(2,1)}), bf16[128,8,2048]{2,1,0:T(8,128)(2,1)}, u32[]{:S(2)}, u32[]{:S(2)}) async-start(bf16[128,8,2048]{2,1,0:T(8,128)(2,1)} %convert_bitcast_fusion), calls=%async_computation.1 | async-start | bytes 8388608 | tf_op jit(solution)/shard_map/all_to_all | solution.py:390
  140.2 4.3 %copy.56 = bf16[2048,576]{1,0:T(8,128)(2,1)} copy(bf16[2048,576]{0,1:T(8,128)(2,1)} %copy-done.1) | data formatting | bytes 4718592 | tf_op jit(solution)/shard_map/jit(_where)/select_n | solution.py:271
  144.5 1.5 fusion.42
  146.1 0.9 select_reduce_fusion
  147.0 47.5 %all-to-all-done.1 = bf16[128,8,2048]{2,1,0:T(8,128)(2,1)} async-done(((bf16[128,8,2048]{2,1,0:T(8,128)(2,1)}), bf16[128,8,2048]{2,1,0:T(8,128)(2,1)}, u32[]{:S(2)}, u32[]{:S(2)}) %all-to-all-start.1) | async-done | bytes 4194336 | tf_op jit(solution)/shard_map/all_to_all | solution.py:390
  194.4 3.7 %fusion.12 = bf16[65,2048]{1,0:T(8,128)(2,1)S(1)} fusion(f32[65,2048]{1,0:T(8,128)S(1)} %get-tuple-element.38, f32[65,512]{1,0:T(8,128)} %select_reduce_fusion, bf16[64,2,8,2048]{3,2,1,0:T(8,128)(2,1)} %bitcast.33), kind=kOutput, calls=%fused_computation.19 | convolution fusion | flops 822349824 | bytes 5126144 | tf_op jit(solution)/shard_map/dot_general | solution.py:397
  198.1 0.7 slice_bitcast_fusion.2
  198.8 0.6 slice_bitcast_fusion.5
  (66 shorter events, 1.9 us)
Async XLA Ops:
  0.6 123.7 %copy-start = (bf16[1,704,2048]{2,1,0:T(8,128)(2,1)S(1)}, bf16[1,704,2048]{2,1,0:T(8,128)(2,1)}, u32[]{:S(2)}) copy-start(bf16[1,704,2048]{2,1,0:T(8,128)(2,1)} %param.39) | copy-start | bytes 8650756
  0.6 10.5 %copy-start.15 = (s32[4,1]{0,1:T(1,128)S(1)}, s32[4,1]{0,1:T(1,128)}, u32[]{:S(2)}) copy-start(s32[4,1]{0,1:T(1,128)} %param.29) | copy-start | bytes 52
  0.7 10.4 %copy-start.11 = (bf16[4,1,8,64]{3,2,1,0:T(8,128)(2,1)S(1)}, bf16[4,1,8,64]{3,2,1,0:T(8,128)(2,1)}, u32[]{:S(2)}) copy-start(bf16[4,1,8,64]{3,2,1,0:T(8,128)(2,1)} %param.27) | copy-start | bytes 12292
  0.7 10.4 %copy-start.13 = (f32[32]{0:T(128)}, f32[32]{0:T(128)S(1)}, u32[]{:S(2)}) copy-start(f32[32]{0:T(128)S(1)} %multiply_power_fusion) | copy-start | bytes 388
  13.8 1.7 copy-start.1
  13.8 4.7 %copy-start.16 = (s32[8]{0:T(128)S(1)}, s32[8]{0:T(128)}, u32[]{:S(2)}) copy-start(s32[8]{0:T(128)} %param.24) | copy-start | bytes 100
  13.8 5.3 %copy-start.8 = (bf16[1,64,576]{2,1,0:T(8,128)(2,1)S(1)}, bf16[1,64,576]{2,1,0:T(8,128)(2,1)}, u32[]{:S(2)}) copy-start(bf16[1,64,576]{2,1,0:T(8,128)(2,1)} %param.20) | copy-start | bytes 221188
  13.8 5.3 %copy-start.14 = (f32[32]{0:T(128)S(1)}, f32[32]{0:T(128)}, u32[]{:S(2)}) copy-start(f32[32]{0:T(128)} %copy-done.13) | copy-start | bytes 388
  13.8 8.4 %copy-start.3 = (bf16[1,64,8,512]{3,2,1,0:T(8,128)(2,1)S(1)}, bf16[1,64,8,512]{3,2,1,0:T(8,128)(2,1)}, u32[]{:S(2)}) copy-start(bf16[1,64,8,512]{3,2,1,0:T(8,128)(2,1)} %param.21) | copy-start | bytes 1572868
  23.1 16.3 %copy-start.4 = (bf16[1,64,8,512]{3,1,2,0:T(8,128)(2,1)S(1)}, bf16[1,64,8,512]{3,1,2,0:T(8,128)(2,1)}, u32[]{:S(2)}) copy-start(bf16[1,64,8,512]{3,1,2,0:T(8,128)(2,1)} %copy.64) | copy-start | bytes 1572868
  36.4 0.6 copy-start.6
  36.4 0.7 copy-start.7
  37.1 4.0 %copy-start.5 = (f32[4,8,640]{2,1,0:T(8,128)S(1)}, f32[4,8,640]{2,1,0:T(8,128)}, u32[]{:S(2)}) copy-start(f32[4,8,640]{2,1,0:T(8,128)} %get-tuple-element.6) | copy-start | bytes 245764
  41.6 5.0 %copy-start.12 = (bf16[4,1,2048]{2,0,1:T(4,128)(2,1)S(1)}, bf16[4,1,2048]{2,0,1:T(4,128)(2,1)}, u32[]{:S(2)}) copy-start(bf16[4,1,2048]{2,0,1:T(4,128)(2,1)} %param.28) | copy-start | bytes 49156
  45.8 4.0 %copy-start.9 = (s32[65,6]{0,1:T(8,128)S(1)}, s32[65,6]{0,1:T(8,128)}, u32[]{:S(2)}) copy-start(s32[65,6]{0,1:T(8,128)} %param.36) | copy-start | bytes 4684
  45.9 4.4 %copy-start.10 = (f32[2048]{0:T(1024)S(1)}, f32[2048]{0:T(1024)}, u32[]{:S(2)}) copy-start(f32[2048]{0:T(1024)} %param.34) | copy-start | bytes 24580
  51.6 67.9 %copy-start.17 = (bf16[1,2048,704]{1,2,0:T(8,128)(2,1)S(1)}, bf16[1,2048,704]{1,2,0:T(8,128)(2,1)}, u32[]{:S(2)}) copy-start(bf16[1,2048,704]{1,2,0:T(8,128)(2,1)} %param.37) | copy-start | bytes 8650756
  117.5 2.0 copy-start.2
  135.4 59.0 %all-to-all-start.1 = ((bf16[128,8,2048]{2,1,0:T(8,128)(2,1)}), bf16[128,8,2048]{2,1,0:T(8,128)(2,1)}, u32[]{:S(2)}, u32[]{:S(2)}) async-start(bf16[128,8,2048]{2,1,0:T(8,128)(2,1)} %convert_bitcast_fusion), calls=%async_computation.1 | async-start | bytes 8388608 | tf_op jit(solution)/shard_map/all_to_all | solution.py:390

commit v6 on v5

--- a/solution.py
+++ b/solution.py
@@ -243,8 +243,7 @@
     rotated = rotate(pre_qrope[0], cos_table[:, None, :], sin_table[:, None, :]).astype(
         jnp.bfloat16
     )
-    queries = jnp.concatenate([pre_qlat[0], rotated], axis=-1)
-    head_count = queries.shape[1]
+    head_count = pre_qlat.shape[2]
 
     lengths = cache_len[:, 0]
     tables = page_table[:, 0, :]
@@ -264,15 +263,10 @@
     target = jnp.where(
         owner_ctx == ctx_index, slot_of * page_rows + lengths % page_rows, slot_count * page_rows
     )
-    row_hit = jnp.arange(slot_count * page_rows)[:, None] == target[None, :]
-    written = jnp.dot(
-        row_hit.astype(jnp.bfloat16), new_rows, preferred_element_type=jnp.float32
-    ).astype(jnp.bfloat16)
-    flat_pool = jnp.where(
-        jnp.any(row_hit, axis=1)[:, None],
-        written,
-        cache_pool.reshape(slot_count * page_rows, row_width),
-    )
+    row_ids = jnp.arange(slot_count * page_rows)[:, None]
+    flat_pool = cache_pool.reshape(slot_count * page_rows, row_width)
+    for request in range(request_count):
+        flat_pool = jnp.where(row_ids == target[request], new_rows[request][None, :], flat_pool)
     page_valid = jnp.any(page_hit, axis=1)
     page_logical = jnp.sum(page_hit.astype(jnp.int32) * jnp.arange(pages_dev)[None, :, None], axis=1)
     page_start = (ctx_index * pages_dev + page_logical) * page_rows
@@ -286,20 +280,21 @@
         jnp.bfloat16
     )
     dec_queries = jnp.concatenate([dec_qlat[:, 0], query_rot], axis=-1)
+    flat_queries = dec_queries.reshape(request_count * head_count, row_width)
     dec_scores = (
-        jnp.einsum("rhd,kd->rhk", dec_queries, flat_pool, preferred_element_type=jnp.float32)
-        * score_scale
-    )
-    dec_masked = jnp.where(dec_visible, dec_scores, NEG_FILL)
-    local_peak = jnp.max(dec_masked, axis=-1)
-    dec_weights = jnp.where(dec_visible, jnp.exp(dec_masked - local_peak[..., None]), 0.0)
-    local_total = jnp.sum(dec_weights, axis=-1)
-    local_accum = jnp.einsum(
-        "rhk,kc->rhc",
-        dec_weights.astype(jnp.bfloat16),
+        jnp.dot(flat_pool, flat_queries.T, preferred_element_type=jnp.float32) * score_scale
+    ).reshape(slot_count * page_rows, request_count, head_count)
+    dec_seen = jnp.transpose(dec_visible[:, 0, :])[:, :, None]
+    dec_masked = jnp.where(dec_seen, dec_scores, NEG_FILL)
+    local_peak = jnp.max(dec_masked, axis=0)
+    dec_weights = jnp.where(dec_seen, jnp.exp(dec_masked - local_peak[None]), 0.0)
+    local_total = jnp.sum(dec_weights, axis=0)
+    local_accum = lax.dot_general(
+        dec_weights.astype(jnp.bfloat16).reshape(slot_count * page_rows, -1),
         flat_pool[:, :DC],
+        (((0,), (0,)), ((), ())),
         preferred_element_type=jnp.float32,
-    )
+    ).reshape(request_count, head_count, DC)
 
     dec_share = request_count // ctx_count
     part_width = 128 * ((DC + 2 + 127) // 128)
@@ -325,21 +320,28 @@
     own_mixed = (merged_accum / merged_total[..., None]).astype(jnp.bfloat16)
 
     key_pos_pre = block_position(block_order, jnp.arange(moving.shape[0]), shard_rows)
+    query_rows = shard_rows * head_count
     scores = (
-        jnp.einsum("qhd,kd->hqk", queries, moving, preferred_element_type=jnp.float32) * score_scale
-    )
-    visible = (key_pos_pre[None, :] <= own_pos[:, None])[None]
+        jnp.dot(
+            pre_qlat[0].reshape(query_rows, DC), moving[:, :DC].T,
+            preferred_element_type=jnp.float32,
+        )
+        + jnp.dot(
+            rotated.reshape(query_rows, DR), moving[:, DC:].T,
+            preferred_element_type=jnp.float32,
+        )
+    ) * score_scale
+    visible = jnp.repeat(key_pos_pre[None, :] <= own_pos[:, None], head_count, axis=0)
     masked = jnp.where(visible, scores, NEG_FILL)
     new_peak = jnp.max(masked, axis=-1)
     weights = jnp.where(visible, jnp.exp(masked - new_peak[..., None]), 0.0)
     totals = jnp.sum(weights, axis=-1)
-    accumulated = jnp.einsum(
-        "hqk,kc->qhc",
-        weights.astype(jnp.bfloat16),
-        moving[:, :DC],
-        preferred_element_type=jnp.float32,
-    )
-    pre_mixed = (accumulated / jnp.transpose(totals)[:, :, None]).astype(jnp.bfloat16)
+    accumulated = jnp.dot(
+        weights.astype(jnp.bfloat16), moving[:, :DC], preferred_element_type=jnp.float32
+    )
+    pre_mixed = (accumulated / totals[:, None]).astype(jnp.bfloat16).reshape(
+        shard_rows, head_count, DC
+    )
 
     own_resid = lax.dynamic_slice_in_dim(dec_resid[:, 0], ctx_index * dec_share, dec_share, 0)
     mixed_all = jnp.concatenate([pre_mixed, own_mixed], axis=0)

time: 200 us -> 193 us (0.965)
  other arithmetic: 13.4 us -> 27.1 us
  local copies, waits for them, and re-layouts: 18.7 us -> 9.03 us
  matrix products: 39 us -> 30.6 us
  waiting for transfers between devices: 47.5 us -> 44.6 us
    select_n x0 -> x2, other arithmetic: none -> 9.14 us  [body(): jnp.where(row_ids == target[request], new_rows[request][None, :], flat_pool)]
    dot_general x5, matrix products: 10.3 us -> 4.99 us  [the longest x1 1.33 us: body(): jnp.dot(pre_qlat[0].reshape(query_rows, DC), moving[:, :DC].T, preferred_...]
    eq x0 -> x4, other arithmetic: none -> 5.06 us  [body(): row_ids == target[request]]
    select_n x1 -> x0, local copies, waits for them, and re-layouts: 4.33 us -> none  [body(): jnp.where(jnp.any(row_hit, axis=1)[:, None], written, cache_pool.reshape(...]
    reshape x1 -> x3, local copies, waits for them, and re-layouts: 4.31 us -> 0.43 us  [the longest x2 0.28 us: body(): jnp.repeat(key_pos_pre[None, :] <= own_pos[:, None], head_count, axis=0)]
    all_to_all x1, waiting for transfers between devices: 47.5 us -> 44.6 us  [body(): lax.all_to_all(partial_out, ('ctx', 'req'), split_axis=0, concat_axis=0,...]
    unnamed x40 -> x48, local copies, waits for them, and re-layouts: 5.31 us -> 3.11 us
    concatenate x0 -> x3, other arithmetic: none -> 2.08 us  [the longest x2 2 us: rotate(): jnp.concatenate([leading * cos_table - trailing * sin_table, trailing * c...]
  transfers between devices with their start and end apart: 1 -> 1, of which waited for: 1 -> 1; matrix products, arithmetic and copies ran while one was open for 3% -> 5% of each run, Pallas kernels for 0% -> 0%
where the time goes in v6:
time: 193 us; the launch traced here: 192 us
  blocking collectives  65.9 us (34%)
  waiting for transfers between devices  44.6 us (23%)
  matrix products  30.6 us (16%)
  other arithmetic  27.1 us (14%)
  Pallas kernels  9.2 us (5%)
  local copies, waits for them, and re-layouts  9.03 us (5%)
  starting transfers between devices  4.77 us (2%)
    all_to_all x1, blocking collectives, body(): lax.all_to_all(doubled, ('ctx', 'req'), split_axis=0, concat_axis=0, tile...  65.9 us
    all_to_all x1, waiting for transfers between devices, body(): lax.all_to_all(partial_out, ('ctx', 'req'), split_axis=0, concat_axis=0,...  44.6 us
    dot_general x1, matrix products, expert_half(): jnp.dot(hidden, down_part, preferred_element_type=jnp.float32)  11.1 us
    pallas_call x1, Pallas kernels, context_exchange(): pl.pallas_call(functools.partial(context_kernel, n_ctx), out_shape=(jax.S...  9.2 us
    select_n x2, other arithmetic, body(): jnp.where(row_ids == target[request], new_rows[request][None, :], flat_pool)  9.14 us
    eq x4, other arithmetic, body(): row_ids == target[request]  5.06 us
    dot_general x1, matrix products, expert_half(): gate_out = jnp.dot(flat_rows, gate_part, preferred_element_type=jnp.float32)  4.82 us
    all_to_all x1, starting transfers between devices, body(): lax.all_to_all(partial_out, ('ctx', 'req'), split_axis=0, concat_axis=0,...  4.77 us
  transfers between devices with their start and end apart: 1, of which 1 were waited for; matrix products, arithmetic and copies ran while one was open for 5% of the time, Pallas kernels for 0%

profile of v6, /device:TPU:8, one launch (start us, length us, event | category | flops | bytes accessed | tf_op | source)
XLA Modules:
  0.0 192.4 jit_solution(3584220742806095128)
XLA Ops:
  0.7 0.8 slice_bitcast_fusion.5
  1.5 0.7 slice_bitcast_fusion.4
  2.2 0.8 select_reduce_fusion.4
  3.0 0.8 fusion.84
  3.8 0.7 convert_bitcast_fusion.1
  4.5 0.9 select_reduce_fusion.7
  5.4 0.7 compare_select_fusion.2
  6.1 0.7 fusion.109
  7.5 1.3 iota_compare_fusion.5
  8.8 1.2 iota_compare_fusion.7
  10.0 0.9 fusion.86
  10.9 0.7 fusion.74
  11.6 4.5 %fusion.10 = bf16[2048,576]{1,0:T(8,128)(2,1)S(1)} fusion(bf16[32,64,576]{2,1,0:T(8,128)(2,1)} %param.31, pred[2048]{0:T(1024)(128)(4,1)S(1)} %get-tuple-element.46, pred[2048]{0:T(1024)(128)(4,1)S(1)} %get-tuple-element.47, pred[2048]{0:T(1024)(128)(4,1)S(1)} %get-tuple-element.48, pred[2048]{0:T(1024)(128)(4,1)S(1)} %get-tuple-element.49, ...), kind=kLoop, calls=%fused_computation.15 | loop fusion | flops 4718592 | bytes 4731392 | tf_op jit(solution)/shard_map/jit(_where)/select_n | solution.py:269
  16.3 1.0 fusion.110
  17.3 1.1 fusion.17
  18.4 0.2 fusion.50
  18.7 0.7 broadcast_in_dim.283
  19.5 0.7 select_reduce_fusion.6
  20.2 0.8 multiply_cosine_fusion
  21.3 0.2 copy.43
  21.6 0.7 pad_maximum_fusion.keys_ref
  22.3 1.6 maximum_maximum_fusion.parts_ref
  23.9 9.2 %shard_map.211 = (bf16[4,64,576]{2,1,0:T(8,128)(2,1)}, f32[4,8,640]{2,1,0:T(8,128)}) custom-call(bf16[64,576]{1,0:T(8,128)(2,1)} %pad_maximum_fusion.keys_ref, f32[4,8,640]{2,1,0:T(8,128)} %maximum_maximum_fusion.parts_ref), custom_call_target="tpu_custom_call" | custom-call | tf_op jit(solution)/shard_map/pallas_call | solution.py:198
  33.1 1.3 convolution_bitcast_fusion
  34.5 1.1 fusion.55
  35.6 1.2 fusion.111
  37.0 0.4 fusion.23
  37.5 0.3 copy-done.4
  38.3 0.4 fusion.30
  38.8 0.7 copy.46
  39.5 3.2 %multiply_reduce_fusion = (f32[65]{0:T(128)S(1)}, f32[65,2048]{1,0:T(8,128)S(1)}) fusion(bf16[65,1024]{1,0:T(8,128)(2,1)} %bitcast.127, bf16[1024,2048]{1,0:T(8,128)(2,1)} %param.33, bf16[1,2048]{1,0:T(2,128)(2,1)S(1)} %dynamic-slice_bitcast_fusion, bf16[64,2048]{1,0:T(8,128)(2,1)} %bitcast.133), kind=kOutput, calls=%fused_computation.48 | convolution fusion | flops 273561536 | bytes 5126404 | tf_op jit(solution)/shard_map/dot_general | solution.py:352
  43.0 0.2 fusion.34
  43.2 0.8 fusion.7
  44.0 0.5 broadcast_in_dim.271
  44.5 65.9 %all_to_all.10 = bf16[128,8,2048]{2,1,0:T(8,128)(2,1)S(1)} all-to-all(bf16[128,8,2048]{2,1,0:T(8,128)(2,1)S(1)} %bitcast.126), channel_id=1, replica_groups=mesh['ctx'=4,'req'=32] {'ctx','req'}, dimensions={0} | all-to-all | bytes 8388608 | tf_op jit(solution)/shard_map/all_to_all | solution.py:387
  110.4 2.0 %copy-done.1 = bf16[128,8,2048]{2,1,0:T(8,128)(2,1)} copy-done((bf16[128,8,2048]{2,1,0:T(8,128)(2,1)}, bf16[128,8,2048]{2,1,0:T(8,128)(2,1)S(1)}, u32[]{:S(2)}) %copy-start.1) | copy-done | bytes 4194328
  112.4 4.8 %fusion.2 = f32[1024,704]{0,1:T(8,128)} fusion(bf16[128,8,2048]{2,1,0:T(8,128)(2,1)S(1)} %all_to_all.10, bf16[1,2048,704]{1,2,0:T(8,128)(2,1)S(1)} %copy-done.21), kind=kOutput, calls=%fused_computation.2 | convolution fusion | flops 2952790016 | bytes 9961472 | tf_op jit(solution)/shard_map/dot_general | solution.py:61
  117.2 11.1 %convert_bitcast_fusion = bf16[128,8,2048]{2,1,0:T(8,128)(2,1)} fusion(bf16[1,704,2048]{2,1,0:T(8,128)(2,1)S(1)} %copy-done, f32[1024,704]{0,1:T(8,128)} %fusion.2, bf16[1,2048,704]{1,2,0:T(8,128)(2,1)} %param.38, bf16[128,8,2048]{2,1,0:T(8,128)(2,1)} %copy-done.1), kind=kOutput, calls=%fused_computation.5 | convolution fusion | flops 5912002560 | bytes 17039360 | tf_op jit(solution)/shard_map/dot_general | solution.py:64
  128.4 4.8 %all-to-all-start.1 = ((bf16[128,8,2048]{2,1,0:T(8,128)(2,1)}), bf16[128,8,2048]{2,1,0:T(8,128)(2,1)}, u32[]{:S(2)}, u32[]{:S(2)}) async-start(bf16[128,8,2048]{2,1,0:T(8,128)(2,1)} %convert_bitcast_fusion), calls=%async_computation.1 | async-start | bytes 8388608 | tf_op jit(solution)/shard_map/all_to_all | solution.py:392
  133.1 1.3 fusion.79
  134.5 1.2 fusion.81
  135.7 1.5 fusion.33
  137.3 0.9 select_reduce_fusion
  138.1 4.6 %select_select_fusion = bf16[32,64,576]{2,1,0:T(8,128)(2,1)} fusion(bf16[32,64,576]{2,1,0:T(8,128)(2,1)} %param.31, pred[32,64]{1,0:T(8,128)(4,1)S(1)} %get-tuple-element.50, pred[32,64]{1,0:T(8,128)(4,1)S(1)} %get-tuple-element.51, pred[32,64]{1,0:T(8,128)(4,1)S(1)} %get-tuple-element.52, pred[32,64]{1,0:T(8,128)(4,1)S(1)} %get-tuple-element.53, ...), kind=kLoop, calls=%fused_computation.16 | loop fusion | flops 4718592 | bytes 4731392 | tf_op jit(solution)/shard_map/jit(_where)/select_n | solution.py:269
  142.7 44.6 %all-to-all-done.1 = bf16[128,8,2048]{2,1,0:T(8,128)(2,1)} async-done(((bf16[128,8,2048]{2,1,0:T(8,128)(2,1)}), bf16[128,8,2048]{2,1,0:T(8,128)(2,1)}, u32[]{:S(2)}, u32[]{:S(2)}) %all-to-all-start.1) | async-done | bytes 4194336 | tf_op jit(solution)/shard_map/all_to_all | solution.py:392
  187.4 3.7 %fusion.11 = bf16[65,2048]{1,0:T(8,128)(2,1)S(1)} fusion(f32[65,2048]{1,0:T(8,128)S(1)} %get-tuple-element.45, f32[65,512]{1,0:T(8,128)} %select_reduce_fusion, bf16[64,2,8,2048]{3,2,1,0:T(8,128)(2,1)} %bitcast.40), kind=kOutput, calls=%fused_computation.19 | convolution fusion | flops 822349824 | bytes 5126144 | tf_op jit(solution)/shard_map/dot_general | solution.py:399
  191.0 0.7 slice_bitcast_fusion.2
  191.7 0.6 slice_bitcast_fusion.3
  (83 shorter events, 2.4 us)
Async XLA Ops:
  0.6 116.6 %copy-start = (bf16[1,704,2048]{2,1,0:T(8,128)(2,1)S(1)}, bf16[1,704,2048]{2,1,0:T(8,128)(2,1)}, u32[]{:S(2)}) copy-start(bf16[1,704,2048]{2,1,0:T(8,128)(2,1)} %param.39) | copy-start | bytes 8650756
  0.6 15.6 %copy-start.7 = (bf16[4,1,8,512]{3,2,1,0:T(8,128)(2,1)S(1)}, bf16[4,1,8,512]{3,2,1,0:T(8,128)(2,1)}, u32[]{:S(2)}) copy-start(bf16[4,1,8,512]{3,2,1,0:T(8,128)(2,1)} %param.26) | copy-start | bytes 98308
  0.7 6.4 %copy-start.18 = (f32[32]{0:T(128)}, f32[32]{0:T(128)S(1)}, u32[]{:S(2)}) copy-start(f32[32]{0:T(128)S(1)} %multiply_power_fusion) | copy-start | bytes 388
  7.0 9.2 %copy-start.9 = (bf16[576]{0:T(1024)(128)(2,1)}, bf16[576]{0:T(1024)(128)(2,1)S(1)}, u32[]{:S(2)}) copy-start(bf16[576]{0:T(1024)(128)(2,1)S(1)} %get-tuple-element.12) | copy-start | bytes 3460
  7.0 9.2 %copy-start.11 = (bf16[576]{0:T(1024)(128)(2,1)}, bf16[576]{0:T(1024)(128)(2,1)S(1)}, u32[]{:S(2)}) copy-start(bf16[576]{0:T(1024)(128)(2,1)S(1)} %get-tuple-element.13) | copy-start | bytes 3460
  7.0 9.2 %copy-start.13 = (bf16[576]{0:T(1024)(128)(2,1)}, bf16[576]{0:T(1024)(128)(2,1)S(1)}, u32[]{:S(2)}) copy-start(bf16[576]{0:T(1024)(128)(2,1)S(1)} %get-tuple-element.14) | copy-start | bytes 3460
  7.0 9.2 %copy-start.15 = (bf16[576]{0:T(1024)(128)(2,1)}, bf16[576]{0:T(1024)(128)(2,1)S(1)}, u32[]{:S(2)}) copy-start(bf16[576]{0:T(1024)(128)(2,1)S(1)} %get-tuple-element.15) | copy-start | bytes 3460
  16.2 4.0 %copy-start.5 = (bf16[1,64,576]{2,1,0:T(8,128)(2,1)S(1)}, bf16[1,64,576]{2,1,0:T(8,128)(2,1)}, u32[]{:S(2)}) copy-start(bf16[1,64,576]{2,1,0:T(8,128)(2,1)} %param.20) | copy-start | bytes 221188
  16.2 4.0 %copy-start.19 = (f32[32]{0:T(128)S(1)}, f32[32]{0:T(128)}, u32[]{:S(2)}) copy-start(f32[32]{0:T(128)} %copy-done.18) | copy-start | bytes 388
  17.3 3.8 %copy-start.20 = (s32[8]{0:T(128)S(1)}, s32[8]{0:T(128)}, u32[]{:S(2)}) copy-start(s32[8]{0:T(128)} %param.24) | copy-start | bytes 100
  17.3 15.9 %copy-start.2 = (bf16[1,64,8,512]{3,2,1,0:T(8,128)(2,1)S(1)}, bf16[1,64,8,512]{3,2,1,0:T(8,128)(2,1)}, u32[]{:S(2)}) copy-start(bf16[1,64,8,512]{3,2,1,0:T(8,128)(2,1)} %param.21) | copy-start | bytes 1572868
  33.1 3.8 %copy-start.3 = (bf16[4,64,576]{2,1,0:T(8,128)(2,1)S(1)}, bf16[4,64,576]{2,1,0:T(8,128)(2,1)}, u32[]{:S(2)}) copy-start(bf16[4,64,576]{2,1,0:T(8,128)(2,1)} %get-tuple-element.5) | copy-start | bytes 884740
  37.0 0.9 copy-start.4
  37.0 1.4 copy-start.22
  37.3 2.1 %copy-start.17 = (bf16[4,1,2048]{2,0,1:T(4,128)(2,1)S(1)}, bf16[4,1,2048]{2,0,1:T(4,128)(2,1)}, u32[]{:S(2)}) copy-start(bf16[4,1,2048]{2,0,1:T(4,128)(2,1)} %param.28) | copy-start | bytes 49156
  38.7 4.0 %copy-start.6 = (s32[65,6]{0,1:T(8,128)S(1)}, s32[65,6]{0,1:T(8,128)}, u32[]{:S(2)}) copy-start(s32[65,6]{0,1:T(8,128)} %param.36) | copy-start | bytes 4684
  38.8 4.4 %copy-start.8 = (f32[2048]{0:T(1024)S(1)}, f32[2048]{0:T(1024)}, u32[]{:S(2)}) copy-start(f32[2048]{0:T(1024)} %param.34) | copy-start | bytes 24580
  44.5 67.9 %copy-start.21 = (bf16[1,2048,704]{1,2,0:T(8,128)(2,1)S(1)}, bf16[1,2048,704]{1,2,0:T(8,128)(2,1)}, u32[]{:S(2)}) copy-start(bf16[1,2048,704]{1,2,0:T(8,128)(2,1)} %param.37) | copy-start | bytes 8650756
  110.4 2.0 %copy-start.1 = (bf16[128,8,2048]{2,1,0:T(8,128)(2,1)}, bf16[128,8,2048]{2,1,0:T(8,128)(2,1)S(1)}, u32[]{:S(2)}) copy-start(bf16[128,8,2048]{2,1,0:T(8,128)(2,1)S(1)} %all_to_all.10) | copy-start | bytes 12582916
  128.3 9.8 %copy-start.10 = (bf16[576]{0:T(1024)(128)(2,1)S(1)}, bf16[576]{0:T(1024)(128)(2,1)}, u32[]{:S(2)}) copy-start(bf16[576]{0:T(1024)(128)(2,1)} %copy-done.9) | copy-start | bytes 3460
  128.3 9.8 %copy-start.12 = (bf16[576]{0:T(1024)(128)(2,1)S(1)}, bf16[576]{0:T(1024)(128)(2,1)}, u32[]{:S(2)}) copy-start(bf16[576]{0:T(1024)(128)(2,1)} %copy-done.11) | copy-start | bytes 3460
  128.3 9.8 %copy-start.14 = (bf16[576]{0:T(1024)(128)(2,1)S(1)}, bf16[576]{0:T(1024)(128)(2,1)}, u32[]{:S(2)}) copy-start(bf16[576]{0:T(1024)(128)(2,1)} %copy-done.13) | copy-start | bytes 3460
  128.3 9.8 %copy-start.16 = (bf16[576]{0:T(1024)(128)(2,1)S(1)}, bf16[576]{0:T(1024)(128)(2,1)}, u32[]{:S(2)}) copy-start(bf16[576]{0:T(1024)(128)(2,1)} %copy-done.15) | copy-start | bytes 3460
  128.4 59.0 %all-to-all-start.1 = ((bf16[128,8,2048]{2,1,0:T(8,128)(2,1)}), bf16[128,8,2048]{2,1,0:T(8,128)(2,1)}, u32[]{:S(2)}, u32[]{:S(2)}) async-start(bf16[128,8,2048]{2,1,0:T(8,128)(2,1)} %convert_bitcast_fusion), calls=%async_computation.1 | async-start | bytes 8388608 | tf_op jit(solution)/shard_map/all_to_all | solution.py:392

commit v7 on v6

--- a/solution.py
+++ b/solution.py
@@ -201,8 +201,8 @@
             jax.ShapeDtypeStruct((n_ctx,) + keys.shape, keys.dtype),
             jax.ShapeDtypeStruct(parts.shape, parts.dtype),
         ),
-        in_specs=[pl.BlockSpec(memory_space=pl.ANY)] * 2,
-        out_specs=(pl.BlockSpec(memory_space=pl.ANY), pl.BlockSpec(memory_space=pl.ANY)),
+        in_specs=[pl.BlockSpec(memory_space=pltpu.VMEM)] * 2,
+        out_specs=(pl.BlockSpec(memory_space=pltpu.VMEM), pl.BlockSpec(memory_space=pltpu.VMEM)),
         scratch_shapes=[pltpu.SemaphoreType.DMA((5, n_ctx))],
         compiler_params=pltpu.CompilerParams(collective_id=2, has_side_effects=True),
     )(keys, parts)

time: 193 us -> 195 us (1.010)
  no operation moved by 1% of the time
where the time goes in v7:
time: 195 us; the launch traced here: 194 us
  blocking collectives  65.8 us (34%)
  waiting for transfers between devices  44.6 us (23%)
  matrix products  30.6 us (16%)
  other arithmetic  27.1 us (14%)
  Pallas kernels  10.7 us (5%)
  local copies, waits for them, and re-layouts  9.04 us (5%)
  starting transfers between devices  4.77 us (2%)
    all_to_all x1, blocking collectives, body(): lax.all_to_all(doubled, ('ctx', 'req'), split_axis=0, concat_axis=0, tile...  65.8 us
    all_to_all x1, waiting for transfers between devices, body(): lax.all_to_all(partial_out, ('ctx', 'req'), split_axis=0, concat_axis=0,...  44.6 us
    dot_general x1, matrix products, expert_half(): jnp.dot(hidden, down_part, preferred_element_type=jnp.float32)  11.1 us
    pallas_call x1, Pallas kernels, context_exchange(): pl.pallas_call(functools.partial(context_kernel, n_ctx), out_shape=(jax.S...  10.7 us
    select_n x2, other arithmetic, body(): jnp.where(row_ids == target[request], new_rows[request][None, :], flat_pool)  9.14 us
    eq x4, other arithmetic, body(): row_ids == target[request]  5.06 us
    dot_general x1, matrix products, expert_half(): gate_out = jnp.dot(flat_rows, gate_part, preferred_element_type=jnp.float32)  4.82 us
    all_to_all x1, starting transfers between devices, body(): lax.all_to_all(partial_out, ('ctx', 'req'), split_axis=0, concat_axis=0,...  4.77 us
  transfers between devices with their start and end apart: 1, of which 1 were waited for; matrix products, arithmetic and copies ran while one was open for 5% of the time, Pallas kernels for 0%

profile of v7, /device:TPU:8, one launch (start us, length us, event | category | flops | bytes accessed | tf_op | source)
XLA Modules:
  0.0 193.8 jit_solution(11208594857656932618)
XLA Ops:
  0.7 0.8 slice_bitcast_fusion.5
  1.5 0.7 slice_bitcast_fusion.4
  2.2 0.8 select_reduce_fusion.4
  3.0 0.8 fusion.84
  3.8 0.7 convert_bitcast_fusion.1
  4.5 0.9 select_reduce_fusion.7
  5.4 0.7 compare_select_fusion.2
  6.1 0.7 fusion.109
  7.5 1.3 iota_compare_fusion.5
  8.8 1.2 iota_compare_fusion.7
  10.0 0.9 fusion.86
  10.9 0.7 fusion.74
  11.6 4.5 %fusion.10 = bf16[2048,576]{1,0:T(8,128)(2,1)S(1)} fusion(bf16[32,64,576]{2,1,0:T(8,128)(2,1)} %param.31, pred[2048]{0:T(1024)(128)(4,1)S(1)} %get-tuple-element.46, pred[2048]{0:T(1024)(128)(4,1)S(1)} %get-tuple-element.47, pred[2048]{0:T(1024)(128)(4,1)S(1)} %get-tuple-element.48, pred[2048]{0:T(1024)(128)(4,1)S(1)} %get-tuple-element.49, ...), kind=kLoop, calls=%fused_computation.15 | loop fusion | flops 4718592 | bytes 4731392 | tf_op jit(solution)/shard_map/jit(_where)/select_n | solution.py:269
  16.3 1.0 fusion.110
  17.3 1.1 fusion.17
  18.4 0.2 fusion.50
  18.7 0.7 broadcast_in_dim.283
  19.5 0.7 select_reduce_fusion.6
  20.2 0.8 multiply_cosine_fusion
  21.3 0.2 copy.43
  21.6 0.7 pad_maximum_fusion.keys_ref
  22.3 1.6 maximum_maximum_fusion.parts_ref
  23.9 10.7 %shard_map.211 = (bf16[4,64,576]{2,1,0:T(8,128)(2,1)}, f32[4,8,640]{2,1,0:T(8,128)}) custom-call(bf16[64,576]{1,0:T(8,128)(2,1)} %pad_maximum_fusion.keys_ref, f32[4,8,640]{2,1,0:T(8,128)} %maximum_maximum_fusion.parts_ref), custom_call_target="tpu_custom_call" | custom-call | tf_op jit(solution)/shard_map/pallas_call | solution.py:198
  34.7 1.3 convolution_bitcast_fusion
  36.0 1.1 fusion.55
  37.2 1.2 fusion.111
  38.5 0.4 fusion.23
  39.1 0.3 copy-done.4
  39.9 0.3 fusion.30
  40.3 0.7 copy.46
  41.0 3.2 %multiply_reduce_fusion = (f32[65]{0:T(128)S(1)}, f32[65,2048]{1,0:T(8,128)S(1)}) fusion(bf16[65,1024]{1,0:T(8,128)(2,1)} %bitcast.127, bf16[1024,2048]{1,0:T(8,128)(2,1)} %param.33, bf16[1,2048]{1,0:T(2,128)(2,1)S(1)} %dynamic-slice_bitcast_fusion, bf16[64,2048]{1,0:T(8,128)(2,1)} %bitcast.133), kind=kOutput, calls=%fused_computation.48 | convolution fusion | flops 273561536 | bytes 5126404 | tf_op jit(solution)/shard_map/dot_general | solution.py:352
  44.5 0.2 fusion.34
  44.7 0.8 fusion.7
  45.5 0.5 broadcast_in_dim.271
  46.1 65.8 %all_to_all.10 = bf16[128,8,2048]{2,1,0:T(8,128)(2,1)S(1)} all-to-all(bf16[128,8,2048]{2,1,0:T(8,128)(2,1)S(1)} %bitcast.126), channel_id=1, replica_groups=mesh['ctx'=4,'req'=32] {'ctx','req'}, dimensions={0} | all-to-all | bytes 8388608 | tf_op jit(solution)/shard_map/all_to_all | solution.py:387
  111.9 2.0 %copy-done.1 = bf16[128,8,2048]{2,1,0:T(8,128)(2,1)} copy-done((bf16[128,8,2048]{2,1,0:T(8,128)(2,1)}, bf16[128,8,2048]{2,1,0:T(8,128)(2,1)S(1)}, u32[]{:S(2)}) %copy-start.1) | copy-done | bytes 4194328
  113.8 4.8 %fusion.2 = f32[1024,704]{0,1:T(8,128)} fusion(bf16[128,8,2048]{2,1,0:T(8,128)(2,1)S(1)} %all_to_all.10, bf16[1,2048,704]{1,2,0:T(8,128)(2,1)S(1)} %copy-done.21), kind=kOutput, calls=%fused_computation.2 | convolution fusion | flops 2952790016 | bytes 9961472 | tf_op jit(solution)/shard_map/dot_general | solution.py:61
  118.7 11.1 %convert_bitcast_fusion = bf16[128,8,2048]{2,1,0:T(8,128)(2,1)} fusion(bf16[1,704,2048]{2,1,0:T(8,128)(2,1)S(1)} %copy-done, f32[1024,704]{0,1:T(8,128)} %fusion.2, bf16[1,2048,704]{1,2,0:T(8,128)(2,1)} %param.38, bf16[128,8,2048]{2,1,0:T(8,128)(2,1)} %copy-done.1), kind=kOutput, calls=%fused_computation.5 | convolution fusion | flops 5912002560 | bytes 17039360 | tf_op jit(solution)/shard_map/dot_general | solution.py:64
  129.8 4.8 %all-to-all-start.1 = ((bf16[128,8,2048]{2,1,0:T(8,128)(2,1)}), bf16[128,8,2048]{2,1,0:T(8,128)(2,1)}, u32[]{:S(2)}, u32[]{:S(2)}) async-start(bf16[128,8,2048]{2,1,0:T(8,128)(2,1)} %convert_bitcast_fusion), calls=%async_computation.1 | async-start | bytes 8388608 | tf_op jit(solution)/shard_map/all_to_all | solution.py:392
  134.6 1.3 fusion.79
  135.9 1.2 fusion.81
  137.1 1.5 fusion.33
  138.7 0.9 select_reduce_fusion
  139.6 4.6 %select_select_fusion = bf16[32,64,576]{2,1,0:T(8,128)(2,1)} fusion(bf16[32,64,576]{2,1,0:T(8,128)(2,1)} %param.31, pred[32,64]{1,0:T(8,128)(4,1)S(1)} %get-tuple-element.50, pred[32,64]{1,0:T(8,128)(4,1)S(1)} %get-tuple-element.51, pred[32,64]{1,0:T(8,128)(4,1)S(1)} %get-tuple-element.52, pred[32,64]{1,0:T(8,128)(4,1)S(1)} %get-tuple-element.53, ...), kind=kLoop, calls=%fused_computation.16 | loop fusion | flops 4718592 | bytes 4731392 | tf_op jit(solution)/shard_map/jit(_where)/select_n | solution.py:269
  144.2 44.6 %all-to-all-done.1 = bf16[128,8,2048]{2,1,0:T(8,128)(2,1)} async-done(((bf16[128,8,2048]{2,1,0:T(8,128)(2,1)}), bf16[128,8,2048]{2,1,0:T(8,128)(2,1)}, u32[]{:S(2)}, u32[]{:S(2)}) %all-to-all-start.1) | async-done | bytes 4194336 | tf_op jit(solution)/shard_map/all_to_all | solution.py:392
  188.8 3.7 %fusion.11 = bf16[65,2048]{1,0:T(8,128)(2,1)S(1)} fusion(f32[65,2048]{1,0:T(8,128)S(1)} %get-tuple-element.45, f32[65,512]{1,0:T(8,128)} %select_reduce_fusion, bf16[64,2,8,2048]{3,2,1,0:T(8,128)(2,1)} %bitcast.40), kind=kOutput, calls=%fused_computation.19 | convolution fusion | flops 822349824 | bytes 5126144 | tf_op jit(solution)/shard_map/dot_general | solution.py:399
  192.5 0.7 slice_bitcast_fusion.2
  193.2 0.6 slice_bitcast_fusion.3
  (83 shorter events, 2.4 us)
Async XLA Ops:
  0.6 118.0 %copy-start = (bf16[1,704,2048]{2,1,0:T(8,128)(2,1)S(1)}, bf16[1,704,2048]{2,1,0:T(8,128)(2,1)}, u32[]{:S(2)}) copy-start(bf16[1,704,2048]{2,1,0:T(8,128)(2,1)} %param.39) | copy-start | bytes 8650756
  0.6 15.6 %copy-start.7 = (bf16[4,1,8,512]{3,2,1,0:T(8,128)(2,1)S(1)}, bf16[4,1,8,512]{3,2,1,0:T(8,128)(2,1)}, u32[]{:S(2)}) copy-start(bf16[4,1,8,512]{3,2,1,0:T(8,128)(2,1)} %param.26) | copy-start | bytes 98308
  0.7 6.4 %copy-start.18 = (f32[32]{0:T(128)}, f32[32]{0:T(128)S(1)}, u32[]{:S(2)}) copy-start(f32[32]{0:T(128)S(1)} %multiply_power_fusion) | copy-start | bytes 388
  7.0 9.2 %copy-start.9 = (bf16[576]{0:T(1024)(128)(2,1)}, bf16[576]{0:T(1024)(128)(2,1)S(1)}, u32[]{:S(2)}) copy-start(bf16[576]{0:T(1024)(128)(2,1)S(1)} %get-tuple-element.12) | copy-start | bytes 3460
  7.0 9.2 %copy-start.11 = (bf16[576]{0:T(1024)(128)(2,1)}, bf16[576]{0:T(1024)(128)(2,1)S(1)}, u32[]{:S(2)}) copy-start(bf16[576]{0:T(1024)(128)(2,1)S(1)} %get-tuple-element.13) | copy-start | bytes 3460
  7.0 9.2 %copy-start.13 = (bf16[576]{0:T(1024)(128)(2,1)}, bf16[576]{0:T(1024)(128)(2,1)S(1)}, u32[]{:S(2)}) copy-start(bf16[576]{0:T(1024)(128)(2,1)S(1)} %get-tuple-element.14) | copy-start | bytes 3460
  7.0 9.2 %copy-start.15 = (bf16[576]{0:T(1024)(128)(2,1)}, bf16[576]{0:T(1024)(128)(2,1)S(1)}, u32[]{:S(2)}) copy-start(bf16[576]{0:T(1024)(128)(2,1)S(1)} %get-tuple-element.15) | copy-start | bytes 3460
  16.2 4.0 %copy-start.5 = (bf16[1,64,576]{2,1,0:T(8,128)(2,1)S(1)}, bf16[1,64,576]{2,1,0:T(8,128)(2,1)}, u32[]{:S(2)}) copy-start(bf16[1,64,576]{2,1,0:T(8,128)(2,1)} %param.20) | copy-start | bytes 221188
  16.2 4.0 %copy-start.19 = (f32[32]{0:T(128)S(1)}, f32[32]{0:T(128)}, u32[]{:S(2)}) copy-start(f32[32]{0:T(128)} %copy-done.18) | copy-start | bytes 388
  17.3 3.8 %copy-start.20 = (s32[8]{0:T(128)S(1)}, s32[8]{0:T(128)}, u32[]{:S(2)}) copy-start(s32[8]{0:T(128)} %param.24) | copy-start | bytes 100
  17.3 17.4 %copy-start.2 = (bf16[1,64,8,512]{3,2,1,0:T(8,128)(2,1)S(1)}, bf16[1,64,8,512]{3,2,1,0:T(8,128)(2,1)}, u32[]{:S(2)}) copy-start(bf16[1,64,8,512]{3,2,1,0:T(8,128)(2,1)} %param.21) | copy-start | bytes 1572868
  34.7 3.8 %copy-start.3 = (bf16[4,64,576]{2,1,0:T(8,128)(2,1)S(1)}, bf16[4,64,576]{2,1,0:T(8,128)(2,1)}, u32[]{:S(2)}) copy-start(bf16[4,64,576]{2,1,0:T(8,128)(2,1)} %get-tuple-element.5) | copy-start | bytes 884740
  38.5 0.9 copy-start.4
  38.5 1.4 copy-start.22
  38.9 2.1 %copy-start.17 = (bf16[4,1,2048]{2,0,1:T(4,128)(2,1)S(1)}, bf16[4,1,2048]{2,0,1:T(4,128)(2,1)}, u32[]{:S(2)}) copy-start(bf16[4,1,2048]{2,0,1:T(4,128)(2,1)} %param.28) | copy-start | bytes 49156
  40.3 4.0 %copy-start.6 = (s32[65,6]{0,1:T(8,128)S(1)}, s32[65,6]{0,1:T(8,128)}, u32[]{:S(2)}) copy-start(s32[65,6]{0,1:T(8,128)} %param.36) | copy-start | bytes 4684
  40.3 4.4 %copy-start.8 = (f32[2048]{0:T(1024)S(1)}, f32[2048]{0:T(1024)}, u32[]{:S(2)}) copy-start(f32[2048]{0:T(1024)} %param.34) | copy-start | bytes 24580
  46.1 67.8 %copy-start.21 = (bf16[1,2048,704]{1,2,0:T(8,128)(2,1)S(1)}, bf16[1,2048,704]{1,2,0:T(8,128)(2,1)}, u32[]{:S(2)}) copy-start(bf16[1,2048,704]{1,2,0:T(8,128)(2,1)} %param.37) | copy-start | bytes 8650756
  111.9 2.0 %copy-start.1 = (bf16[128,8,2048]{2,1,0:T(8,128)(2,1)}, bf16[128,8,2048]{2,1,0:T(8,128)(2,1)S(1)}, u32[]{:S(2)}) copy-start(bf16[128,8,2048]{2,1,0:T(8,128)(2,1)S(1)} %all_to_all.10) | copy-start | bytes 12582916
  129.8 9.8 %copy-start.10 = (bf16[576]{0:T(1024)(128)(2,1)S(1)}, bf16[576]{0:T(1024)(128)(2,1)}, u32[]{:S(2)}) copy-start(bf16[576]{0:T(1024)(128)(2,1)} %copy-done.9) | copy-start | bytes 3460
  129.8 9.8 %copy-start.12 = (bf16[576]{0:T(1024)(128)(2,1)S(1)}, bf16[576]{0:T(1024)(128)(2,1)}, u32[]{:S(2)}) copy-start(bf16[576]{0:T(1024)(128)(2,1)} %copy-done.11) | copy-start | bytes 3460
  129.8 9.8 %copy-start.14 = (bf16[576]{0:T(1024)(128)(2,1)S(1)}, bf16[576]{0:T(1024)(128)(2,1)}, u32[]{:S(2)}) copy-start(bf16[576]{0:T(1024)(128)(2,1)} %copy-done.13) | copy-start | bytes 3460
  129.8 9.8 %copy-start.16 = (bf16[576]{0:T(1024)(128)(2,1)S(1)}, bf16[576]{0:T(1024)(128)(2,1)}, u32[]{:S(2)}) copy-start(bf16[576]{0:T(1024)(128)(2,1)} %copy-done.15) | copy-start | bytes 3460
  129.8 59.0 %all-to-all-start.1 = ((bf16[128,8,2048]{2,1,0:T(8,128)(2,1)}), bf16[128,8,2048]{2,1,0:T(8,128)(2,1)}, u32[]{:S(2)}, u32[]{:S(2)}) async-start(bf16[128,8,2048]{2,1,0:T(8,128)(2,1)} %convert_bitcast_fusion), calls=%async_computation.1 | async-start | bytes 8388608 | tf_op jit(solution)/shard_map/all_to_all | solution.py:392

commit v8 on v6

--- a/solution.py
+++ b/solution.py
@@ -78,7 +78,7 @@
     return (new_peak, merged_total, merged_accum)
 
 
-def exchange_kernel(n_req, total, x_ref, out_ref, send_sem, recv_sem, local_sem):
+def exchange_kernel(n_req, total, window, x_ref, out_ref, send_sem, recv_sem, local_sem):
     me = lax.axis_index("ctx") * n_req + lax.axis_index("req")
 
     def device(d):
@@ -118,12 +118,22 @@
 
     def send(k, carry):
         outgoing(lax.rem(me + k, total)).start()
+
+        @pl.when(k > window)
+        def _():
+            outgoing(lax.rem(me + k - window, total)).wait_send()
+
         return carry
 
     lax.fori_loop(1, total, send, 0)
 
+    def drain(k, carry):
+        outgoing(lax.rem(me + k, total)).wait_send()
+        return carry
+
+    lax.fori_loop(max(1, total - window), total, drain, 0)
+
     def finish(k, carry):
-        outgoing(lax.rem(me + k, total)).wait_send()
         incoming(lax.rem(me + total - k, total)).wait_recv()
         return carry
 
@@ -133,7 +143,7 @@
 
 def exchange(x, n_req, total, collective_id):
     return pl.pallas_call(
-        functools.partial(exchange_kernel, n_req, total),
+        functools.partial(exchange_kernel, n_req, total, min(16, total // 4)),
         out_shape=jax.ShapeDtypeStruct(x.shape, x.dtype),
         in_specs=[pl.BlockSpec(memory_space=pl.ANY)],
         out_specs=pl.BlockSpec(memory_space=pl.ANY),
@@ -383,15 +393,16 @@
     doubled = jnp.broadcast_to(outgoing[:, None], (expert_count, 2, capacity, width)).reshape(
         devices, capacity, width
     )
+    req_count = lax.axis_size("req")
     partial_out = expert_half(
-        lax.all_to_all(doubled, ("ctx", "req"), split_axis=0, concat_axis=0, tiled=True),
+        exchange(doubled, req_count, devices, 0),
         w_gate[0],
         w_up[0],
         w_down[0],
     )
-    returned = lax.all_to_all(
-        partial_out, ("ctx", "req"), split_axis=0, concat_axis=0, tiled=True
-    ).reshape(expert_count, 2, capacity, width)
+    returned = exchange(partial_out, req_count, devices, 1).reshape(
+        expert_count, 2, capacity, width
+    )
     results = (returned[:, 0].astype(jnp.float32) + returned[:, 1].astype(jnp.float32)).astype(
         jnp.bfloat16
     ).reshape(expert_count * capacity, width)

time: 193 us -> 249 us (1.29)
  Pallas kernels: 9.2 us -> 174 us
  blocking collectives: 65.9 us -> 0 us
  waiting for transfers between devices: 44.6 us -> 0 us
  matrix products: 30.6 us -> 35.8 us
  starting transfers between devices: 4.77 us -> 0 us
    pallas_call x0 -> x2, Pallas kernels: none -> 165 us  [exchange(): pl.pallas_call(functools.partial(exchange_kernel, n_req, total, min(16, t...]
    all_to_all x1 -> x0, blocking collectives: 65.9 us -> none  [body(): lax.all_to_all(doubled, ('ctx', 'req'), split_axis=0, concat_axis=0, tile...]
    all_to_all x1 -> x0, waiting for transfers between devices: 44.6 us -> none  [body(): lax.all_to_all(partial_out, ('ctx', 'req'), split_axis=0, concat_axis=0,...]
    all_to_all x1 -> x0, starting transfers between devices: 4.77 us -> none  [body(): lax.all_to_all(partial_out, ('ctx', 'req'), split_axis=0, concat_axis=0,...]
    dot_general x1, matrix products: 4.82 us -> 7.92 us  [expert_half(): gate_out = jnp.dot(flat_rows, gate_part, preferred_element_type=jnp.float32)]
  transfers between devices with their start and end apart: 1 -> 0, of which waited for: 1 -> 0; matrix products, arithmetic and copies ran while one was open for 5% -> 0% of each run, Pallas kernels for 0% -> 0%
where the time goes in v8:
time: 249 us; the launch traced here: 247 us
  Pallas kernels  174 us (70%)
  matrix products  35.8 us (14%)
  other arithmetic  25.1 us (10%)
  local copies, waits for them, and re-layouts  11.5 us (5%)
    pallas_call x2, Pallas kernels, exchange(): pl.pallas_call(functools.partial(exchange_kernel, n_req, total, min(16, t...  165 us
    dot_general x1, matrix products, expert_half(): jnp.dot(hidden, down_part, preferred_element_type=jnp.float32)  11.2 us
    pallas_call x1, Pallas kernels, context_exchange(): pl.pallas_call(functools.partial(context_kernel, n_ctx), out_shape=(jax.S...  9.2 us
    select_n x2, other arithmetic, body(): jnp.where(row_ids == target[request], new_rows[request][None, :], flat_pool)  8.54 us
    dot_general x1, matrix products, expert_half(): gate_out = jnp.dot(flat_rows, gate_part, preferred_element_type=jnp.float32)  7.92 us
    eq x4, other arithmetic, body(): row_ids == target[request]  5.26 us

profile of v8, /device:TPU:8, one launch (start us, length us, event | category | flops | bytes accessed | tf_op | source)
XLA Modules:
  0.0 247.3 jit_solution(7043477859661644797)
XLA Ops:
  0.7 0.8 convert_bitcast_fusion.1
  1.5 0.9 select_reduce_fusion.7
  2.5 0.7 compare_select_fusion.2
  3.1 0.6 fusion.109
  3.8 1.3 iota_compare_fusion.5
  5.1 1.3 iota_compare_fusion.7
  6.5 0.7 slice_bitcast_fusion.5
  7.3 0.7 slice_bitcast_fusion.4
  8.1 0.5 copy-done.11
  8.7 5.8 %fusion.10 = bf16[2048,576]{1,0:T(8,128)(2,1)} fusion(bf16[32,64,576]{2,1,0:T(8,128)(2,1)} %param.31, pred[2048]{0:T(1024)(128)(4,1)S(1)} %get-tuple-element.46, pred[2048]{0:T(1024)(128)(4,1)S(1)} %get-tuple-element.47, pred[2048]{0:T(1024)(128)(4,1)S(1)} %get-tuple-element.48, pred[2048]{0:T(1024)(128)(4,1)S(1)} %get-tuple-element.49, ...), kind=kLoop, calls=%fused_computation.15 | loop fusion | flops 4718592 | bytes 4731392 | tf_op jit(solution)/shard_map/jit(_where)/select_n | solution.py:279
  15.3 2.9 %fusion.110 = (f32[32]{0:T(128)S(1)}, f32[2048,32]{0,1:T(8,128)S(1)}) fusion(bf16[2048,576]{1,0:T(8,128)(2,1)} %fusion.10, bf16[32,32]{1,0:T(8,128)(2,1)S(1)} %get-tuple-element.23, bf16[32,32]{1,0:T(8,128)(2,1)S(1)} %get-tuple-element.22, bf16[32,512]{1,0:T(8,128)(2,1)S(1)} %bitcast.140, pred[2048,4]{0,1:T(4,128)(4,1)S(1)} %fusion.74), kind=kOutput, calls=%fused_computation.215 | convolution fusion | flops 75804640 | bytes 2666624 | tf_op jit(solution)/shard_map/dot_general | solution.py:295
  18.2 1.1 fusion.17
  19.4 0.7 fusion.50
  20.1 0.7 broadcast_in_dim.283
  20.9 1.3 broadcast_in_dim.282
  22.2 1.6 maximum_maximum_fusion.parts_ref
  23.8 0.7 select_reduce_fusion.6
  24.6 1.6 multiply_cosine_fusion
  26.2 0.8 slice.120
  27.0 0.7 pad_maximum_fusion.keys_ref
  27.8 9.2 %shard_map.211 = (bf16[4,64,576]{2,1,0:T(8,128)(2,1)}, f32[4,8,640]{2,1,0:T(8,128)}) custom-call(bf16[64,576]{1,0:T(8,128)(2,1)} %pad_maximum_fusion.keys_ref, f32[4,8,640]{2,1,0:T(8,128)} %maximum_maximum_fusion.parts_ref), custom_call_target="tpu_custom_call" | custom-call | tf_op jit(solution)/shard_map/pallas_call | solution.py:208
  37.0 1.3 convolution_bitcast_fusion
  38.3 0.9 fusion.55
  39.3 0.7 select_reduce_fusion.5
  40.2 0.2 copy.43
  40.4 1.2 fusion.111
  41.7 0.4 fusion.23
  42.1 0.2 copy.44
  42.3 0.3 copy-done.6
  42.7 0.2 slice_reduce_fusion
  43.1 0.4 fusion.30
  43.5 0.7 copy.46
  44.3 3.2 %multiply_reduce_fusion = (f32[65]{0:T(128)S(1)}, f32[65,2048]{1,0:T(8,128)S(1)}) fusion(bf16[65,1024]{1,0:T(8,128)(2,1)} %bitcast.128, bf16[1024,2048]{1,0:T(8,128)(2,1)} %param.33, bf16[1,2048]{1,0:T(2,128)(2,1)S(1)} %dynamic-slice_bitcast_fusion, bf16[64,2048]{1,0:T(8,128)(2,1)} %bitcast.134), kind=kOutput, calls=%fused_computation.48 | convolution fusion | flops 273561536 | bytes 5126404 | tf_op jit(solution)/shard_map/dot_general | solution.py:362
  47.8 0.2 fusion.34
  48.0 0.8 fusion.7
  48.8 2.5 %broadcast_in_dim.271 = bf16[64,2,8,2048]{3,2,1,0:T(8,128)(2,1)} broadcast(bf16[64,8,2048]{2,1,0:T(8,128)(2,1)S(1)} %fusion.7), dimensions={0,2,3} | broadcast | bytes 6291456 | tf_op jit(solution)/shard_map/broadcast_in_dim | solution.py:393
  51.2 80.6 %shard_map.212 = bf16[128,8,2048]{2,1,0:T(8,128)(2,1)} custom-call(bf16[128,8,2048]{2,1,0:T(8,128)(2,1)} %bitcast.126), custom_call_target="tpu_custom_call" | custom-call | tf_op jit(solution)/shard_map/pallas_call | solution.py:145
  131.9 7.9 %fusion.2 = f32[1024,704]{0,1:T(8,128)} fusion(bf16[128,8,2048]{2,1,0:T(8,128)(2,1)} %shard_map.212, bf16[1,2048,704]{1,2,0:T(8,128)(2,1)} %param.37), kind=kOutput, calls=%fused_computation.2 | convolution fusion | flops 2952790016 | bytes 9961472 | tf_op jit(solution)/shard_map/dot_general | solution.py:61
  139.8 11.2 %convert_bitcast_fusion.x_ref = bf16[128,8,2048]{2,1,0:T(8,128)(2,1)} fusion(bf16[1,704,2048]{2,1,0:T(8,128)(2,1)S(1)} %copy-done, f32[1024,704]{0,1:T(8,128)} %fusion.2, bf16[1,2048,704]{1,2,0:T(8,128)(2,1)} %param.38, bf16[128,8,2048]{2,1,0:T(8,128)(2,1)} %shard_map.212), kind=kOutput, calls=%fused_computation.5 | convolution fusion | flops 5912002560 | bytes 17039360 | tf_op jit(solution)/shard_map/dot_general | solution.py:64
  151.0 83.9 %shard_map.213 = bf16[128,8,2048]{2,1,0:T(8,128)(2,1)} custom-call(bf16[128,8,2048]{2,1,0:T(8,128)(2,1)} %convert_bitcast_fusion.x_ref), custom_call_target="tpu_custom_call" | custom-call | tf_op jit(solution)/shard_map/pallas_call | solution.py:145
  234.9 1.5 fusion.33
  236.5 0.2 select_reduce_fusion
  236.7 3.8 %fusion.11 = bf16[65,2048]{1,0:T(8,128)(2,1)S(1)} fusion(f32[65,2048]{1,0:T(8,128)S(1)} %get-tuple-element.45, f32[65,512]{1,0:T(8,128)S(1)} %select_reduce_fusion, bf16[64,2,8,2048]{3,2,1,0:T(8,128)(2,1)} %bitcast.127), kind=kOutput, calls=%fused_computation.19 | convolution fusion | flops 822349824 | bytes 5126144 | tf_op jit(solution)/shard_map/dot_general | solution.py:410
  240.5 0.7 slice_bitcast_fusion.2
  241.2 0.6 slice_bitcast_fusion.3
  241.8 1.3 fusion.79
  243.2 1.3 fusion.81
  244.5 2.8 %select_select_fusion = bf16[32,64,576]{2,1,0:T(8,128)(2,1)} fusion(bf16[32,64,576]{2,1,0:T(8,128)(2,1)S(1)} %copy-done.2, pred[32,64]{1,0:T(8,128)(4,1)S(1)} %get-tuple-element.50, pred[32,64]{1,0:T(8,128)(4,1)S(1)} %get-tuple-element.51, pred[32,64]{1,0:T(8,128)(4,1)S(1)} %get-tuple-element.52, pred[32,64]{1,0:T(8,128)(4,1)S(1)} %get-tuple-element.53, ...), kind=kLoop, calls=%fused_computation.16 | loop fusion | flops 4718592 | bytes 4731392 | tf_op jit(solution)/shard_map/jit(_where)/select_n | solution.py:279
  (86 shorter events, 2.3 us)
Async XLA Ops:
  0.6 139.2 %copy-start = (bf16[1,704,2048]{2,1,0:T(8,128)(2,1)S(1)}, bf16[1,704,2048]{2,1,0:T(8,128)(2,1)}, u32[]{:S(2)}) copy-start(bf16[1,704,2048]{2,1,0:T(8,128)(2,1)} %param.39) | copy-start | bytes 8650756
  0.6 13.8 %copy-start.19 = (s32[4,1,8]{2,1,0:T(1,128)S(1)}, s32[4,1,8]{2,1,0:T(1,128)}, u32[]{:S(2)}) copy-start(s32[4,1,8]{2,1,0:T(1,128)} %param.30) | copy-start | bytes 388
  0.7 14.5 %copy-start.23 = (s32[4,1]{0,1:T(1,128)S(1)}, s32[4,1]{0,1:T(1,128)}, u32[]{:S(2)}) copy-start(s32[4,1]{0,1:T(1,128)} %param.29) | copy-start | bytes 52
  0.7 14.5 %copy-start.10 = (bf16[4,1,8,64]{3,2,1,0:T(8,128)(2,1)S(1)}, bf16[4,1,8,64]{3,2,1,0:T(8,128)(2,1)}, u32[]{:S(2)}) copy-start(bf16[4,1,8,64]{3,2,1,0:T(8,128)(2,1)} %param.27) | copy-start | bytes 12292
  0.7 14.6 %copy-start.8 = (bf16[4,1,8,512]{3,2,1,0:T(8,128)(2,1)S(1)}, bf16[4,1,8,512]{3,2,1,0:T(8,128)(2,1)}, u32[]{:S(2)}) copy-start(bf16[4,1,8,512]{3,2,1,0:T(8,128)(2,1)} %param.26) | copy-start | bytes 98308
  6.4 0.8 copy-start.22
  8.1 0.5 copy-start.11
  8.1 0.6 copy-start.13
  8.1 0.6 copy-start.15
  8.1 0.6 copy-start.17
  15.1 3.1 %copy-start.1 = (bf16[2048,576]{1,0:T(8,128)(2,1)S(1)}, bf16[2048,576]{1,0:T(8,128)(2,1)}, u32[]{:S(2)}) copy-start(bf16[2048,576]{1,0:T(8,128)(2,1)} %fusion.10) | copy-start | bytes 7077892
  18.2 1.2 copy-start.20
  18.2 18.8 %copy-start.3 = (bf16[1,64,8,512]{3,2,1,0:T(8,128)(2,1)S(1)}, bf16[1,64,8,512]{3,2,1,0:T(8,128)(2,1)}, u32[]{:S(2)}) copy-start(bf16[1,64,8,512]{3,2,1,0:T(8,128)(2,1)} %param.21) | copy-start | bytes 1572868
  18.2 20.1 %copy-start.4 = (bf16[1,64,8,64]{3,2,1,0:T(8,128)(2,1)S(1)}, bf16[1,64,8,64]{3,2,1,0:T(8,128)(2,1)}, u32[]{:S(2)}) copy-start(bf16[1,64,8,64]{3,2,1,0:T(8,128)(2,1)} %param.22) | copy-start | bytes 196612
  37.0 4.8 %copy-start.5 = (bf16[4,64,576]{2,1,0:T(8,128)(2,1)S(1)}, bf16[4,64,576]{2,1,0:T(8,128)(2,1)}, u32[]{:S(2)}) copy-start(bf16[4,64,576]{2,1,0:T(8,128)(2,1)} %get-tuple-element.5) | copy-start | bytes 884740
  41.7 0.9 copy-start.6
  41.7 1.4 copy-start.24
  42.1 2.1 copy-start.21
  43.5 4.0 %copy-start.7 = (s32[65,6]{0,1:T(8,128)S(1)}, s32[65,6]{0,1:T(8,128)}, u32[]{:S(2)}) copy-start(s32[65,6]{0,1:T(8,128)} %param.36) | copy-start | bytes 4684
  43.5 4.4 %copy-start.9 = (f32[2048]{0:T(1024)S(1)}, f32[2048]{0:T(1024)}, u32[]{:S(2)}) copy-start(f32[2048]{0:T(1024)} %param.34) | copy-start | bytes 24580
  236.4 8.1 %copy-start.2 = (bf16[32,64,576]{2,1,0:T(8,128)(2,1)S(1)}, bf16[32,64,576]{2,1,0:T(8,128)(2,1)}, u32[]{:S(2)}) copy-start(bf16[32,64,576]{2,1,0:T(8,128)(2,1)} %param.31) | copy-start | bytes 7077892
  236.4 8.1 %copy-start.12 = (bf16[576]{0:T(1024)(128)(2,1)S(1)}, bf16[576]{0:T(1024)(128)(2,1)}, u32[]{:S(2)}) copy-start(bf16[576]{0:T(1024)(128)(2,1)} %copy-done.11) | copy-start | bytes 3460
  236.4 8.1 %copy-start.14 = (bf16[576]{0:T(1024)(128)(2,1)S(1)}, bf16[576]{0:T(1024)(128)(2,1)}, u32[]{:S(2)}) copy-start(bf16[576]{0:T(1024)(128)(2,1)} %copy-done.13) | copy-start | bytes 3460
  236.4 8.1 %copy-start.16 = (bf16[576]{0:T(1024)(128)(2,1)S(1)}, bf16[576]{0:T(1024)(128)(2,1)}, u32[]{:S(2)}) copy-start(bf16[576]{0:T(1024)(128)(2,1)} %copy-done.15) | copy-start | bytes 3460
  236.4 8.1 %copy-start.18 = (bf16[576]{0:T(1024)(128)(2,1)S(1)}, bf16[576]{0:T(1024)(128)(2,1)}, u32[]{:S(2)}) copy-start(bf16[576]{0:T(1024)(128)(2,1)} %copy-done.17) | copy-start | bytes 3460

commit v9 on v6

--- a/solution.py
+++ b/solution.py
@@ -206,6 +206,42 @@
         scratch_shapes=[pltpu.SemaphoreType.DMA((5, n_ctx))],
         compiler_params=pltpu.CompilerParams(collective_id=2, has_side_effects=True),
     )(keys, parts)
+
+
+def ffn_kernel(x_ref, gate_ref, up_ref, down_ref, out_ref):
+    rows = x_ref[...]
+    gate_out = jnp.dot(rows, gate_ref[...], preferred_element_type=jnp.float32)
+    upward = jnp.dot(rows, up_ref[...], preferred_element_type=jnp.float32)
+    hidden = (jax.nn.silu(gate_out) * upward).astype(jnp.bfloat16)
+    out_ref[...] = jnp.dot(hidden, down_ref[...], preferred_element_type=jnp.float32).astype(
+        out_ref.dtype
+    )
+
+
+def ffn_half(inputs, gate_part, up_part, down_part, tile=128):
+    flat_rows = inputs.reshape(-1, inputs.shape[-1])
+    rows, width = flat_rows.shape
+    hidden = gate_part.shape[1]
+    fixed = lambda i: (0, 0)
+    out = pl.pallas_call(
+        ffn_kernel,
+        grid=(rows // tile,),
+        in_specs=[
+            pl.BlockSpec((tile, width), lambda i: (i, 0)),
+            pl.BlockSpec((width, hidden), fixed),
+            pl.BlockSpec((width, hidden), fixed),
+            pl.BlockSpec((hidden, width), fixed),
+        ],
+        out_specs=pl.BlockSpec((tile, width), lambda i: (i, 0)),
+        out_shape=jax.ShapeDtypeStruct((rows, width), jnp.bfloat16),
+        compiler_params=pltpu.CompilerParams(vmem_limit_bytes=48 * 1024 * 1024),
+        cost_estimate=pl.CostEstimate(
+            flops=6 * rows * width * hidden,
+            transcendentals=rows * hidden,
+            bytes_accessed=2 * (2 * rows * width + 3 * width * hidden),
+        ),
+    )(flat_rows, gate_part, up_part, down_part)
+    return out.reshape(inputs.shape)
 
 
 def body(
@@ -383,7 +419,7 @@
     doubled = jnp.broadcast_to(outgoing[:, None], (expert_count, 2, capacity, width)).reshape(
         devices, capacity, width
     )
-    partial_out = expert_half(
+    partial_out = ffn_half(
         lax.all_to_all(doubled, ("ctx", "req"), split_axis=0, concat_axis=0, tiled=True),
         w_gate[0],
         w_up[0],

time: 193 us -> 191 us (0.990)
  blocking collectives: 65.9 us -> 0 us
  waiting for transfers between devices: 44.6 us -> 92.5 us
  matrix products: 30.6 us -> 12.9 us
  Pallas kernels: 9.2 us -> 24 us
  local copies, waits for them, and re-layouts: 9.03 us -> 20.5 us
  starting transfers between devices: 4.77 us -> 15.4 us
  other arithmetic: 27.1 us -> 23.4 us
    all_to_all x1 -> x0, blocking collectives: 65.9 us -> none  [body(): lax.all_to_all(doubled, ('ctx', 'req'), split_axis=0, concat_axis=0, tile...]
    all_to_all x0 -> x1, waiting for transfers between devices: none -> 46.4 us  [body(): lax.all_to_all(doubled, ('ctx', 'req'), split_axis=0, concat_axis=0, tile...]
    dot_general x2 -> x0, matrix products: 15.9 us -> none  [the longest x1 11.1 us: expert_half(): jnp.dot(hidden, down_part, preferred_element_type=jnp.float32)]
    pallas_call x0 -> x1, Pallas kernels: none -> 14.8 us  [ffn_half(): pl.pallas_call(ffn_kernel, grid=(rows // tile,), in_specs=[pl.BlockSpec((...]
    all_to_all x0 -> x1, starting transfers between devices: none -> 10.5 us  [body(): lax.all_to_all(doubled, ('ctx', 'req'), split_axis=0, concat_axis=0, tile...]
    unnamed x48 -> x34, local copies, waits for them, and re-layouts: 3.11 us -> 13.4 us
  transfers between devices with their start and end apart: 1 -> 2, of which waited for: 1 -> 2; matrix products, arithmetic and copies ran while one was open for 5% -> 9% of each run, Pallas kernels for 0% -> 0%
where the time goes in v9:
time: 191 us; the launch traced here: 190 us
  waiting for transfers between devices  92.5 us (48%)
  Pallas kernels  24 us (13%)
  other arithmetic  23.4 us (12%)
  local copies, waits for them, and re-layouts  20.5 us (11%)
  starting transfers between devices  15.4 us (8%)
  matrix products  12.9 us (7%)
    all_to_all x1, waiting for transfers between devices, body(): lax.all_to_all(doubled, ('ctx', 'req'), split_axis=0, concat_axis=0, tile...  46.4 us
    all_to_all x1, waiting for transfers between devices, body(): lax.all_to_all(partial_out, ('ctx', 'req'), split_axis=0, concat_axis=0,...  46.1 us
    pallas_call x1, Pallas kernels, ffn_half(): pl.pallas_call(ffn_kernel, grid=(rows // tile,), in_specs=[pl.BlockSpec((...  14.8 us
    unnamed x34, local copies, waits for them, and re-layouts  13.4 us
    all_to_all x1, starting transfers between devices, body(): lax.all_to_all(doubled, ('ctx', 'req'), split_axis=0, concat_axis=0, tile...  10.5 us
    pallas_call x1, Pallas kernels, context_exchange(): pl.pallas_call(functools.partial(context_kernel, n_ctx), out_shape=(jax.S...  9.2 us
    select_n x2, other arithmetic, body(): jnp.where(row_ids == target[request], new_rows[request][None, :], flat_pool)  9.14 us
    eq x4, other arithmetic, body(): row_ids == target[request]  5.21 us
  transfers between devices with their start and end apart: 2, of which 2 were waited for; matrix products, arithmetic and copies ran while one was open for 9% of the time, Pallas kernels for 0%

profile of v9, /device:TPU:8, one launch (start us, length us, event | category | flops | bytes accessed | tf_op | source)
XLA Modules:
  0.0 189.9 jit_solution(3068909248755975668)
XLA Ops:
  0.7 0.8 slice_bitcast_fusion.5
  1.4 0.7 slice_bitcast_fusion.4
  2.1 0.8 select_reduce_fusion.4
  2.9 0.8 fusion.69
  3.7 0.7 convert_bitcast_fusion
  4.4 0.9 select_reduce_fusion.7
  5.3 0.7 compare_select_fusion.2
  5.9 0.7 fusion.93
  7.3 1.3 iota_compare_fusion.5
  8.7 1.3 iota_compare_fusion.7
  9.9 0.9 fusion.71
  10.8 0.7 fusion.59
  11.5 4.5 %fusion.3 = bf16[2048,576]{1,0:T(8,128)(2,1)S(1)} fusion(bf16[32,64,576]{2,1,0:T(8,128)(2,1)} %param.31, pred[2048]{0:T(1024)(128)(4,1)S(1)} %get-tuple-element.46, pred[2048]{0:T(1024)(128)(4,1)S(1)} %get-tuple-element.47, pred[2048]{0:T(1024)(128)(4,1)S(1)} %get-tuple-element.48, pred[2048]{0:T(1024)(128)(4,1)S(1)} %get-tuple-element.49, ...), kind=kLoop, calls=%fused_computation.6 | loop fusion | flops 4718592 | bytes 4731392 | tf_op jit(solution)/shard_map/jit(_where)/select_n | solution.py:305
  16.1 1.0 fusion.94
  17.2 0.5 fusion.10
  17.6 0.2 fusion.35
  18.2 0.2 multiply_cosine_fusion
  18.7 0.2 copy.47
  19.0 0.7 pad_maximum_fusion.keys_ref
  19.7 0.7 maximum_maximum_fusion.parts_ref
  20.4 9.2 %shard_map.211 = (bf16[4,64,576]{2,1,0:T(8,128)(2,1)}, f32[4,8,640]{2,1,0:T(8,128)}) custom-call(bf16[64,576]{1,0:T(8,128)(2,1)} %pad_maximum_fusion.keys_ref, f32[4,8,640]{2,1,0:T(8,128)} %maximum_maximum_fusion.parts_ref), custom_call_target="tpu_custom_call" | custom-call | tf_op jit(solution)/shard_map/pallas_call | solution.py:198
  29.7 1.3 convolution_bitcast_fusion
  31.2 1.2 fusion.95
  32.5 0.4 fusion.12
  33.1 0.3 copy-done.8
  33.5 0.2 slice_reduce_fusion
  33.9 0.3 fusion.15
  34.4 3.2 %multiply_reduce_fusion = (f32[65]{0:T(128)S(1)}, f32[65,2048]{1,0:T(8,128)S(1)}) fusion(bf16[65,1024]{1,0:T(8,128)(2,1)S(1)} %bitcast.112, bf16[1024,2048]{1,0:T(8,128)(2,1)} %param.33, bf16[1,2048]{1,0:T(2,128)(2,1)S(1)} %dynamic-slice_bitcast_fusion, bf16[64,2048]{1,0:T(8,128)(2,1)S(1)} %bitcast.118), kind=kOutput, calls=%fused_computation.39 | convolution fusion | flops 273561536 | bytes 5126404 | tf_op jit(solution)/shard_map/dot_general | solution.py:388
  37.8 0.2 fusion.19
  38.0 0.8 fusion
  38.8 2.5 %broadcast_in_dim.271 = bf16[64,2,8,2048]{3,2,1,0:T(8,128)(2,1)} broadcast(bf16[64,8,2048]{2,1,0:T(8,128)(2,1)S(1)} %fusion), dimensions={0,2,3} | broadcast | bytes 6291456 | tf_op jit(solution)/shard_map/broadcast_in_dim | solution.py:419
  41.3 10.5 %all-to-all-start = ((bf16[128,8,2048]{2,1,0:T(8,128)(2,1)}), bf16[128,8,2048]{2,1,0:T(8,128)(2,1)}, u32[]{:S(2)}, u32[]{:S(2)}) async-start(bf16[128,8,2048]{2,1,0:T(8,128)(2,1)} %bitcast.109), calls=%async_computation | async-start | bytes 8388608 | tf_op jit(solution)/shard_map/all_to_all | solution.py:423
  51.8 4.6 %copy.50 = bf16[1,2048,704]{2,1,0:T(8,128)(2,1)} copy(bf16[1,2048,704]{1,2,0:T(8,128)(2,1)} %param.37) | data formatting | bytes 5767168 | tf_op args[17]
  56.4 4.6 %copy.51 = bf16[1,2048,704]{2,1,0:T(8,128)(2,1)} copy(bf16[1,2048,704]{1,2,0:T(8,128)(2,1)} %param.38) | data formatting | bytes 5767168 | tf_op args[18]
  61.1 46.4 %all-to-all-done = bf16[128,8,2048]{2,1,0:T(8,128)(2,1)} async-done(((bf16[128,8,2048]{2,1,0:T(8,128)(2,1)}), bf16[128,8,2048]{2,1,0:T(8,128)(2,1)}, u32[]{:S(2)}, u32[]{:S(2)}) %all-to-all-start) | async-done | bytes 4194336 | tf_op jit(solution)/shard_map/all_to_all | solution.py:423
  107.5 1.9 copy-done.1
  109.3 1.8 copy-done.2
  111.2 14.8 %shard_map.212 = bf16[1024,2048]{1,0:T(8,128)(2,1)} custom-call(bf16[1024,2048]{1,0:T(8,128)(2,1)} %bitcast.35.x_ref, bf16[2048,704]{1,0:T(8,128)(2,1)S(1)} %bitcast.107, bf16[2048,704]{1,0:T(8,128)(2,1)} %bitcast.111, bf16[704,2048]{1,0:T(8,128)(2,1)S(1)} %bitcast.108), custom_call_target="tpu_custom_call" | custom-call | flops 8858370048 | bytes 17039360 | tf_op jit(solution)/shard_map/pallas_call | solution.py:226
  125.9 4.9 %all-to-all-start.1 = ((bf16[128,8,2048]{2,1,0:T(8,128)(2,1)}), bf16[128,8,2048]{2,1,0:T(8,128)(2,1)}, u32[]{:S(2)}, u32[]{:S(2)}) async-start(bf16[128,8,2048]{2,1,0:T(8,128)(2,1)} %bitcast.110), calls=%async_computation.1 | async-start | bytes 8388608 | tf_op jit(solution)/shard_map/all_to_all | solution.py:428
  130.8 1.3 fusion.64
  132.2 1.3 fusion.66
  133.5 0.5 fusion.18
  134.0 0.2 select_reduce_fusion
  134.2 4.6 %select_select_fusion = bf16[32,64,576]{2,1,0:T(8,128)(2,1)} fusion(bf16[32,64,576]{2,1,0:T(8,128)(2,1)} %param.31, pred[32,64]{1,0:T(8,128)(4,1)S(1)} %get-tuple-element.50, pred[32,64]{1,0:T(8,128)(4,1)S(1)} %get-tuple-element.51, pred[32,64]{1,0:T(8,128)(4,1)S(1)} %get-tuple-element.52, pred[32,64]{1,0:T(8,128)(4,1)S(1)} %get-tuple-element.53, ...), kind=kLoop, calls=%fused_computation.7 | loop fusion | flops 4718592 | bytes 4731392 | tf_op jit(solution)/shard_map/jit(_where)/select_n | solution.py:305
  138.8 46.1 %all-to-all-done.1 = bf16[128,8,2048]{2,1,0:T(8,128)(2,1)} async-done(((bf16[128,8,2048]{2,1,0:T(8,128)(2,1)}), bf16[128,8,2048]{2,1,0:T(8,128)(2,1)}, u32[]{:S(2)}, u32[]{:S(2)}) %all-to-all-start.1) | async-done | bytes 4194336 | tf_op jit(solution)/shard_map/all_to_all | solution.py:428
  184.9 3.6 %fusion.4 = bf16[65,2048]{1,0:T(8,128)(2,1)S(1)} fusion(f32[65,2048]{1,0:T(8,128)S(1)} %get-tuple-element.45, f32[65,512]{1,0:T(8,128)S(1)} %select_reduce_fusion, bf16[64,2,8,2048]{3,2,1,0:T(8,128)(2,1)} %bitcast.40), kind=kOutput, calls=%fused_computation.10 | convolution fusion | flops 822349824 | bytes 5126144 | tf_op jit(solution)/shard_map/dot_general | solution.py:435
  188.6 0.7 slice_bitcast_fusion.2
  189.3 0.6 slice_bitcast_fusion.3
  (69 shorter events, 2.5 us)
Async XLA Ops:
  0.6 33.3 %copy-start = (bf16[8,512,128]{2,1,0:T(8,128)(2,1)S(1)}, bf16[8,512,128]{2,1,0:T(8,128)(2,1)}, u32[]{:S(2)}) copy-start(bf16[8,512,128]{2,1,0:T(8,128)(2,1)} %param.32) | copy-start | bytes 3145732
  11.5 4.6 %copy-start.11 = (bf16[4,1,8,512]{3,2,1,0:T(8,128)(2,1)S(1)}, bf16[4,1,8,512]{3,2,1,0:T(8,128)(2,1)}, u32[]{:S(2)}) copy-start(bf16[4,1,8,512]{3,2,1,0:T(8,128)(2,1)} %param.26) | copy-start | bytes 98308
  17.1 1.0 copy-start.14
  17.1 1.1 copy-start.9
  17.1 12.5 %copy-start.3 = (bf16[1,64,8,512]{3,2,1,0:T(8,128)(2,1)S(1)}, bf16[1,64,8,512]{3,2,1,0:T(8,128)(2,1)}, u32[]{:S(2)}) copy-start(bf16[1,64,8,512]{3,2,1,0:T(8,128)(2,1)} %param.21) | copy-start | bytes 1572868
  17.1 13.9 %copy-start.5 = (bf16[1,64,8,64]{3,2,1,0:T(8,128)(2,1)S(1)}, bf16[1,64,8,64]{3,2,1,0:T(8,128)(2,1)}, u32[]{:S(2)}) copy-start(bf16[1,64,8,64]{3,2,1,0:T(8,128)(2,1)} %param.22) | copy-start | bytes 196612
  29.6 2.9 %copy-start.6 = (bf16[4,64,576]{2,1,0:T(8,128)(2,1)S(1)}, bf16[4,64,576]{2,1,0:T(8,128)(2,1)}, u32[]{:S(2)}) copy-start(bf16[4,64,576]{2,1,0:T(8,128)(2,1)} %get-tuple-element.5) | copy-start | bytes 884740
  32.5 0.9 copy-start.8
  32.9 1.5 copy-start.13
  32.9 1.5 copy-start.7
  34.3 3.3 %copy-start.10 = (s32[65,6]{0,1:T(8,128)S(1)}, s32[65,6]{0,1:T(8,128)}, u32[]{:S(2)}) copy-start(s32[65,6]{0,1:T(8,128)} %param.36) | copy-start | bytes 4684
  34.4 3.6 %copy-start.12 = (f32[2048]{0:T(1024)S(1)}, f32[2048]{0:T(1024)}, u32[]{:S(2)}) copy-start(f32[2048]{0:T(1024)} %param.34) | copy-start | bytes 24580
  41.3 66.2 %all-to-all-start = ((bf16[128,8,2048]{2,1,0:T(8,128)(2,1)}), bf16[128,8,2048]{2,1,0:T(8,128)(2,1)}, u32[]{:S(2)}, u32[]{:S(2)}) async-start(bf16[128,8,2048]{2,1,0:T(8,128)(2,1)} %bitcast.109), calls=%async_computation | async-start | bytes 8388608 | tf_op jit(solution)/shard_map/all_to_all | solution.py:423
  107.5 1.9 copy-start.1
  109.3 1.8 copy-start.2
  125.9 7.5 %copy-start.4 = (f32[2048,64]{0,1:T(8,128)S(1)}, f32[2048,64]{0,1:T(8,128)}, u32[]{:S(2)}) copy-start(f32[2048,64]{0,1:T(8,128)} %param.35) | copy-start | bytes 1572868
  125.9 59.0 %all-to-all-start.1 = ((bf16[128,8,2048]{2,1,0:T(8,128)(2,1)}), bf16[128,8,2048]{2,1,0:T(8,128)(2,1)}, u32[]{:S(2)}, u32[]{:S(2)}) async-start(bf16[128,8,2048]{2,1,0:T(8,128)(2,1)} %bitcast.110), calls=%async_computation.1 | async-start | bytes 8388608 | tf_op jit(solution)/shard_map/all_to_all | solution.py:428

commit v10 on v9

--- a/solution.py
+++ b/solution.py
@@ -210,8 +210,9 @@
 
 def ffn_kernel(x_ref, gate_ref, up_ref, down_ref, out_ref):
     rows = x_ref[...]
-    gate_out = jnp.dot(rows, gate_ref[...], preferred_element_type=jnp.float32)
-    upward = jnp.dot(rows, up_ref[...], preferred_element_type=jnp.float32)
+    by_width = (((1,), (1,)), ((), ()))
+    gate_out = lax.dot_general(rows, gate_ref[...], by_width, preferred_element_type=jnp.float32)
+    upward = lax.dot_general(rows, up_ref[...], by_width, preferred_element_type=jnp.float32)
     hidden = (jax.nn.silu(gate_out) * upward).astype(jnp.bfloat16)
     out_ref[...] = jnp.dot(hidden, down_ref[...], preferred_element_type=jnp.float32).astype(
         out_ref.dtype
@@ -228,8 +229,8 @@
         grid=(rows // tile,),
         in_specs=[
             pl.BlockSpec((tile, width), lambda i: (i, 0)),
-            pl.BlockSpec((width, hidden), fixed),
-            pl.BlockSpec((width, hidden), fixed),
+            pl.BlockSpec((hidden, width), fixed),
+            pl.BlockSpec((hidden, width), fixed),
             pl.BlockSpec((hidden, width), fixed),
         ],
         out_specs=pl.BlockSpec((tile, width), lambda i: (i, 0)),
@@ -240,7 +241,7 @@
             transcendentals=rows * hidden,
             bytes_accessed=2 * (2 * rows * width + 3 * width * hidden),
         ),
-    )(flat_rows, gate_part, up_part, down_part)
+    )(flat_rows, jnp.swapaxes(gate_part, 0, 1), jnp.swapaxes(up_part, 0, 1), down_part)
     return out.reshape(inputs.shape)
 
 

time: 191 us -> 192 us (level)
  blocking collectives: 0 us -> 66 us
  waiting for transfers between devices: 92.5 us -> 46.3 us
  local copies, waits for them, and re-layouts: 20.5 us -> 5.61 us
  starting transfers between devices: 15.4 us -> 4.89 us
  Pallas kernels: 24 us -> 31 us
    all_to_all x0 -> x1, blocking collectives: none -> 66 us  [body(): lax.all_to_all(doubled, ('ctx', 'req'), split_axis=0, concat_axis=0, tile...]
    all_to_all x1 -> x0, waiting for transfers between devices: 46.4 us -> none  [body(): lax.all_to_all(doubled, ('ctx', 'req'), split_axis=0, concat_axis=0, tile...]
    unnamed x34 -> x32, local copies, waits for them, and re-layouts: 13.4 us -> 0.45 us
    all_to_all x1 -> x0, starting transfers between devices: 10.5 us -> none  [body(): lax.all_to_all(doubled, ('ctx', 'req'), split_axis=0, concat_axis=0, tile...]
    pallas_call x1, Pallas kernels: 14.8 us -> 21.8 us  [ffn_half(): pl.pallas_call(ffn_kernel, grid=(rows // tile,), in_specs=[pl.BlockSpec((...]
  transfers between devices with their start and end apart: 2 -> 1, of which waited for: 2 -> 1; matrix products, arithmetic and copies ran while one was open for 9% -> 4% of each run, Pallas kernels for 0% -> 0%
where the time goes in v10:
time: 192 us; the launch traced here: 191 us
  blocking collectives  66 us (34%)
  waiting for transfers between devices  46.3 us (24%)
  Pallas kernels  31 us (16%)
  other arithmetic  23.1 us (12%)
  matrix products  12.9 us (7%)
  local copies, waits for them, and re-layouts  5.61 us (3%)
  starting transfers between devices  4.89 us (3%)
    all_to_all x1, blocking collectives, body(): lax.all_to_all(doubled, ('ctx', 'req'), split_axis=0, concat_axis=0, tile...  66 us
    all_to_all x1, waiting for transfers between devices, body(): lax.all_to_all(partial_out, ('ctx', 'req'), split_axis=0, concat_axis=0,...  46.3 us
    pallas_call x1, Pallas kernels, ffn_half(): pl.pallas_call(ffn_kernel, grid=(rows // tile,), in_specs=[pl.BlockSpec((...  21.8 us
    pallas_call x1, Pallas kernels, context_exchange(): pl.pallas_call(functools.partial(context_kernel, n_ctx), out_shape=(jax.S...  9.2 us
    select_n x2, other arithmetic, body(): jnp.where(row_ids == target[request], new_rows[request][None, :], flat_pool)  9.14 us
    all_to_all x1, starting transfers between devices, body(): lax.all_to_all(partial_out, ('ctx', 'req'), split_axis=0, concat_axis=0,...  4.89 us
    eq x4, other arithmetic, body(): row_ids == target[request]  4.86 us
  transfers between devices with their start and end apart: 1, of which 1 were waited for; matrix products, arithmetic and copies ran while one was open for 4% of the time, Pallas kernels for 0%

profile of v10, /device:TPU:8, one launch (start us, length us, event | category | flops | bytes accessed | tf_op | source)
XLA Modules:
  0.0 190.9 jit_solution(9630690658518890739)
XLA Ops:
  0.7 0.8 slice_bitcast_fusion.5
  1.4 0.7 slice_bitcast_fusion.4
  2.1 0.8 select_reduce_fusion.4
  2.9 0.8 fusion.69
  3.7 0.7 convert_bitcast_fusion
  4.4 0.9 select_reduce_fusion.7
  5.3 0.7 compare_select_fusion.2
  5.9 0.6 fusion.93
  7.3 1.2 iota_compare_fusion.5
  8.5 1.2 iota_compare_fusion.7
  9.7 0.9 fusion.71
  10.5 0.7 fusion.59
  11.3 4.5 %fusion.3 = bf16[2048,576]{1,0:T(8,128)(2,1)S(1)} fusion(bf16[32,64,576]{2,1,0:T(8,128)(2,1)} %param.31, pred[2048]{0:T(1024)(128)(4,1)S(1)} %get-tuple-element.46, pred[2048]{0:T(1024)(128)(4,1)S(1)} %get-tuple-element.47, pred[2048]{0:T(1024)(128)(4,1)S(1)} %get-tuple-element.48, pred[2048]{0:T(1024)(128)(4,1)S(1)} %get-tuple-element.49, ...), kind=kLoop, calls=%fused_computation.6 | loop fusion | flops 4718592 | bytes 4731392 | tf_op jit(solution)/shard_map/jit(_where)/select_n | solution.py:306
  15.9 1.0 fusion.94
  16.9 0.5 fusion.10
  17.4 0.2 fusion.35
  18.0 0.2 multiply_cosine_fusion
  18.5 0.2 copy.43
  18.8 0.7 pad_maximum_fusion.keys_ref
  19.5 0.7 maximum_maximum_fusion.parts_ref
  20.2 9.2 %shard_map.211 = (bf16[4,64,576]{2,1,0:T(8,128)(2,1)}, f32[4,8,640]{2,1,0:T(8,128)}) custom-call(bf16[64,576]{1,0:T(8,128)(2,1)} %pad_maximum_fusion.keys_ref, f32[4,8,640]{2,1,0:T(8,128)} %maximum_maximum_fusion.parts_ref), custom_call_target="tpu_custom_call" | custom-call | tf_op jit(solution)/shard_map/pallas_call | solution.py:198
  29.4 1.3 convolution_bitcast_fusion
  30.8 0.2 fusion.40
  30.9 1.2 fusion.95
  32.1 0.1 fusion.24
  32.3 0.4 fusion.12
  32.7 0.2 copy.44
  32.8 0.3 copy-done.8
  33.1 0.1 slice_reduce_fusion.2
  33.3 0.2 slice_reduce_fusion
  33.6 0.3 fusion.15
  34.1 3.2 %multiply_reduce_fusion = (f32[65]{0:T(128)S(1)}, f32[65,2048]{1,0:T(8,128)S(1)}) fusion(bf16[65,1024]{1,0:T(8,128)(2,1)S(1)} %bitcast.116, bf16[1024,2048]{1,0:T(8,128)(2,1)} %param.33, bf16[1,2048]{1,0:T(2,128)(2,1)S(1)} %dynamic-slice_bitcast_fusion, bf16[64,2048]{1,0:T(8,128)(2,1)S(1)} %bitcast.122), kind=kOutput, calls=%fused_computation.39 | convolution fusion | flops 273561536 | bytes 5126404 | tf_op jit(solution)/shard_map/dot_general | solution.py:389
  37.4 0.1 convolution_convert_fusion.2
  37.6 0.2 fusion.19
  37.8 0.8 fusion
  38.6 0.5 broadcast_in_dim.271
  39.1 66.0 %all_to_all.10 = bf16[128,8,2048]{2,1,0:T(8,128)(2,1)} all-to-all(bf16[128,8,2048]{2,1,0:T(8,128)(2,1)S(1)} %bitcast.113), channel_id=1, replica_groups=mesh['ctx'=4,'req'=32] {'ctx','req'}, dimensions={0} | all-to-all | bytes 8388608 | tf_op jit(solution)/shard_map/all_to_all | solution.py:424
  105.1 21.8 %shard_map.212 = bf16[1024,2048]{1,0:T(8,128)(2,1)} custom-call(bf16[1024,2048]{1,0:T(8,128)(2,1)} %bitcast.115, bf16[704,2048]{1,0:T(8,128)(2,1)S(1)} %bitcast.111, bf16[704,2048]{1,0:T(8,128)(2,1)S(1)} %bitcast.112, bf16[704,2048]{1,0:T(8,128)(2,1)} %bitcast.134), custom_call_target="tpu_custom_call" | custom-call | flops 8858370048 | bytes 17039360 | tf_op jit(solution)/shard_map/pallas_call | solution.py:227
  126.9 4.9 %all-to-all-start.1 = ((bf16[128,8,2048]{2,1,0:T(8,128)(2,1)}), bf16[128,8,2048]{2,1,0:T(8,128)(2,1)}, u32[]{:S(2)}, u32[]{:S(2)}) async-start(bf16[128,8,2048]{2,1,0:T(8,128)(2,1)} %bitcast.114), calls=%async_computation.1 | async-start | bytes 8388608 | tf_op jit(solution)/shard_map/all_to_all | solution.py:429
  131.8 1.2 fusion.64
  133.0 1.2 fusion.66
  134.3 0.5 fusion.18
  134.8 0.2 select_reduce_fusion
  135.0 4.6 %select_select_fusion = bf16[32,64,576]{2,1,0:T(8,128)(2,1)} fusion(bf16[32,64,576]{2,1,0:T(8,128)(2,1)} %param.31, pred[32,64]{1,0:T(8,128)(4,1)S(1)} %get-tuple-element.50, pred[32,64]{1,0:T(8,128)(4,1)S(1)} %get-tuple-element.51, pred[32,64]{1,0:T(8,128)(4,1)S(1)} %get-tuple-element.52, pred[32,64]{1,0:T(8,128)(4,1)S(1)} %get-tuple-element.53, ...), kind=kLoop, calls=%fused_computation.7 | loop fusion | flops 4718592 | bytes 4731392 | tf_op jit(solution)/shard_map/jit(_where)/select_n | solution.py:306
  139.6 46.3 %all-to-all-done.1 = bf16[128,8,2048]{2,1,0:T(8,128)(2,1)} async-done(((bf16[128,8,2048]{2,1,0:T(8,128)(2,1)}), bf16[128,8,2048]{2,1,0:T(8,128)(2,1)}, u32[]{:S(2)}, u32[]{:S(2)}) %all-to-all-start.1) | async-done | bytes 4194336 | tf_op jit(solution)/shard_map/all_to_all | solution.py:429
  185.9 3.6 %fusion.4 = bf16[65,2048]{1,0:T(8,128)(2,1)S(1)} fusion(f32[65,2048]{1,0:T(8,128)S(1)} %get-tuple-element.45, f32[65,512]{1,0:T(8,128)S(1)} %select_reduce_fusion, bf16[64,2,8,2048]{3,2,1,0:T(8,128)(2,1)} %bitcast.42), kind=kOutput, calls=%fused_computation.10 | convolution fusion | flops 822349824 | bytes 5126144 | tf_op jit(solution)/shard_map/dot_general | solution.py:436
  189.6 0.7 slice_bitcast_fusion.2
  190.3 0.6 slice_bitcast_fusion.3
  (66 shorter events, 1.8 us)
Async XLA Ops:
  0.6 33.0 %copy-start = (bf16[8,512,128]{2,1,0:T(8,128)(2,1)S(1)}, bf16[8,512,128]{2,1,0:T(8,128)(2,1)}, u32[]{:S(2)}) copy-start(bf16[8,512,128]{2,1,0:T(8,128)(2,1)} %param.32) | copy-start | bytes 3145732
  11.3 4.6 %copy-start.11 = (bf16[4,1,8,512]{3,2,1,0:T(8,128)(2,1)S(1)}, bf16[4,1,8,512]{3,2,1,0:T(8,128)(2,1)}, u32[]{:S(2)}) copy-start(bf16[4,1,8,512]{3,2,1,0:T(8,128)(2,1)} %param.26) | copy-start | bytes 98308
  16.9 1.0 copy-start.14
  16.9 1.1 copy-start.9
  16.9 12.5 %copy-start.3 = (bf16[1,64,8,512]{3,2,1,0:T(8,128)(2,1)S(1)}, bf16[1,64,8,512]{3,2,1,0:T(8,128)(2,1)}, u32[]{:S(2)}) copy-start(bf16[1,64,8,512]{3,2,1,0:T(8,128)(2,1)} %param.21) | copy-start | bytes 1572868
  16.9 13.9 %copy-start.5 = (bf16[1,64,8,64]{3,2,1,0:T(8,128)(2,1)S(1)}, bf16[1,64,8,64]{3,2,1,0:T(8,128)(2,1)}, u32[]{:S(2)}) copy-start(bf16[1,64,8,64]{3,2,1,0:T(8,128)(2,1)} %param.22) | copy-start | bytes 196612
  29.4 2.9 %copy-start.6 = (bf16[4,64,576]{2,1,0:T(8,128)(2,1)S(1)}, bf16[4,64,576]{2,1,0:T(8,128)(2,1)}, u32[]{:S(2)}) copy-start(bf16[4,64,576]{2,1,0:T(8,128)(2,1)} %get-tuple-element.5) | copy-start | bytes 884740
  32.3 0.9 copy-start.8
  32.6 1.5 copy-start.13
  32.6 1.5 copy-start.7
  34.1 3.3 %copy-start.10 = (s32[65,6]{0,1:T(8,128)S(1)}, s32[65,6]{0,1:T(8,128)}, u32[]{:S(2)}) copy-start(s32[65,6]{0,1:T(8,128)} %param.36) | copy-start | bytes 4684
  34.1 3.6 %copy-start.12 = (f32[2048]{0:T(1024)S(1)}, f32[2048]{0:T(1024)}, u32[]{:S(2)}) copy-start(f32[2048]{0:T(1024)} %param.34) | copy-start | bytes 24580
  39.1 66.0 %copy-start.1 = (bf16[1,2048,704]{1,2,0:T(8,128)(2,1)S(1)}, bf16[1,2048,704]{1,2,0:T(8,128)(2,1)}, u32[]{:S(2)}) copy-start(bf16[1,2048,704]{1,2,0:T(8,128)(2,1)} %param.37) | copy-start | bytes 8650756
  39.1 66.0 %copy-start.2 = (bf16[1,2048,704]{1,2,0:T(8,128)(2,1)S(1)}, bf16[1,2048,704]{1,2,0:T(8,128)(2,1)}, u32[]{:S(2)}) copy-start(bf16[1,2048,704]{1,2,0:T(8,128)(2,1)} %param.38) | copy-start | bytes 8650756
  126.9 7.3 %copy-start.4 = (f32[2048,64]{0,1:T(8,128)S(1)}, f32[2048,64]{0,1:T(8,128)}, u32[]{:S(2)}) copy-start(f32[2048,64]{0,1:T(8,128)} %param.35) | copy-start | bytes 1572868
  126.9 59.0 %all-to-all-start.1 = ((bf16[128,8,2048]{2,1,0:T(8,128)(2,1)}), bf16[128,8,2048]{2,1,0:T(8,128)(2,1)}, u32[]{:S(2)}, u32[]{:S(2)}) async-start(bf16[128,8,2048]{2,1,0:T(8,128)(2,1)} %bitcast.114), calls=%async_computation.1 | async-start | bytes 8388608 | tf_op jit(solution)/shard_map/all_to_all | solution.py:429

commit v11 on v9

--- a/solution.py
+++ b/solution.py
@@ -218,7 +218,7 @@
     )
 
 
-def ffn_half(inputs, gate_part, up_part, down_part, tile=128):
+def ffn_half(inputs, gate_part, up_part, down_part, tile=256):
     flat_rows = inputs.reshape(-1, inputs.shape[-1])
     rows, width = flat_rows.shape
     hidden = gate_part.shape[1]
@@ -432,7 +432,11 @@
         jnp.bfloat16
     ).reshape(expert_count * capacity, width)
     combine = jnp.sum(jnp.where(slot_hit, mixing[:, :, None], 0.0), axis=1)
-    moe = jnp.dot(combine, results.astype(jnp.float32), precision=lax.Precision.HIGHEST)
+    combine_high = combine.astype(jnp.bfloat16)
+    combine_low = (combine - combine_high.astype(jnp.float32)).astype(jnp.bfloat16)
+    moe = jnp.dot(combine_high, results, preferred_element_type=jnp.float32) + jnp.dot(
+        combine_low, results, preferred_element_type=jnp.float32
+    )
     final = (hidden_state + moe).astype(jnp.bfloat16)
     pre_out = final[:shard_rows][None]
     dec_out = final[shard_rows:][:, None]

time: 191 us -> 196 us (1.026)
  matrix products: 12.9 us -> 16.7 us
  other arithmetic: 23.4 us -> 25.8 us
    dot_general x1 -> x2, matrix products: 3.62 us -> 5.87 us  [the longest x1 2.96 us: body(): jnp.dot(combine_low, results, preferred_element_type=jnp.float32)]
where the time goes in v11:
time: 196 us; the launch traced here: 195 us
  waiting for transfers between devices  92.5 us (47%)
  other arithmetic  25.8 us (13%)
  Pallas kernels  22.9 us (12%)
  local copies, waits for them, and re-layouts  20.6 us (11%)
  matrix products  16.7 us (9%)
  starting transfers between devices  15.4 us (8%)
    all_to_all x1, waiting for transfers between devices, body(): lax.all_to_all(doubled, ('ctx', 'req'), split_axis=0, concat_axis=0, tile...  46.4 us
    all_to_all x1, waiting for transfers between devices, body(): lax.all_to_all(partial_out, ('ctx', 'req'), split_axis=0, concat_axis=0,...  46.1 us
    pallas_call x1, Pallas kernels, ffn_half(): pl.pallas_call(ffn_kernel, grid=(rows // tile,), in_specs=[pl.BlockSpec((...  13.7 us
    unnamed x34, local copies, waits for them, and re-layouts  13.5 us
    all_to_all x1, starting transfers between devices, body(): lax.all_to_all(doubled, ('ctx', 'req'), split_axis=0, concat_axis=0, tile...  10.5 us
    pallas_call x1, Pallas kernels, context_exchange(): pl.pallas_call(functools.partial(context_kernel, n_ctx), out_shape=(jax.S...  9.2 us
    select_n x2, other arithmetic, body(): jnp.where(row_ids == target[request], new_rows[request][None, :], flat_pool)  9.15 us
    eq x4, other arithmetic, body(): row_ids == target[request]  5.21 us
  transfers between devices with their start and end apart: 2, of which 2 were waited for; matrix products, arithmetic and copies ran while one was open for 9% of the time, Pallas kernels for 0%

profile of v11, /device:TPU:8, one launch (start us, length us, event | category | flops | bytes accessed | tf_op | source)
XLA Modules:
  0.0 195.1 jit_solution(13463031247822763592)
XLA Ops:
  0.7 0.8 slice_bitcast_fusion.5
  1.4 0.7 slice_bitcast_fusion.4
  2.1 0.8 fusion.72
  2.9 0.8 select_reduce_fusion.4
  3.7 0.7 convert_bitcast_fusion
  4.4 0.9 select_reduce_fusion.7
  5.3 0.7 compare_select_fusion.2
  5.9 0.7 fusion.96
  7.3 1.3 iota_compare_fusion.5
  8.7 1.3 iota_compare_fusion.7
  9.9 0.9 fusion.74
  10.8 0.7 fusion.62
  11.5 4.5 %fusion.3 = bf16[2048,576]{1,0:T(8,128)(2,1)S(1)} fusion(bf16[32,64,576]{2,1,0:T(8,128)(2,1)} %param.31, pred[2048]{0:T(1024)(128)(4,1)S(1)} %get-tuple-element.46, pred[2048]{0:T(1024)(128)(4,1)S(1)} %get-tuple-element.47, pred[2048]{0:T(1024)(128)(4,1)S(1)} %get-tuple-element.48, pred[2048]{0:T(1024)(128)(4,1)S(1)} %get-tuple-element.49, ...), kind=kLoop, calls=%fused_computation.6 | loop fusion | flops 4718592 | bytes 4731392 | tf_op jit(solution)/shard_map/jit(_where)/select_n | solution.py:305
  16.1 1.0 fusion.97
  17.1 0.5 copy-done.3
  17.7 0.2 fusion.36
  17.9 2.1 %fusion.8 = f32[4,8,512]{2,1,0:T(8,128)S(1)} fusion(bf16[2048,576]{1,0:T(8,128)(2,1)} %copy-done.3, f32[2048,32]{0,1:T(8,128)S(1)} %get-tuple-element.41, f32[32]{0:T(128)S(1)} %get-tuple-element.40, pred[2048,4]{0,1:T(4,128)(4,1)S(1)} %fusion.62), kind=kOutput, calls=%fused_computation.16 | convolution fusion | flops 67305472 | bytes 2433152 | tf_op jit(solution)/shard_map/dot_general | solution.py:328
  20.6 0.7 pad_maximum_fusion.keys_ref
  21.3 0.7 maximum_maximum_fusion.parts_ref
  22.0 9.2 %shard_map.211 = (bf16[4,64,576]{2,1,0:T(8,128)(2,1)}, f32[4,8,640]{2,1,0:T(8,128)}) custom-call(bf16[64,576]{1,0:T(8,128)(2,1)} %pad_maximum_fusion.keys_ref, f32[4,8,640]{2,1,0:T(8,128)} %maximum_maximum_fusion.parts_ref), custom_call_target="tpu_custom_call" | custom-call | tf_op jit(solution)/shard_map/pallas_call | solution.py:198
  31.3 0.9 slice_reduce_fusion.2
  32.1 1.0 slice_reduce_fusion
  33.1 0.9 fusion.48
  34.3 0.2 copy.47
  34.5 1.3 convolution_bitcast_fusion
  36.0 1.2 fusion.98
  37.3 0.3 fusion.10
  38.0 0.3 fusion.13
  38.9 3.2 %multiply_reduce_fusion = (f32[65]{0:T(128)S(1)}, f32[65,2048]{1,0:T(8,128)S(1)}) fusion(bf16[65,1024]{1,0:T(8,128)(2,1)S(1)} %bitcast.112, bf16[1024,2048]{1,0:T(8,128)(2,1)} %param.33, bf16[1,2048]{1,0:T(2,128)(2,1)S(1)} %dynamic-slice_bitcast_fusion, bf16[64,2048]{1,0:T(8,128)(2,1)S(1)} %bitcast.118), kind=kOutput, calls=%fused_computation.38 | convolution fusion | flops 273561536 | bytes 5126404 | tf_op jit(solution)/shard_map/dot_general | solution.py:388
  42.1 0.8 fusion
  42.9 2.5 %broadcast_in_dim.271 = bf16[64,2,8,2048]{3,2,1,0:T(8,128)(2,1)} broadcast(bf16[64,8,2048]{2,1,0:T(8,128)(2,1)S(1)} %fusion), dimensions={0,2,3} | broadcast | bytes 6291456 | tf_op jit(solution)/shard_map/broadcast_in_dim | solution.py:419
  45.4 10.5 %all-to-all-start = ((bf16[128,8,2048]{2,1,0:T(8,128)(2,1)}), bf16[128,8,2048]{2,1,0:T(8,128)(2,1)}, u32[]{:S(2)}, u32[]{:S(2)}) async-start(bf16[128,8,2048]{2,1,0:T(8,128)(2,1)} %bitcast.109), calls=%async_computation | async-start | bytes 8388608 | tf_op jit(solution)/shard_map/all_to_all | solution.py:423
  55.9 4.6 %copy.50 = bf16[1,2048,704]{2,1,0:T(8,128)(2,1)} copy(bf16[1,2048,704]{1,2,0:T(8,128)(2,1)} %param.37) | data formatting | bytes 5767168 | tf_op args[17]
  60.5 4.6 %copy.51 = bf16[1,2048,704]{2,1,0:T(8,128)(2,1)} copy(bf16[1,2048,704]{1,2,0:T(8,128)(2,1)} %param.38) | data formatting | bytes 5767168 | tf_op args[18]
  65.1 46.4 %all-to-all-done = bf16[128,8,2048]{2,1,0:T(8,128)(2,1)} async-done(((bf16[128,8,2048]{2,1,0:T(8,128)(2,1)}), bf16[128,8,2048]{2,1,0:T(8,128)(2,1)}, u32[]{:S(2)}, u32[]{:S(2)}) %all-to-all-start) | async-done | bytes 4194336 | tf_op jit(solution)/shard_map/all_to_all | solution.py:423
  111.5 1.9 copy-done.1
  113.4 1.8 copy-done.2
  115.2 13.7 %shard_map.212 = bf16[1024,2048]{1,0:T(8,128)(2,1)} custom-call(bf16[1024,2048]{1,0:T(8,128)(2,1)} %bitcast.35.x_ref, bf16[2048,704]{1,0:T(8,128)(2,1)S(1)} %bitcast.107, bf16[2048,704]{1,0:T(8,128)(2,1)} %bitcast.111, bf16[704,2048]{1,0:T(8,128)(2,1)S(1)} %bitcast.108), custom_call_target="tpu_custom_call" | custom-call | flops 8858370048 | bytes 17039360 | tf_op jit(solution)/shard_map/pallas_call | solution.py:226
  128.9 4.9 %all-to-all-start.1 = ((bf16[128,8,2048]{2,1,0:T(8,128)(2,1)}), bf16[128,8,2048]{2,1,0:T(8,128)(2,1)}, u32[]{:S(2)}, u32[]{:S(2)}) async-start(bf16[128,8,2048]{2,1,0:T(8,128)(2,1)} %bitcast.110), calls=%async_computation.1 | async-start | bytes 8388608 | tf_op jit(solution)/shard_map/all_to_all | solution.py:428
  133.8 1.3 fusion.67
  135.2 1.3 fusion.69
  136.5 0.5 fusion.16
  137.2 4.6 %select_select_fusion = bf16[32,64,576]{2,1,0:T(8,128)(2,1)} fusion(bf16[32,64,576]{2,1,0:T(8,128)(2,1)} %param.31, pred[32,64]{1,0:T(8,128)(4,1)S(1)} %get-tuple-element.50, pred[32,64]{1,0:T(8,128)(4,1)S(1)} %get-tuple-element.51, pred[32,64]{1,0:T(8,128)(4,1)S(1)} %get-tuple-element.52, pred[32,64]{1,0:T(8,128)(4,1)S(1)} %get-tuple-element.53, ...), kind=kLoop, calls=%fused_computation.7 | loop fusion | flops 4718592 | bytes 4731392 | tf_op jit(solution)/shard_map/jit(_where)/select_n | solution.py:305
  141.8 46.1 %all-to-all-done.1 = bf16[128,8,2048]{2,1,0:T(8,128)(2,1)} async-done(((bf16[128,8,2048]{2,1,0:T(8,128)(2,1)}), bf16[128,8,2048]{2,1,0:T(8,128)(2,1)}, u32[]{:S(2)}, u32[]{:S(2)}) %all-to-all-start.1) | async-done | bytes 4194336 | tf_op jit(solution)/shard_map/all_to_all | solution.py:428
  187.9 2.9 %fusion.25 = f32[65,2048]{1,0:T(8,128)S(1)} fusion(bf16[64,2,8,2048]{3,2,1,0:T(8,128)(2,1)} %bitcast.40, f32[65,512]{1,0:T(8,128)S(1)} %select_reduce_fusion), kind=kOutput, calls=%fused_computation.48 | convolution fusion | flops 140542464 | bytes 4859904 | tf_op jit(solution)/shard_map/dot_general | solution.py:437
  190.8 3.0 %fusion.5 = bf16[65,2048]{1,0:T(8,128)(2,1)S(1)} fusion(f32[65,2048]{1,0:T(8,128)S(1)} %get-tuple-element.45, f32[65,2048]{1,0:T(8,128)S(1)} %fusion.25, bf16[64,2,8,2048]{3,2,1,0:T(8,128)(2,1)} %bitcast.40, f32[65,512]{1,0:T(8,128)S(1)} %select_reduce_fusion), kind=kOutput, calls=%fused_computation.11 | convolution fusion | flops 141041664 | bytes 5658624 | tf_op jit(solution)/shard_map/dot_general | solution.py:437
  193.8 0.7 slice_bitcast_fusion.2
  194.5 0.6 slice_bitcast_fusion.3
  (70 shorter events, 2.9 us)
Async XLA Ops:
  0.6 37.3 %copy-start = (bf16[8,512,128]{2,1,0:T(8,128)(2,1)S(1)}, bf16[8,512,128]{2,1,0:T(8,128)(2,1)}, u32[]{:S(2)}) copy-start(bf16[8,512,128]{2,1,0:T(8,128)(2,1)} %param.32) | copy-start | bytes 3145732
  11.5 4.6 %copy-start.11 = (bf16[4,1,8,512]{3,2,1,0:T(8,128)(2,1)S(1)}, bf16[4,1,8,512]{3,2,1,0:T(8,128)(2,1)}, u32[]{:S(2)}) copy-start(bf16[4,1,8,512]{3,2,1,0:T(8,128)(2,1)} %param.26) | copy-start | bytes 98308
  16.1 1.5 copy-start.3
  17.6 2.5 %copy-start.14 = (s32[8]{0:T(128)S(1)}, s32[8]{0:T(128)}, u32[]{:S(2)}) copy-start(s32[8]{0:T(128)} %param.24) | copy-start | bytes 100
  17.6 2.6 %copy-start.9 = (bf16[1,64,576]{2,1,0:T(8,128)(2,1)S(1)}, bf16[1,64,576]{2,1,0:T(8,128)(2,1)}, u32[]{:S(2)}) copy-start(bf16[1,64,576]{2,1,0:T(8,128)(2,1)} %param.20) | copy-start | bytes 221188
  17.6 16.9 %copy-start.4 = (bf16[1,64,8,512]{3,2,1,0:T(8,128)(2,1)S(1)}, bf16[1,64,8,512]{3,2,1,0:T(8,128)(2,1)}, u32[]{:S(2)}) copy-start(bf16[1,64,8,512]{3,2,1,0:T(8,128)(2,1)} %param.21) | copy-start | bytes 1572868
  17.9 17.9 %copy-start.6 = (bf16[1,64,8,64]{3,2,1,0:T(8,128)(2,1)S(1)}, bf16[1,64,8,64]{3,2,1,0:T(8,128)(2,1)}, u32[]{:S(2)}) copy-start(bf16[1,64,8,64]{3,2,1,0:T(8,128)(2,1)} %param.22) | copy-start | bytes 196612
  31.3 6.0 %copy-start.7 = (bf16[4,64,576]{2,1,0:T(8,128)(2,1)S(1)}, bf16[4,64,576]{2,1,0:T(8,128)(2,1)}, u32[]{:S(2)}) copy-start(bf16[4,64,576]{2,1,0:T(8,128)(2,1)} %get-tuple-element.5) | copy-start | bytes 884740
  37.6 0.8 copy-start.10
  37.7 1.2 copy-start.13
  37.7 1.2 copy-start.8
  38.8 3.3 %copy-start.12 = (f32[2048]{0:T(1024)S(1)}, f32[2048]{0:T(1024)}, u32[]{:S(2)}) copy-start(f32[2048]{0:T(1024)} %param.34) | copy-start | bytes 24580
  45.4 66.2 %all-to-all-start = ((bf16[128,8,2048]{2,1,0:T(8,128)(2,1)}), bf16[128,8,2048]{2,1,0:T(8,128)(2,1)}, u32[]{:S(2)}, u32[]{:S(2)}) async-start(bf16[128,8,2048]{2,1,0:T(8,128)(2,1)} %bitcast.109), calls=%async_computation | async-start | bytes 8388608 | tf_op jit(solution)/shard_map/all_to_all | solution.py:423
  111.5 1.9 copy-start.1
  113.4 1.8 copy-start.2
  128.9 7.5 %copy-start.5 = (f32[2048,64]{0,1:T(8,128)S(1)}, f32[2048,64]{0,1:T(8,128)}, u32[]{:S(2)}) copy-start(f32[2048,64]{0,1:T(8,128)} %param.35) | copy-start | bytes 1572868
  128.9 59.0 %all-to-all-start.1 = ((bf16[128,8,2048]{2,1,0:T(8,128)(2,1)}), bf16[128,8,2048]{2,1,0:T(8,128)(2,1)}, u32[]{:S(2)}, u32[]{:S(2)}) async-start(bf16[128,8,2048]{2,1,0:T(8,128)(2,1)} %bitcast.110), calls=%async_computation.1 | async-start | bytes 8388608 | tf_op jit(solution)/shard_map/all_to_all | solution.py:428

commit v12 on v9

--- a/solution.py
+++ b/solution.py
@@ -218,7 +218,7 @@
     )
 
 
-def ffn_half(inputs, gate_part, up_part, down_part, tile=128):
+def ffn_half(inputs, gate_part, up_part, down_part, tile=256):
     flat_rows = inputs.reshape(-1, inputs.shape[-1])
     rows, width = flat_rows.shape
     hidden = gate_part.shape[1]

time: 191 us -> 190 us (level)
  no operation moved by 1% of the time
where the time goes in v12:
time: 190 us; the launch traced here: 189 us
  waiting for transfers between devices  92.5 us (49%)
  other arithmetic  23.4 us (12%)
  Pallas kernels  22.9 us (12%)
  local copies, waits for them, and re-layouts  20.5 us (11%)
  starting transfers between devices  15.4 us (8%)
  matrix products  12.9 us (7%)
    all_to_all x1, waiting for transfers between devices, body(): lax.all_to_all(doubled, ('ctx', 'req'), split_axis=0, concat_axis=0, tile...  46.4 us
    all_to_all x1, waiting for transfers between devices, body(): lax.all_to_all(partial_out, ('ctx', 'req'), split_axis=0, concat_axis=0,...  46.1 us
    pallas_call x1, Pallas kernels, ffn_half(): pl.pallas_call(ffn_kernel, grid=(rows // tile,), in_specs=[pl.BlockSpec((...  13.7 us
    unnamed x34, local copies, waits for them, and re-layouts  13.4 us
    all_to_all x1, starting transfers between devices, body(): lax.all_to_all(doubled, ('ctx', 'req'), split_axis=0, concat_axis=0, tile...  10.5 us
    pallas_call x1, Pallas kernels, context_exchange(): pl.pallas_call(functools.partial(context_kernel, n_ctx), out_shape=(jax.S...  9.2 us
    select_n x2, other arithmetic, body(): jnp.where(row_ids == target[request], new_rows[request][None, :], flat_pool)  9.14 us
    eq x4, other arithmetic, body(): row_ids == target[request]  5.21 us
  transfers between devices with their start and end apart: 2, of which 2 were waited for; matrix products, arithmetic and copies ran while one was open for 9% of the time, Pallas kernels for 0%

profile of v12, /device:TPU:8, one launch (start us, length us, event | category | flops | bytes accessed | tf_op | source)
XLA Modules:
  0.0 188.8 jit_solution(9072195291921377902)
XLA Ops:
  0.7 0.8 slice_bitcast_fusion.5
  1.4 0.7 slice_bitcast_fusion.4
  2.1 0.8 select_reduce_fusion.4
  2.9 0.8 fusion.69
  3.7 0.7 convert_bitcast_fusion
  4.4 0.9 select_reduce_fusion.7
  5.3 0.7 compare_select_fusion.2
  5.9 0.7 fusion.93
  7.3 1.3 iota_compare_fusion.5
  8.7 1.3 iota_compare_fusion.7
  9.9 0.9 fusion.71
  10.8 0.7 fusion.59
  11.5 4.5 %fusion.3 = bf16[2048,576]{1,0:T(8,128)(2,1)S(1)} fusion(bf16[32,64,576]{2,1,0:T(8,128)(2,1)} %param.31, pred[2048]{0:T(1024)(128)(4,1)S(1)} %get-tuple-element.46, pred[2048]{0:T(1024)(128)(4,1)S(1)} %get-tuple-element.47, pred[2048]{0:T(1024)(128)(4,1)S(1)} %get-tuple-element.48, pred[2048]{0:T(1024)(128)(4,1)S(1)} %get-tuple-element.49, ...), kind=kLoop, calls=%fused_computation.6 | loop fusion | flops 4718592 | bytes 4731392 | tf_op jit(solution)/shard_map/jit(_where)/select_n | solution.py:305
  16.1 1.0 fusion.94
  17.2 0.5 fusion.10
  17.6 0.2 fusion.35
  18.2 0.2 multiply_cosine_fusion
  18.7 0.2 copy.47
  19.0 0.7 pad_maximum_fusion.keys_ref
  19.7 0.7 maximum_maximum_fusion.parts_ref
  20.4 9.2 %shard_map.211 = (bf16[4,64,576]{2,1,0:T(8,128)(2,1)}, f32[4,8,640]{2,1,0:T(8,128)}) custom-call(bf16[64,576]{1,0:T(8,128)(2,1)} %pad_maximum_fusion.keys_ref, f32[4,8,640]{2,1,0:T(8,128)} %maximum_maximum_fusion.parts_ref), custom_call_target="tpu_custom_call" | custom-call | tf_op jit(solution)/shard_map/pallas_call | solution.py:198
  29.7 1.3 convolution_bitcast_fusion
  31.2 1.2 fusion.95
  32.5 0.4 fusion.12
  33.1 0.3 copy-done.8
  33.5 0.2 slice_reduce_fusion
  33.9 0.3 fusion.15
  34.4 3.2 %multiply_reduce_fusion = (f32[65]{0:T(128)S(1)}, f32[65,2048]{1,0:T(8,128)S(1)}) fusion(bf16[65,1024]{1,0:T(8,128)(2,1)S(1)} %bitcast.112, bf16[1024,2048]{1,0:T(8,128)(2,1)} %param.33, bf16[1,2048]{1,0:T(2,128)(2,1)S(1)} %dynamic-slice_bitcast_fusion, bf16[64,2048]{1,0:T(8,128)(2,1)S(1)} %bitcast.118), kind=kOutput, calls=%fused_computation.39 | convolution fusion | flops 273561536 | bytes 5126404 | tf_op jit(solution)/shard_map/dot_general | solution.py:388
  37.8 0.2 fusion.19
  38.0 0.8 fusion
  38.8 2.5 %broadcast_in_dim.271 = bf16[64,2,8,2048]{3,2,1,0:T(8,128)(2,1)} broadcast(bf16[64,8,2048]{2,1,0:T(8,128)(2,1)S(1)} %fusion), dimensions={0,2,3} | broadcast | bytes 6291456 | tf_op jit(solution)/shard_map/broadcast_in_dim | solution.py:419
  41.3 10.5 %all-to-all-start = ((bf16[128,8,2048]{2,1,0:T(8,128)(2,1)}), bf16[128,8,2048]{2,1,0:T(8,128)(2,1)}, u32[]{:S(2)}, u32[]{:S(2)}) async-start(bf16[128,8,2048]{2,1,0:T(8,128)(2,1)} %bitcast.109), calls=%async_computation | async-start | bytes 8388608 | tf_op jit(solution)/shard_map/all_to_all | solution.py:423
  51.8 4.6 %copy.50 = bf16[1,2048,704]{2,1,0:T(8,128)(2,1)} copy(bf16[1,2048,704]{1,2,0:T(8,128)(2,1)} %param.37) | data formatting | bytes 5767168 | tf_op args[17]
  56.4 4.6 %copy.51 = bf16[1,2048,704]{2,1,0:T(8,128)(2,1)} copy(bf16[1,2048,704]{1,2,0:T(8,128)(2,1)} %param.38) | data formatting | bytes 5767168 | tf_op args[18]
  61.1 46.4 %all-to-all-done = bf16[128,8,2048]{2,1,0:T(8,128)(2,1)} async-done(((bf16[128,8,2048]{2,1,0:T(8,128)(2,1)}), bf16[128,8,2048]{2,1,0:T(8,128)(2,1)}, u32[]{:S(2)}, u32[]{:S(2)}) %all-to-all-start) | async-done | bytes 4194336 | tf_op jit(solution)/shard_map/all_to_all | solution.py:423
  107.5 1.9 copy-done.1
  109.3 1.8 copy-done.2
  111.2 13.7 %shard_map.212 = bf16[1024,2048]{1,0:T(8,128)(2,1)} custom-call(bf16[1024,2048]{1,0:T(8,128)(2,1)} %bitcast.35.x_ref, bf16[2048,704]{1,0:T(8,128)(2,1)S(1)} %bitcast.107, bf16[2048,704]{1,0:T(8,128)(2,1)} %bitcast.111, bf16[704,2048]{1,0:T(8,128)(2,1)S(1)} %bitcast.108), custom_call_target="tpu_custom_call" | custom-call | flops 8858370048 | bytes 17039360 | tf_op jit(solution)/shard_map/pallas_call | solution.py:226
  124.9 4.9 %all-to-all-start.1 = ((bf16[128,8,2048]{2,1,0:T(8,128)(2,1)}), bf16[128,8,2048]{2,1,0:T(8,128)(2,1)}, u32[]{:S(2)}, u32[]{:S(2)}) async-start(bf16[128,8,2048]{2,1,0:T(8,128)(2,1)} %bitcast.110), calls=%async_computation.1 | async-start | bytes 8388608 | tf_op jit(solution)/shard_map/all_to_all | solution.py:428
  129.8 1.3 fusion.64
  131.1 1.3 fusion.66
  132.4 0.5 fusion.18
  132.9 0.2 select_reduce_fusion
  133.1 4.6 %select_select_fusion = bf16[32,64,576]{2,1,0:T(8,128)(2,1)} fusion(bf16[32,64,576]{2,1,0:T(8,128)(2,1)} %param.31, pred[32,64]{1,0:T(8,128)(4,1)S(1)} %get-tuple-element.50, pred[32,64]{1,0:T(8,128)(4,1)S(1)} %get-tuple-element.51, pred[32,64]{1,0:T(8,128)(4,1)S(1)} %get-tuple-element.52, pred[32,64]{1,0:T(8,128)(4,1)S(1)} %get-tuple-element.53, ...), kind=kLoop, calls=%fused_computation.7 | loop fusion | flops 4718592 | bytes 4731392 | tf_op jit(solution)/shard_map/jit(_where)/select_n | solution.py:305
  137.7 46.1 %all-to-all-done.1 = bf16[128,8,2048]{2,1,0:T(8,128)(2,1)} async-done(((bf16[128,8,2048]{2,1,0:T(8,128)(2,1)}), bf16[128,8,2048]{2,1,0:T(8,128)(2,1)}, u32[]{:S(2)}, u32[]{:S(2)}) %all-to-all-start.1) | async-done | bytes 4194336 | tf_op jit(solution)/shard_map/all_to_all | solution.py:428
  183.9 3.6 %fusion.4 = bf16[65,2048]{1,0:T(8,128)(2,1)S(1)} fusion(f32[65,2048]{1,0:T(8,128)S(1)} %get-tuple-element.45, f32[65,512]{1,0:T(8,128)S(1)} %select_reduce_fusion, bf16[64,2,8,2048]{3,2,1,0:T(8,128)(2,1)} %bitcast.40), kind=kOutput, calls=%fused_computation.10 | convolution fusion | flops 822349824 | bytes 5126144 | tf_op jit(solution)/shard_map/dot_general | solution.py:435
  187.5 0.7 slice_bitcast_fusion.2
  188.2 0.6 slice_bitcast_fusion.3
  (69 shorter events, 2.5 us)
Async XLA Ops:
  0.6 33.3 %copy-start = (bf16[8,512,128]{2,1,0:T(8,128)(2,1)S(1)}, bf16[8,512,128]{2,1,0:T(8,128)(2,1)}, u32[]{:S(2)}) copy-start(bf16[8,512,128]{2,1,0:T(8,128)(2,1)} %param.32) | copy-start | bytes 3145732
  11.5 4.6 %copy-start.11 = (bf16[4,1,8,512]{3,2,1,0:T(8,128)(2,1)S(1)}, bf16[4,1,8,512]{3,2,1,0:T(8,128)(2,1)}, u32[]{:S(2)}) copy-start(bf16[4,1,8,512]{3,2,1,0:T(8,128)(2,1)} %param.26) | copy-start | bytes 98308
  17.1 1.0 copy-start.14
  17.1 1.1 copy-start.9
  17.1 12.5 %copy-start.3 = (bf16[1,64,8,512]{3,2,1,0:T(8,128)(2,1)S(1)}, bf16[1,64,8,512]{3,2,1,0:T(8,128)(2,1)}, u32[]{:S(2)}) copy-start(bf16[1,64,8,512]{3,2,1,0:T(8,128)(2,1)} %param.21) | copy-start | bytes 1572868
  17.1 13.9 %copy-start.5 = (bf16[1,64,8,64]{3,2,1,0:T(8,128)(2,1)S(1)}, bf16[1,64,8,64]{3,2,1,0:T(8,128)(2,1)}, u32[]{:S(2)}) copy-start(bf16[1,64,8,64]{3,2,1,0:T(8,128)(2,1)} %param.22) | copy-start | bytes 196612
  29.6 2.9 %copy-start.6 = (bf16[4,64,576]{2,1,0:T(8,128)(2,1)S(1)}, bf16[4,64,576]{2,1,0:T(8,128)(2,1)}, u32[]{:S(2)}) copy-start(bf16[4,64,576]{2,1,0:T(8,128)(2,1)} %get-tuple-element.5) | copy-start | bytes 884740
  32.5 0.9 copy-start.8
  32.9 1.5 copy-start.13
  32.9 1.5 copy-start.7
  34.3 3.3 %copy-start.10 = (s32[65,6]{0,1:T(8,128)S(1)}, s32[65,6]{0,1:T(8,128)}, u32[]{:S(2)}) copy-start(s32[65,6]{0,1:T(8,128)} %param.36) | copy-start | bytes 4684
  34.4 3.6 %copy-start.12 = (f32[2048]{0:T(1024)S(1)}, f32[2048]{0:T(1024)}, u32[]{:S(2)}) copy-start(f32[2048]{0:T(1024)} %param.34) | copy-start | bytes 24580
  41.3 66.2 %all-to-all-start = ((bf16[128,8,2048]{2,1,0:T(8,128)(2,1)}), bf16[128,8,2048]{2,1,0:T(8,128)(2,1)}, u32[]{:S(2)}, u32[]{:S(2)}) async-start(bf16[128,8,2048]{2,1,0:T(8,128)(2,1)} %bitcast.109), calls=%async_computation | async-start | bytes 8388608 | tf_op jit(solution)/shard_map/all_to_all | solution.py:423
  107.5 1.9 %copy-start.1 = (bf16[1,2048,704]{2,1,0:T(8,128)(2,1)S(1)}, bf16[1,2048,704]{2,1,0:T(8,128)(2,1)}, u32[]{:S(2)}) copy-start(bf16[1,2048,704]{2,1,0:T(8,128)(2,1)} %copy.50) | copy-start | bytes 8650756
  109.3 1.8 copy-start.2
  124.9 7.5 %copy-start.4 = (f32[2048,64]{0,1:T(8,128)S(1)}, f32[2048,64]{0,1:T(8,128)}, u32[]{:S(2)}) copy-start(f32[2048,64]{0,1:T(8,128)} %param.35) | copy-start | bytes 1572868
  124.9 59.0 %all-to-all-start.1 = ((bf16[128,8,2048]{2,1,0:T(8,128)(2,1)}), bf16[128,8,2048]{2,1,0:T(8,128)(2,1)}, u32[]{:S(2)}, u32[]{:S(2)}) async-start(bf16[128,8,2048]{2,1,0:T(8,128)(2,1)} %bitcast.110), calls=%async_computation.1 | async-start | bytes 8388608 | tf_op jit(solution)/shard_map/all_to_all | solution.py:428

commit v13 on v12

--- a/solution.py
+++ b/solution.py
@@ -412,13 +412,11 @@
     slot_index = jnp.sum(jnp.where(route_hit, before[:, None, :], 0), axis=-1)
     target_slot = routes * capacity + slot_index
     slot_hit = target_slot[:, :, None] == jnp.arange(expert_count * capacity)[None, None, :]
-    dispatch = jnp.any(slot_hit, axis=1).astype(jnp.bfloat16)
-    outgoing = lax.dot_general(
+    dispatch = jnp.any(slot_hit, axis=1).astype(jnp.bfloat16).reshape(row_count, expert_count, 1, capacity)
+    dispatch = jnp.broadcast_to(dispatch, (row_count, expert_count, 2, capacity)).reshape(row_count, -1)
+    doubled = lax.dot_general(
         dispatch, normed, (((0,), (0,)), ((), ())), preferred_element_type=jnp.float32
-    ).astype(jnp.bfloat16).reshape(expert_count, capacity, width)
-    doubled = jnp.broadcast_to(outgoing[:, None], (expert_count, 2, capacity, width)).reshape(
-        devices, capacity, width
-    )
+    ).astype(jnp.bfloat16).reshape(devices, capacity, width)
     partial_out = ffn_half(
         lax.all_to_all(doubled, ("ctx", "req"), split_axis=0, concat_axis=0, tiled=True),
         w_gate[0],

time: 190 us -> 190 us (level)
  matrix products: 12.9 us -> 15.4 us
  local copies, waits for them, and re-layouts: 20.5 us -> 18.2 us
    dot_general x1, matrix products: 0.78 us -> 3.25 us  [body(): lax.dot_general(dispatch, normed, (((0,), (0,)), ((), ())), preferred_ele...]
    broadcast_in_dim x1, local copies, waits for them, and re-layouts: 2.45 us -> 0.04 us  [body(): jnp.broadcast_to(dispatch, (row_count, expert_count, 2, capacity))]
where the time goes in v13:
time: 190 us; the launch traced here: 189 us
  waiting for transfers between devices  92.5 us (49%)
  other arithmetic  23.4 us (12%)
  Pallas kernels  22.9 us (12%)
  local copies, waits for them, and re-layouts  18.2 us (10%)
  matrix products  15.4 us (8%)
  starting transfers between devices  15.4 us (8%)
    all_to_all x1, waiting for transfers between devices, body(): lax.all_to_all(doubled, ('ctx', 'req'), split_axis=0, concat_axis=0, tile...  46.4 us
    all_to_all x1, waiting for transfers between devices, body(): lax.all_to_all(partial_out, ('ctx', 'req'), split_axis=0, concat_axis=0,...  46.1 us
    pallas_call x1, Pallas kernels, ffn_half(): pl.pallas_call(ffn_kernel, grid=(rows // tile,), in_specs=[pl.BlockSpec((...  13.7 us
    unnamed x34, local copies, waits for them, and re-layouts  13.4 us
    all_to_all x1, starting transfers between devices, body(): lax.all_to_all(doubled, ('ctx', 'req'), split_axis=0, concat_axis=0, tile...  10.5 us
    pallas_call x1, Pallas kernels, context_exchange(): pl.pallas_call(functools.partial(context_kernel, n_ctx), out_shape=(jax.S...  9.2 us
    select_n x2, other arithmetic, body(): jnp.where(row_ids == target[request], new_rows[request][None, :], flat_pool)  9.14 us
    eq x4, other arithmetic, body(): row_ids == target[request]  5.21 us
  transfers between devices with their start and end apart: 2, of which 2 were waited for; matrix products, arithmetic and copies ran while one was open for 9% of the time, Pallas kernels for 0%

profile of v13, /device:TPU:8, one launch (start us, length us, event | category | flops | bytes accessed | tf_op | source)
XLA Modules:
  0.0 189.0 jit_solution(15753702566704364325)
XLA Ops:
  0.7 0.8 slice_bitcast_fusion.5
  1.4 0.7 slice_bitcast_fusion.4
  2.1 0.8 select_reduce_fusion.4
  2.9 0.8 fusion.68
  3.7 0.7 convert_bitcast_fusion.1
  4.4 0.9 select_reduce_fusion.7
  5.3 0.7 compare_select_fusion.2
  5.9 0.7 fusion.92
  7.3 1.3 iota_compare_fusion.5
  8.7 1.3 iota_compare_fusion.7
  9.9 0.9 fusion.70
  10.8 0.7 fusion.58
  11.5 4.5 %fusion.2 = bf16[2048,576]{1,0:T(8,128)(2,1)S(1)} fusion(bf16[32,64,576]{2,1,0:T(8,128)(2,1)} %param.31, pred[2048]{0:T(1024)(128)(4,1)S(1)} %get-tuple-element.46, pred[2048]{0:T(1024)(128)(4,1)S(1)} %get-tuple-element.47, pred[2048]{0:T(1024)(128)(4,1)S(1)} %get-tuple-element.48, pred[2048]{0:T(1024)(128)(4,1)S(1)} %get-tuple-element.49, ...), kind=kLoop, calls=%fused_computation.5 | loop fusion | flops 4718592 | bytes 4731392 | tf_op jit(solution)/shard_map/jit(_where)/select_n | solution.py:305
  16.1 1.0 fusion.93
  17.2 0.5 fusion.9
  17.6 0.2 fusion.34
  18.2 0.2 multiply_cosine_fusion
  18.7 0.2 copy.47
  19.0 0.7 pad_maximum_fusion.keys_ref
  19.7 0.7 maximum_maximum_fusion.parts_ref
  20.4 9.2 %shard_map.211 = (bf16[4,64,576]{2,1,0:T(8,128)(2,1)}, f32[4,8,640]{2,1,0:T(8,128)}) custom-call(bf16[64,576]{1,0:T(8,128)(2,1)} %pad_maximum_fusion.keys_ref, f32[4,8,640]{2,1,0:T(8,128)} %maximum_maximum_fusion.parts_ref), custom_call_target="tpu_custom_call" | custom-call | tf_op jit(solution)/shard_map/pallas_call | solution.py:198
  29.7 1.3 convolution_bitcast_fusion
  31.2 1.2 fusion.94
  32.5 0.4 fusion.11
  32.9 0.2 copy.48
  33.1 0.3 copy-done.8
  33.5 0.2 slice_reduce_fusion
  33.9 0.3 fusion.14
  34.4 3.2 %multiply_reduce_fusion = (f32[65]{0:T(128)S(1)}, f32[65,2048]{1,0:T(8,128)S(1)}) fusion(bf16[65,1024]{1,0:T(8,128)(2,1)S(1)} %bitcast.113, bf16[1024,2048]{1,0:T(8,128)(2,1)} %param.33, bf16[1,2048]{1,0:T(2,128)(2,1)S(1)} %dynamic-slice_bitcast_fusion, bf16[64,2048]{1,0:T(8,128)(2,1)S(1)} %bitcast.120), kind=kOutput, calls=%fused_computation.38 | convolution fusion | flops 273561536 | bytes 5126404 | tf_op jit(solution)/shard_map/dot_general | solution.py:388
  37.8 0.2 fusion.18
  38.2 3.3 %convert_bitcast_fusion = bf16[128,8,2048]{2,1,0:T(8,128)(2,1)} fusion(bf16[65,1024]{0,1:T(8,128)(2,1)S(1)} %bitcast.112, f32[65,2048]{1,0:T(8,128)S(1)} %get-tuple-element.45, f32[2048]{0:T(1024)S(1)} %copy-done.12, f32[65]{0:T(128)S(1)} %add_rsqrt_fusion), kind=kOutput, calls=%fused_computation.1 | convolution fusion | flops 275126272 | bytes 4868356 | tf_op jit(solution)/shard_map/dot_general | solution.py:417
  41.5 10.5 %all-to-all-start = ((bf16[128,8,2048]{2,1,0:T(8,128)(2,1)}), bf16[128,8,2048]{2,1,0:T(8,128)(2,1)}, u32[]{:S(2)}, u32[]{:S(2)}) async-start(bf16[128,8,2048]{2,1,0:T(8,128)(2,1)} %convert_bitcast_fusion), calls=%async_computation | async-start | bytes 8388608 | tf_op jit(solution)/shard_map/all_to_all | solution.py:421
  52.0 4.6 %copy.51 = bf16[1,2048,704]{2,1,0:T(8,128)(2,1)} copy(bf16[1,2048,704]{1,2,0:T(8,128)(2,1)} %param.37) | data formatting | bytes 5767168 | tf_op args[17]
  56.6 4.6 %copy.52 = bf16[1,2048,704]{2,1,0:T(8,128)(2,1)} copy(bf16[1,2048,704]{1,2,0:T(8,128)(2,1)} %param.38) | data formatting | bytes 5767168 | tf_op args[18]
  61.3 46.4 %all-to-all-done = bf16[128,8,2048]{2,1,0:T(8,128)(2,1)} async-done(((bf16[128,8,2048]{2,1,0:T(8,128)(2,1)}), bf16[128,8,2048]{2,1,0:T(8,128)(2,1)}, u32[]{:S(2)}, u32[]{:S(2)}) %all-to-all-start) | async-done | bytes 4194336 | tf_op jit(solution)/shard_map/all_to_all | solution.py:421
  107.7 1.9 copy-done.1
  109.5 1.8 copy-done.2
  111.4 13.7 %shard_map.212 = bf16[1024,2048]{1,0:T(8,128)(2,1)} custom-call(bf16[1024,2048]{1,0:T(8,128)(2,1)} %bitcast.36.x_ref, bf16[2048,704]{1,0:T(8,128)(2,1)S(1)} %bitcast.108, bf16[2048,704]{1,0:T(8,128)(2,1)} %bitcast.111, bf16[704,2048]{1,0:T(8,128)(2,1)S(1)} %bitcast.109), custom_call_target="tpu_custom_call" | custom-call | flops 8858370048 | bytes 17039360 | tf_op jit(solution)/shard_map/pallas_call | solution.py:226
  125.1 4.9 %all-to-all-start.1 = ((bf16[128,8,2048]{2,1,0:T(8,128)(2,1)}), bf16[128,8,2048]{2,1,0:T(8,128)(2,1)}, u32[]{:S(2)}, u32[]{:S(2)}) async-start(bf16[128,8,2048]{2,1,0:T(8,128)(2,1)} %bitcast.110), calls=%async_computation.1 | async-start | bytes 8388608 | tf_op jit(solution)/shard_map/all_to_all | solution.py:426
  130.0 1.3 fusion.63
  131.3 1.3 fusion.65
  132.6 0.5 fusion.17
  133.1 0.2 select_reduce_fusion
  133.3 4.6 %select_select_fusion = bf16[32,64,576]{2,1,0:T(8,128)(2,1)} fusion(bf16[32,64,576]{2,1,0:T(8,128)(2,1)} %param.31, pred[32,64]{1,0:T(8,128)(4,1)S(1)} %get-tuple-element.50, pred[32,64]{1,0:T(8,128)(4,1)S(1)} %get-tuple-element.51, pred[32,64]{1,0:T(8,128)(4,1)S(1)} %get-tuple-element.52, pred[32,64]{1,0:T(8,128)(4,1)S(1)} %get-tuple-element.53, ...), kind=kLoop, calls=%fused_computation.6 | loop fusion | flops 4718592 | bytes 4731392 | tf_op jit(solution)/shard_map/jit(_where)/select_n | solution.py:305
  137.9 46.1 %all-to-all-done.1 = bf16[128,8,2048]{2,1,0:T(8,128)(2,1)} async-done(((bf16[128,8,2048]{2,1,0:T(8,128)(2,1)}), bf16[128,8,2048]{2,1,0:T(8,128)(2,1)}, u32[]{:S(2)}, u32[]{:S(2)}) %all-to-all-start.1) | async-done | bytes 4194336 | tf_op jit(solution)/shard_map/all_to_all | solution.py:426
  184.1 3.6 %fusion.3 = bf16[65,2048]{1,0:T(8,128)(2,1)S(1)} fusion(f32[65,2048]{1,0:T(8,128)S(1)} %get-tuple-element.45, f32[65,512]{1,0:T(8,128)S(1)} %select_reduce_fusion, bf16[64,2,8,2048]{3,2,1,0:T(8,128)(2,1)} %bitcast.41), kind=kOutput, calls=%fused_computation.9 | convolution fusion | flops 822349824 | bytes 5126144 | tf_op jit(solution)/shard_map/dot_general | solution.py:433
  187.7 0.7 slice_bitcast_fusion.2
  188.4 0.6 slice_bitcast_fusion.3
  (71 shorter events, 2.5 us)
Async XLA Ops:
  0.6 33.3 %copy-start = (bf16[8,512,128]{2,1,0:T(8,128)(2,1)S(1)}, bf16[8,512,128]{2,1,0:T(8,128)(2,1)}, u32[]{:S(2)}) copy-start(bf16[8,512,128]{2,1,0:T(8,128)(2,1)} %param.32) | copy-start | bytes 3145732
  11.5 4.6 %copy-start.11 = (bf16[4,1,8,512]{3,2,1,0:T(8,128)(2,1)S(1)}, bf16[4,1,8,512]{3,2,1,0:T(8,128)(2,1)}, u32[]{:S(2)}) copy-start(bf16[4,1,8,512]{3,2,1,0:T(8,128)(2,1)} %param.26) | copy-start | bytes 98308
  17.1 1.0 copy-start.14
  17.1 1.1 copy-start.9
  17.1 12.5 %copy-start.3 = (bf16[1,64,8,512]{3,2,1,0:T(8,128)(2,1)S(1)}, bf16[1,64,8,512]{3,2,1,0:T(8,128)(2,1)}, u32[]{:S(2)}) copy-start(bf16[1,64,8,512]{3,2,1,0:T(8,128)(2,1)} %param.21) | copy-start | bytes 1572868
  17.1 13.9 %copy-start.5 = (bf16[1,64,8,64]{3,2,1,0:T(8,128)(2,1)S(1)}, bf16[1,64,8,64]{3,2,1,0:T(8,128)(2,1)}, u32[]{:S(2)}) copy-start(bf16[1,64,8,64]{3,2,1,0:T(8,128)(2,1)} %param.22) | copy-start | bytes 196612
  29.6 2.9 %copy-start.6 = (bf16[4,64,576]{2,1,0:T(8,128)(2,1)S(1)}, bf16[4,64,576]{2,1,0:T(8,128)(2,1)}, u32[]{:S(2)}) copy-start(bf16[4,64,576]{2,1,0:T(8,128)(2,1)} %get-tuple-element.5) | copy-start | bytes 884740
  32.5 0.9 copy-start.8
  32.9 1.5 copy-start.13
  32.9 1.5 copy-start.7
  34.3 3.3 %copy-start.10 = (s32[65,6]{0,1:T(8,128)S(1)}, s32[65,6]{0,1:T(8,128)}, u32[]{:S(2)}) copy-start(s32[65,6]{0,1:T(8,128)} %param.36) | copy-start | bytes 4684
  34.4 3.8 %copy-start.12 = (f32[2048]{0:T(1024)S(1)}, f32[2048]{0:T(1024)}, u32[]{:S(2)}) copy-start(f32[2048]{0:T(1024)} %param.34) | copy-start | bytes 24580
  41.5 66.2 %all-to-all-start = ((bf16[128,8,2048]{2,1,0:T(8,128)(2,1)}), bf16[128,8,2048]{2,1,0:T(8,128)(2,1)}, u32[]{:S(2)}, u32[]{:S(2)}) async-start(bf16[128,8,2048]{2,1,0:T(8,128)(2,1)} %convert_bitcast_fusion), calls=%async_computation | async-start | bytes 8388608 | tf_op jit(solution)/shard_map/all_to_all | solution.py:421
  107.7 1.9 copy-start.1
  109.5 1.8 copy-start.2
  125.1 7.5 %copy-start.4 = (f32[2048,64]{0,1:T(8,128)S(1)}, f32[2048,64]{0,1:T(8,128)}, u32[]{:S(2)}) copy-start(f32[2048,64]{0,1:T(8,128)} %param.35) | copy-start | bytes 1572868
  125.1 59.0 %all-to-all-start.1 = ((bf16[128,8,2048]{2,1,0:T(8,128)(2,1)}), bf16[128,8,2048]{2,1,0:T(8,128)(2,1)}, u32[]{:S(2)}, u32[]{:S(2)}) async-start(bf16[128,8,2048]{2,1,0:T(8,128)(2,1)} %bitcast.110), calls=%async_computation.1 | async-start | bytes 8388608 | tf_op jit(solution)/shard_map/all_to_all | solution.py:426

commit v14 on v13

--- a/solution.py
+++ b/solution.py
@@ -175,10 +175,6 @@
             device_id_type=MESH,
         )
 
-    own_keys = pltpu.make_async_copy(keys_ref, keys_out.at[me], sems.at[4, 0])
-    own_parts = pltpu.make_async_copy(parts_ref.at[me], parts_out.at[me], sems.at[4, 1])
-    own_keys.start()
-    own_parts.start()
     for step in range(1, n_ctx):
         other = lax.rem(me + step, n_ctx)
         key_copy(me, other).start()
@@ -190,8 +186,6 @@
         part_copy(me, other).wait_send()
         key_copy(source, me).wait_recv()
         part_copy(source, me).wait_recv()
-    own_keys.wait()
-    own_parts.wait()
 
 
 def context_exchange(keys, parts, n_ctx):
@@ -203,7 +197,7 @@
         ),
         in_specs=[pl.BlockSpec(memory_space=pl.ANY)] * 2,
         out_specs=(pl.BlockSpec(memory_space=pl.ANY), pl.BlockSpec(memory_space=pl.ANY)),
-        scratch_shapes=[pltpu.SemaphoreType.DMA((5, n_ctx))],
+        scratch_shapes=[pltpu.SemaphoreType.DMA((4, n_ctx))],
         compiler_params=pltpu.CompilerParams(collective_id=2, has_side_effects=True),
     )(keys, parts)
 
@@ -344,6 +338,10 @@
         axis=2,
     ).reshape(ctx_count, dec_share * head_count, part_width)
     keys_all, own_parts = context_exchange(stored, dec_block, ctx_count)
+    keys_all = lax.dynamic_update_index_in_dim(keys_all, stored, ctx_index, 0)
+    own_parts = lax.dynamic_update_index_in_dim(
+        own_parts, lax.dynamic_index_in_dim(dec_block, ctx_index, 0, False), ctx_index, 0
+    )
     moving = keys_all.reshape(ctx_count * shard_rows, row_width)
     own_parts = own_parts.reshape(ctx_count, dec_share, head_count, part_width)
     part_accum = own_parts[..., :DC]

time: 190 us -> 190 us (level)
  matrix products: 15.4 us -> 13.2 us
    dot_general x1, matrix products: 3.18 us -> 1 us  [body(): jnp.dot(values.reshape(values.shape[0], -1), w_out, preferred_element_typ...]
    unnamed x34 -> x36, local copies, waits for them, and re-layouts: 13.4 us -> 13.4 us
where the time goes in v14:
time: 190 us; the launch traced here: 189 us
  waiting for transfers between devices  92.5 us (49%)
  other arithmetic  24.1 us (13%)
  Pallas kernels  22.9 us (12%)
  local copies, waits for them, and re-layouts  19.4 us (10%)
  starting transfers between devices  15.4 us (8%)
  matrix products  13.2 us (7%)
    all_to_all x1, waiting for transfers between devices, body(): lax.all_to_all(doubled, ('ctx', 'req'), split_axis=0, concat_axis=0, tile...  46.4 us
    all_to_all x1, waiting for transfers between devices, body(): lax.all_to_all(partial_out, ('ctx', 'req'), split_axis=0, concat_axis=0,...  46.1 us
    pallas_call x1, Pallas kernels, ffn_half(): pl.pallas_call(ffn_kernel, grid=(rows // tile,), in_specs=[pl.BlockSpec((...  13.7 us
    unnamed x36, local copies, waits for them, and re-layouts  13.4 us
    all_to_all x1, starting transfers between devices, body(): lax.all_to_all(doubled, ('ctx', 'req'), split_axis=0, concat_axis=0, tile...  10.5 us
    pallas_call x1, Pallas kernels, context_exchange(): pl.pallas_call(functools.partial(context_kernel, n_ctx), out_shape=(jax.S...  9.16 us
    select_n x2, other arithmetic, body(): jnp.where(row_ids == target[request], new_rows[request][None, :], flat_pool)  9.14 us
    eq x4, other arithmetic, body(): row_ids == target[request]  5.21 us
  transfers between devices with their start and end apart: 2, of which 2 were waited for; matrix products, arithmetic and copies ran while one was open for 9% of the time, Pallas kernels for 0%

profile of v14, /device:TPU:8, one launch (start us, length us, event | category | flops | bytes accessed | tf_op | source)
XLA Modules:
  0.0 188.7 jit_solution(2884360666007572344)
XLA Ops:
  0.7 0.8 slice_bitcast_fusion.5
  1.4 0.7 slice_bitcast_fusion.4
  2.1 0.8 select_reduce_fusion.4
  2.9 0.8 fusion.68
  3.7 0.7 convert_bitcast_fusion.1
  4.4 0.9 select_reduce_fusion.7
  5.3 0.7 compare_select_fusion.2
  5.9 0.7 fusion.92
  7.3 1.3 iota_compare_fusion.5
  8.7 1.3 iota_compare_fusion.7
  9.9 0.9 fusion.70
  10.8 0.7 fusion.58
  11.5 4.5 %fusion.2 = bf16[2048,576]{1,0:T(8,128)(2,1)S(1)} fusion(bf16[32,64,576]{2,1,0:T(8,128)(2,1)} %param.31, pred[2048]{0:T(1024)(128)(4,1)S(1)} %get-tuple-element.46, pred[2048]{0:T(1024)(128)(4,1)S(1)} %get-tuple-element.47, pred[2048]{0:T(1024)(128)(4,1)S(1)} %get-tuple-element.48, pred[2048]{0:T(1024)(128)(4,1)S(1)} %get-tuple-element.49, ...), kind=kLoop, calls=%fused_computation.5 | loop fusion | flops 4718592 | bytes 4731392 | tf_op jit(solution)/shard_map/jit(_where)/select_n | solution.py:299
  16.1 1.0 fusion.93
  17.2 0.5 fusion.9
  17.6 0.2 fusion.34
  18.2 0.2 multiply_cosine_fusion
  18.7 0.2 copy.47
  19.0 0.7 pad_maximum_fusion.keys_ref
  19.7 0.7 maximum_maximum_fusion.parts_ref
  20.4 9.2 %shard_map.211 = (bf16[4,64,576]{2,1,0:T(8,128)(2,1)}, f32[4,8,640]{2,1,0:T(8,128)}) custom-call(bf16[64,576]{1,0:T(8,128)(2,1)} %pad_maximum_fusion.keys_ref, f32[4,8,640]{2,1,0:T(8,128)} %maximum_maximum_fusion.parts_ref), custom_call_target="tpu_custom_call" | custom-call | tf_op jit(solution)/shard_map/pallas_call | solution.py:192
  29.6 0.7 bitcast_dynamic-update-slice_fusion
  30.3 1.3 convolution_bitcast_fusion
  31.8 1.2 fusion.94
  33.2 0.4 fusion.11
  33.7 0.3 copy-done.9
  34.1 1.2 bitcast_dynamic-update-slice_fusion.1
  35.7 0.3 fusion.14
  36.3 1.0 multiply_reduce_fusion
  37.5 0.2 fusion.18
  37.9 3.3 %convert_bitcast_fusion = bf16[128,8,2048]{2,1,0:T(8,128)(2,1)} fusion(bf16[65,1024]{0,1:T(8,128)(2,1)S(1)} %bitcast.116, f32[65,2048]{1,0:T(8,128)S(1)} %get-tuple-element.45, f32[2048]{0:T(1024)S(1)} %copy-done.13, f32[65]{0:T(128)S(1)} %add_rsqrt_fusion), kind=kOutput, calls=%fused_computation.1 | convolution fusion | flops 275126272 | bytes 4868356 | tf_op jit(solution)/shard_map/dot_general | solution.py:415
  41.2 10.5 %all-to-all-start = ((bf16[128,8,2048]{2,1,0:T(8,128)(2,1)}), bf16[128,8,2048]{2,1,0:T(8,128)(2,1)}, u32[]{:S(2)}, u32[]{:S(2)}) async-start(bf16[128,8,2048]{2,1,0:T(8,128)(2,1)} %convert_bitcast_fusion), calls=%async_computation | async-start | bytes 8388608 | tf_op jit(solution)/shard_map/all_to_all | solution.py:419
  51.7 4.6 %copy.51 = bf16[1,2048,704]{2,1,0:T(8,128)(2,1)} copy(bf16[1,2048,704]{1,2,0:T(8,128)(2,1)} %param.37) | data formatting | bytes 5767168 | tf_op args[17]
  56.3 4.6 %copy.52 = bf16[1,2048,704]{2,1,0:T(8,128)(2,1)} copy(bf16[1,2048,704]{1,2,0:T(8,128)(2,1)} %param.38) | data formatting | bytes 5767168 | tf_op args[18]
  60.9 46.4 %all-to-all-done = bf16[128,8,2048]{2,1,0:T(8,128)(2,1)} async-done(((bf16[128,8,2048]{2,1,0:T(8,128)(2,1)}), bf16[128,8,2048]{2,1,0:T(8,128)(2,1)}, u32[]{:S(2)}, u32[]{:S(2)}) %all-to-all-start) | async-done | bytes 4194336 | tf_op jit(solution)/shard_map/all_to_all | solution.py:419
  107.3 1.9 %copy-done.1 = bf16[1,2048,704]{2,1,0:T(8,128)(2,1)S(1)} copy-done((bf16[1,2048,704]{2,1,0:T(8,128)(2,1)S(1)}, bf16[1,2048,704]{2,1,0:T(8,128)(2,1)}, u32[]{:S(2)}) %copy-start.1) | copy-done | bytes 2883608
  109.2 1.8 copy-done.2
  111.0 13.7 %shard_map.212 = bf16[1024,2048]{1,0:T(8,128)(2,1)} custom-call(bf16[1024,2048]{1,0:T(8,128)(2,1)} %bitcast.38.x_ref, bf16[2048,704]{1,0:T(8,128)(2,1)S(1)} %bitcast.112, bf16[2048,704]{1,0:T(8,128)(2,1)} %bitcast.115, bf16[704,2048]{1,0:T(8,128)(2,1)S(1)} %bitcast.113), custom_call_target="tpu_custom_call" | custom-call | flops 8858370048 | bytes 17039360 | tf_op jit(solution)/shard_map/pallas_call | solution.py:220
  124.7 4.9 %all-to-all-start.1 = ((bf16[128,8,2048]{2,1,0:T(8,128)(2,1)}), bf16[128,8,2048]{2,1,0:T(8,128)(2,1)}, u32[]{:S(2)}, u32[]{:S(2)}) async-start(bf16[128,8,2048]{2,1,0:T(8,128)(2,1)} %bitcast.114), calls=%async_computation.1 | async-start | bytes 8388608 | tf_op jit(solution)/shard_map/all_to_all | solution.py:424
  129.6 1.3 fusion.63
  131.0 1.3 fusion.65
  132.3 0.5 fusion.17
  132.8 0.2 select_reduce_fusion
  133.0 4.6 %select_select_fusion = bf16[32,64,576]{2,1,0:T(8,128)(2,1)} fusion(bf16[32,64,576]{2,1,0:T(8,128)(2,1)} %param.31, pred[32,64]{1,0:T(8,128)(4,1)S(1)} %get-tuple-element.50, pred[32,64]{1,0:T(8,128)(4,1)S(1)} %get-tuple-element.51, pred[32,64]{1,0:T(8,128)(4,1)S(1)} %get-tuple-element.52, pred[32,64]{1,0:T(8,128)(4,1)S(1)} %get-tuple-element.53, ...), kind=kLoop, calls=%fused_computation.6 | loop fusion | flops 4718592 | bytes 4731392 | tf_op jit(solution)/shard_map/jit(_where)/select_n | solution.py:299
  137.6 46.1 %all-to-all-done.1 = bf16[128,8,2048]{2,1,0:T(8,128)(2,1)} async-done(((bf16[128,8,2048]{2,1,0:T(8,128)(2,1)}), bf16[128,8,2048]{2,1,0:T(8,128)(2,1)}, u32[]{:S(2)}, u32[]{:S(2)}) %all-to-all-start.1) | async-done | bytes 4194336 | tf_op jit(solution)/shard_map/all_to_all | solution.py:424
  183.7 3.6 %fusion.3 = bf16[65,2048]{1,0:T(8,128)(2,1)S(1)} fusion(f32[65,2048]{1,0:T(8,128)S(1)} %get-tuple-element.45, f32[65,512]{1,0:T(8,128)S(1)} %select_reduce_fusion, bf16[64,2,8,2048]{3,2,1,0:T(8,128)(2,1)} %bitcast.43), kind=kOutput, calls=%fused_computation.9 | convolution fusion | flops 822349824 | bytes 5126144 | tf_op jit(solution)/shard_map/dot_general | solution.py:431
  187.4 0.7 slice_bitcast_fusion.2
  188.1 0.6 slice_bitcast_fusion.3
  (75 shorter events, 2.9 us)
Async XLA Ops:
  0.6 35.1 %copy-start = (bf16[8,512,128]{2,1,0:T(8,128)(2,1)S(1)}, bf16[8,512,128]{2,1,0:T(8,128)(2,1)}, u32[]{:S(2)}) copy-start(bf16[8,512,128]{2,1,0:T(8,128)(2,1)} %param.32) | copy-start | bytes 3145732
  11.5 4.6 %copy-start.12 = (bf16[4,1,8,512]{3,2,1,0:T(8,128)(2,1)S(1)}, bf16[4,1,8,512]{3,2,1,0:T(8,128)(2,1)}, u32[]{:S(2)}) copy-start(bf16[4,1,8,512]{3,2,1,0:T(8,128)(2,1)} %param.26) | copy-start | bytes 98308
  17.1 1.0 copy-start.15
  17.1 1.1 copy-start.10
  17.1 13.2 %copy-start.4 = (bf16[1,64,8,512]{3,2,1,0:T(8,128)(2,1)S(1)}, bf16[1,64,8,512]{3,2,1,0:T(8,128)(2,1)}, u32[]{:S(2)}) copy-start(bf16[1,64,8,512]{3,2,1,0:T(8,128)(2,1)} %param.21) | copy-start | bytes 1572868
  17.1 14.5 %copy-start.6 = (bf16[1,64,8,64]{3,2,1,0:T(8,128)(2,1)S(1)}, bf16[1,64,8,64]{3,2,1,0:T(8,128)(2,1)}, u32[]{:S(2)}) copy-start(bf16[1,64,8,64]{3,2,1,0:T(8,128)(2,1)} %param.22) | copy-start | bytes 196612
  30.3 2.9 %copy-start.7 = (bf16[4,64,576]{2,1,0:T(8,128)(2,1)S(1)}, bf16[4,64,576]{2,1,0:T(8,128)(2,1)}, u32[]{:S(2)}) copy-start(bf16[4,64,576]{2,1,0:T(8,128)(2,1)} %bitcast_dynamic-update-slice_fusion) | copy-start | bytes 884740
  33.2 0.9 copy-start.9
  33.2 3.0 %copy-start.3 = (bf16[1024,2048]{1,0:T(8,128)(2,1)S(1)}, bf16[1024,2048]{1,0:T(8,128)(2,1)}, u32[]{:S(2)}) copy-start(bf16[1024,2048]{1,0:T(8,128)(2,1)} %param.33) | copy-start | bytes 12582916
  33.6 2.6 %copy-start.14 = (bf16[4,1,2048]{2,0,1:T(4,128)(2,1)S(1)}, bf16[4,1,2048]{2,0,1:T(4,128)(2,1)}, u32[]{:S(2)}) copy-start(bf16[4,1,2048]{2,0,1:T(4,128)(2,1)} %param.28) | copy-start | bytes 49156
  33.6 2.7 %copy-start.8 = (bf16[1,64,2048]{2,1,0:T(8,128)(2,1)S(1)}, bf16[1,64,2048]{2,1,0:T(8,128)(2,1)}, u32[]{:S(2)}) copy-start(bf16[1,64,2048]{2,1,0:T(8,128)(2,1)} %param.23) | copy-start | bytes 786436
  36.2 1.1 copy-start.11
  36.2 1.7 copy-start.13
  41.2 66.2 %all-to-all-start = ((bf16[128,8,2048]{2,1,0:T(8,128)(2,1)}), bf16[128,8,2048]{2,1,0:T(8,128)(2,1)}, u32[]{:S(2)}, u32[]{:S(2)}) async-start(bf16[128,8,2048]{2,1,0:T(8,128)(2,1)} %convert_bitcast_fusion), calls=%async_computation | async-start | bytes 8388608 | tf_op jit(solution)/shard_map/all_to_all | solution.py:419
  107.3 1.9 %copy-start.1 = (bf16[1,2048,704]{2,1,0:T(8,128)(2,1)S(1)}, bf16[1,2048,704]{2,1,0:T(8,128)(2,1)}, u32[]{:S(2)}) copy-start(bf16[1,2048,704]{2,1,0:T(8,128)(2,1)} %copy.51) | copy-start | bytes 8650756
  109.2 1.8 copy-start.2
  124.7 7.5 %copy-start.5 = (f32[2048,64]{0,1:T(8,128)S(1)}, f32[2048,64]{0,1:T(8,128)}, u32[]{:S(2)}) copy-start(f32[2048,64]{0,1:T(8,128)} %param.35) | copy-start | bytes 1572868
  124.7 59.0 %all-to-all-start.1 = ((bf16[128,8,2048]{2,1,0:T(8,128)(2,1)}), bf16[128,8,2048]{2,1,0:T(8,128)(2,1)}, u32[]{:S(2)}, u32[]{:S(2)}) async-start(bf16[128,8,2048]{2,1,0:T(8,128)(2,1)} %bitcast.114), calls=%async_computation.1 | async-start | bytes 8388608 | tf_op jit(solution)/shard_map/all_to_all | solution.py:424

commit v15 on v14

--- a/solution.py
+++ b/solution.py
@@ -294,9 +294,11 @@
         owner_ctx == ctx_index, slot_of * page_rows + lengths % page_rows, slot_count * page_rows
     )
     row_ids = jnp.arange(slot_count * page_rows)[:, None]
-    flat_pool = cache_pool.reshape(slot_count * page_rows, row_width)
+    raw_pool = cache_pool.reshape(slot_count * page_rows, row_width)
+    flat_pool = raw_pool
     for request in range(request_count):
         flat_pool = jnp.where(row_ids == target[request], new_rows[request][None, :], flat_pool)
+    new_hit = (row_ids == target[None, :])[:, :, None]
     page_valid = jnp.any(page_hit, axis=1)
     page_logical = jnp.sum(page_hit.astype(jnp.int32) * jnp.arange(pages_dev)[None, :, None], axis=1)
     page_start = (ctx_index * pages_dev + page_logical) * page_rows
@@ -312,19 +314,28 @@
     dec_queries = jnp.concatenate([dec_qlat[:, 0], query_rot], axis=-1)
     flat_queries = dec_queries.reshape(request_count * head_count, row_width)
     dec_scores = (
-        jnp.dot(flat_pool, flat_queries.T, preferred_element_type=jnp.float32) * score_scale
+        jnp.dot(raw_pool, flat_queries.T, preferred_element_type=jnp.float32) * score_scale
     ).reshape(slot_count * page_rows, request_count, head_count)
+    new_scores = (
+        jnp.einsum("rd,rhd->rh", new_rows, dec_queries, preferred_element_type=jnp.float32)
+        * score_scale
+    )
+    dec_scores = jnp.where(new_hit, new_scores[None], dec_scores)
     dec_seen = jnp.transpose(dec_visible[:, 0, :])[:, :, None]
     dec_masked = jnp.where(dec_seen, dec_scores, NEG_FILL)
     local_peak = jnp.max(dec_masked, axis=0)
     dec_weights = jnp.where(dec_seen, jnp.exp(dec_masked - local_peak[None]), 0.0)
     local_total = jnp.sum(dec_weights, axis=0)
+    rounded = dec_weights.astype(jnp.bfloat16)
+    new_weight = jnp.sum(jnp.where(new_hit, rounded, 0.0).astype(jnp.float32), axis=0)
     local_accum = lax.dot_general(
-        dec_weights.astype(jnp.bfloat16).reshape(slot_count * page_rows, -1),
-        flat_pool[:, :DC],
+        jnp.where(new_hit, jnp.zeros_like(rounded), rounded).reshape(slot_count * page_rows, -1),
+        raw_pool[:, :DC],
         (((0,), (0,)), ((), ())),
         preferred_element_type=jnp.float32,
-    ).reshape(request_count, head_count, DC)
+    ).reshape(request_count, head_count, DC) + new_weight[..., None] * new_rows[:, None, :DC].astype(
+        jnp.float32
+    )
 
     dec_share = request_count // ctx_count
     part_width = 128 * ((DC + 2 + 127) // 128)

time: 190 us -> 186 us (0.979)
  other arithmetic: 24.1 us -> 17.8 us
  matrix products: 13.2 us -> 17.5 us
    select_n x2 -> x1, other arithmetic: 9.14 us -> 4.6 us  [body(): jnp.where(row_ids == target[request], new_rows[request][None, :], flat_pool)]
    dot_general x2 -> x3, matrix products: 1.49 us -> 5.79 us  [the longest x1 2.75 us: body(): jnp.dot(raw_pool, flat_queries.T, preferred_element_type=jnp.float32)]
    eq x4 -> x2, other arithmetic: 5.21 us -> 2.53 us  [body(): row_ids == target[request]]
    unnamed x36 -> x34, local copies, waits for them, and re-layouts: 13.4 us -> 13.4 us
  transfers between devices with their start and end apart: 2 -> 2, of which waited for: 2 -> 2; matrix products, arithmetic and copies ran while one was open for 9% -> 10% of each run, Pallas kernels for 0% -> 0%
where the time goes in v15:
time: 186 us; the launch traced here: 185 us
  waiting for transfers between devices  91.9 us (49%)
  Pallas kernels  22.8 us (12%)
  local copies, waits for them, and re-layouts  18.8 us (10%)
  other arithmetic  17.8 us (10%)
  matrix products  17.5 us (9%)
  starting transfers between devices  15.4 us (8%)
    all_to_all x1, waiting for transfers between devices, body(): lax.all_to_all(doubled, ('ctx', 'req'), split_axis=0, concat_axis=0, tile...  46.4 us
    all_to_all x1, waiting for transfers between devices, body(): lax.all_to_all(partial_out, ('ctx', 'req'), split_axis=0, concat_axis=0,...  45.5 us
    pallas_call x1, Pallas kernels, ffn_half(): pl.pallas_call(ffn_kernel, grid=(rows // tile,), in_specs=[pl.BlockSpec((...  13.7 us
    unnamed x34, local copies, waits for them, and re-layouts  13.4 us
    all_to_all x1, starting transfers between devices, body(): lax.all_to_all(doubled, ('ctx', 'req'), split_axis=0, concat_axis=0, tile...  10.5 us
    pallas_call x1, Pallas kernels, context_exchange(): pl.pallas_call(functools.partial(context_kernel, n_ctx), out_shape=(jax.S...  9.16 us
    all_to_all x1, starting transfers between devices, body(): lax.all_to_all(partial_out, ('ctx', 'req'), split_axis=0, concat_axis=0,...  4.89 us
    select_n x1, other arithmetic, body(): jnp.where(row_ids == target[request], new_rows[request][None, :], flat_pool)  4.6 us
  transfers between devices with their start and end apart: 2, of which 2 were waited for; matrix products, arithmetic and copies ran while one was open for 10% of the time, Pallas kernels for 0%

profile of v15, /device:TPU:8, one launch (start us, length us, event | category | flops | bytes accessed | tf_op | source)
XLA Modules:
  0.0 185.4 jit_solution(14361088552198412914)
XLA Ops:
  0.7 0.8 slice_bitcast_fusion.7
  1.4 0.7 fusion.95
  2.1 0.8 select_reduce_fusion.4
  2.9 0.8 fusion.73
  3.7 0.7 convert_bitcast_fusion.1
  4.6 0.9 fusion.65
  5.5 1.0 fusion.47
  7.0 0.9 select_reduce_fusion.7
  7.8 0.7 compare_select_fusion.2
  8.6 0.7 fusion.63
  9.4 2.7 %fusion.100 = (f32[32]{0:T(128)S(1)}, f32[2048,32]{0,1:T(8,128)S(1)}) fusion(bf16[2048,576]{1,0:T(8,128)(2,1)} %bitcast.131, bf16[32,32]{1,0:T(8,128)(2,1)S(1)} %bitcast.150, bf16[32,32]{1,0:T(8,128)(2,1)S(1)} %bitcast.149, bf16[32,512]{1,0:T(8,128)(2,1)} %bitcast.148, f32[32]{0:T(128)S(1)} %broadcast_in_dim.277, ...), kind=kOutput, calls=%fused_computation.212 | convolution fusion | flops 75870176 | bytes 2674944 | tf_op jit(solution)/shard_map/dot_general | solution.py:317
  12.2 0.3 convert_reduce_fusion
  12.8 0.2 multiply_cosine_fusion
  13.3 0.2 copy.47
  13.5 2.1 %fusion.14 = f32[4,8,512]{2,1,0:T(8,128)S(1)} fusion(bf16[2048,576]{1,0:T(8,128)(2,1)} %bitcast.132, pred[2048,4]{0,1:T(4,128)(4,1)S(1)} %iota_compare_fusion.4, f32[4,512]{1,0:T(4,128)S(1)} %get-tuple-element.26, f32[4,8]{1,0:T(4,128)S(1)} %mul.313, f32[2048,32]{0,1:T(8,128)S(1)} %get-tuple-element.43, f32[32]{0:T(128)S(1)} %get-tuple-element.42, ...), kind=kOutput, calls=%fused_computation.24 | convolution fusion | flops 67403776 | bytes 2449664 | tf_op jit(solution)/shard_map/dot_general | solution.py:331
  15.7 0.7 pad_maximum_fusion.keys_ref
  16.4 0.7 maximum_maximum_fusion.parts_ref
  17.1 9.2 %shard_map.211 = (bf16[4,64,576]{2,1,0:T(8,128)(2,1)}, f32[4,8,640]{2,1,0:T(8,128)}) custom-call(bf16[64,576]{1,0:T(8,128)(2,1)} %pad_maximum_fusion.keys_ref, f32[4,8,640]{2,1,0:T(8,128)} %maximum_maximum_fusion.parts_ref), custom_call_target="tpu_custom_call" | custom-call | tf_op jit(solution)/shard_map/pallas_call | solution.py:192
  26.3 0.7 bitcast_dynamic-update-slice_fusion
  27.0 1.3 convolution_bitcast_fusion
  28.5 1.2 fusion.101
  29.9 0.4 fusion.10
  30.3 0.2 copy.48
  30.4 0.3 copy-done.9
  30.7 1.2 bitcast_dynamic-update-slice_fusion.1
  32.0 0.2 slice_reduce_fusion
  32.4 0.3 fusion.13
  32.9 1.0 multiply_reduce_fusion
  34.2 0.2 fusion.18
  34.6 3.3 %convert_bitcast_fusion = bf16[128,8,2048]{2,1,0:T(8,128)(2,1)} fusion(bf16[65,1024]{0,1:T(8,128)(2,1)S(1)} %bitcast.135, f32[65,2048]{1,0:T(8,128)S(1)} %get-tuple-element.47, f32[2048]{0:T(1024)S(1)} %copy-done.12, f32[65]{0:T(128)S(1)} %add_rsqrt_fusion), kind=kOutput, calls=%fused_computation.1 | convolution fusion | flops 275126272 | bytes 4868356 | tf_op jit(solution)/shard_map/dot_general | solution.py:426
  37.9 10.5 %all-to-all-start = ((bf16[128,8,2048]{2,1,0:T(8,128)(2,1)}), bf16[128,8,2048]{2,1,0:T(8,128)(2,1)}, u32[]{:S(2)}, u32[]{:S(2)}) async-start(bf16[128,8,2048]{2,1,0:T(8,128)(2,1)} %convert_bitcast_fusion), calls=%async_computation | async-start | bytes 8388608 | tf_op jit(solution)/shard_map/all_to_all | solution.py:430
  48.4 4.6 %copy.51 = bf16[1,2048,704]{2,1,0:T(8,128)(2,1)} copy(bf16[1,2048,704]{1,2,0:T(8,128)(2,1)} %param.37) | data formatting | bytes 5767168 | tf_op args[17]
  53.0 4.6 %copy.52 = bf16[1,2048,704]{2,1,0:T(8,128)(2,1)} copy(bf16[1,2048,704]{1,2,0:T(8,128)(2,1)} %param.38) | data formatting | bytes 5767168 | tf_op args[18]
  57.7 46.4 %all-to-all-done = bf16[128,8,2048]{2,1,0:T(8,128)(2,1)} async-done(((bf16[128,8,2048]{2,1,0:T(8,128)(2,1)}), bf16[128,8,2048]{2,1,0:T(8,128)(2,1)}, u32[]{:S(2)}, u32[]{:S(2)}) %all-to-all-start) | async-done | bytes 4194336 | tf_op jit(solution)/shard_map/all_to_all | solution.py:430
  104.1 1.9 %copy-done.1 = bf16[1,2048,704]{2,1,0:T(8,128)(2,1)S(1)} copy-done((bf16[1,2048,704]{2,1,0:T(8,128)(2,1)S(1)}, bf16[1,2048,704]{2,1,0:T(8,128)(2,1)}, u32[]{:S(2)}) %copy-start.1) | copy-done | bytes 2883608
  106.0 1.8 copy-done.2
  107.8 13.7 %shard_map.212 = bf16[1024,2048]{1,0:T(8,128)(2,1)} custom-call(bf16[1024,2048]{1,0:T(8,128)(2,1)} %bitcast.40.x_ref, bf16[2048,704]{1,0:T(8,128)(2,1)S(1)} %bitcast.129, bf16[2048,704]{1,0:T(8,128)(2,1)} %bitcast.134, bf16[704,2048]{1,0:T(8,128)(2,1)S(1)} %bitcast.130), custom_call_target="tpu_custom_call" | custom-call | flops 8858370048 | bytes 17039360 | tf_op jit(solution)/shard_map/pallas_call | solution.py:220
  121.4 4.9 %all-to-all-start.1 = ((bf16[128,8,2048]{2,1,0:T(8,128)(2,1)}), bf16[128,8,2048]{2,1,0:T(8,128)(2,1)}, u32[]{:S(2)}, u32[]{:S(2)}) async-start(bf16[128,8,2048]{2,1,0:T(8,128)(2,1)} %bitcast.133), calls=%async_computation.1 | async-start | bytes 8388608 | tf_op jit(solution)/shard_map/all_to_all | solution.py:435
  126.4 0.6 fusion.99
  127.0 1.3 fusion.68
  128.3 1.2 fusion.70
  129.6 0.5 fusion.17
  130.2 0.2 select_reduce_fusion
  130.4 4.6 %select_select_fusion = bf16[32,64,576]{2,1,0:T(8,128)(2,1)} fusion(bf16[32,64,576]{2,1,0:T(8,128)(2,1)} %param.31, pred[32,64]{1,0:T(8,128)(4,1)S(1)} %get-tuple-element.48, pred[32,64]{1,0:T(8,128)(4,1)S(1)} %get-tuple-element.49, pred[32,64]{1,0:T(8,128)(4,1)S(1)} %get-tuple-element.50, pred[32,64]{1,0:T(8,128)(4,1)S(1)} %get-tuple-element.51, ...), kind=kLoop, calls=%fused_computation.2 | loop fusion | flops 4718592 | bytes 4731392 | tf_op jit(solution)/shard_map/jit(_where)/select_n | solution.py:300
  135.0 45.5 %all-to-all-done.1 = bf16[128,8,2048]{2,1,0:T(8,128)(2,1)} async-done(((bf16[128,8,2048]{2,1,0:T(8,128)(2,1)}), bf16[128,8,2048]{2,1,0:T(8,128)(2,1)}, u32[]{:S(2)}, u32[]{:S(2)}) %all-to-all-start.1) | async-done | bytes 4194336 | tf_op jit(solution)/shard_map/all_to_all | solution.py:435
  180.4 3.6 %fusion = bf16[65,2048]{1,0:T(8,128)(2,1)S(1)} fusion(f32[65,2048]{1,0:T(8,128)S(1)} %get-tuple-element.47, f32[65,512]{1,0:T(8,128)S(1)} %select_reduce_fusion, bf16[64,2,8,2048]{3,2,1,0:T(8,128)(2,1)} %bitcast.45), kind=kOutput, calls=%fused_computation.5 | convolution fusion | flops 822349824 | bytes 5126144 | tf_op jit(solution)/shard_map/dot_general | solution.py:442
  184.1 0.7 slice_bitcast_fusion.4
  184.8 0.6 slice_bitcast_fusion.5
  (76 shorter events, 2.9 us)
Async XLA Ops:
  0.6 31.8 %copy-start = (bf16[8,512,128]{2,1,0:T(8,128)(2,1)S(1)}, bf16[8,512,128]{2,1,0:T(8,128)(2,1)}, u32[]{:S(2)}) copy-start(bf16[8,512,128]{2,1,0:T(8,128)(2,1)} %param.32) | copy-start | bytes 3145732
  0.6 12.0 %copy-start.14 = (s32[8]{0:T(128)S(1)}, s32[8]{0:T(128)}, u32[]{:S(2)}) copy-start(s32[8]{0:T(128)} %param.24) | copy-start | bytes 100
  0.7 12.1 %copy-start.10 = (bf16[1,64,576]{2,1,0:T(8,128)(2,1)S(1)}, bf16[1,64,576]{2,1,0:T(8,128)(2,1)}, u32[]{:S(2)}) copy-start(bf16[1,64,576]{2,1,0:T(8,128)(2,1)} %param.20) | copy-start | bytes 221188
  12.1 14.9 %copy-start.4 = (bf16[1,64,8,512]{3,2,1,0:T(8,128)(2,1)S(1)}, bf16[1,64,8,512]{3,2,1,0:T(8,128)(2,1)}, u32[]{:S(2)}) copy-start(bf16[1,64,8,512]{3,2,1,0:T(8,128)(2,1)} %param.21) | copy-start | bytes 1572868
  12.8 15.5 %copy-start.6 = (bf16[1,64,8,64]{3,2,1,0:T(8,128)(2,1)S(1)}, bf16[1,64,8,64]{3,2,1,0:T(8,128)(2,1)}, u32[]{:S(2)}) copy-start(bf16[1,64,8,64]{3,2,1,0:T(8,128)(2,1)} %param.22) | copy-start | bytes 196612
  27.0 2.9 %copy-start.7 = (bf16[4,64,576]{2,1,0:T(8,128)(2,1)S(1)}, bf16[4,64,576]{2,1,0:T(8,128)(2,1)}, u32[]{:S(2)}) copy-start(bf16[4,64,576]{2,1,0:T(8,128)(2,1)} %bitcast_dynamic-update-slice_fusion) | copy-start | bytes 884740
  29.9 0.9 copy-start.9
  29.9 3.0 %copy-start.3 = (bf16[1024,2048]{1,0:T(8,128)(2,1)S(1)}, bf16[1024,2048]{1,0:T(8,128)(2,1)}, u32[]{:S(2)}) copy-start(bf16[1024,2048]{1,0:T(8,128)(2,1)} %param.33) | copy-start | bytes 12582916
  30.2 2.6 %copy-start.13 = (bf16[4,1,2048]{2,0,1:T(4,128)(2,1)S(1)}, bf16[4,1,2048]{2,0,1:T(4,128)(2,1)}, u32[]{:S(2)}) copy-start(bf16[4,1,2048]{2,0,1:T(4,128)(2,1)} %param.28) | copy-start | bytes 49156
  30.2 2.7 %copy-start.8 = (bf16[1,64,2048]{2,1,0:T(8,128)(2,1)S(1)}, bf16[1,64,2048]{2,1,0:T(8,128)(2,1)}, u32[]{:S(2)}) copy-start(bf16[1,64,2048]{2,1,0:T(8,128)(2,1)} %param.23) | copy-start | bytes 786436
  32.9 1.1 copy-start.11
  32.9 1.7 copy-start.12
  37.9 66.2 %all-to-all-start = ((bf16[128,8,2048]{2,1,0:T(8,128)(2,1)}), bf16[128,8,2048]{2,1,0:T(8,128)(2,1)}, u32[]{:S(2)}, u32[]{:S(2)}) async-start(bf16[128,8,2048]{2,1,0:T(8,128)(2,1)} %convert_bitcast_fusion), calls=%async_computation | async-start | bytes 8388608 | tf_op jit(solution)/shard_map/all_to_all | solution.py:430
  104.1 1.9 %copy-start.1 = (bf16[1,2048,704]{2,1,0:T(8,128)(2,1)S(1)}, bf16[1,2048,704]{2,1,0:T(8,128)(2,1)}, u32[]{:S(2)}) copy-start(bf16[1,2048,704]{2,1,0:T(8,128)(2,1)} %copy.51) | copy-start | bytes 8650756
  106.0 1.8 copy-start.2
  121.4 8.2 %copy-start.5 = (f32[2048,64]{0,1:T(8,128)S(1)}, f32[2048,64]{0,1:T(8,128)}, u32[]{:S(2)}) copy-start(f32[2048,64]{0,1:T(8,128)} %param.35) | copy-start | bytes 1572868
  121.4 59.0 %all-to-all-start.1 = ((bf16[128,8,2048]{2,1,0:T(8,128)(2,1)}), bf16[128,8,2048]{2,1,0:T(8,128)(2,1)}, u32[]{:S(2)}, u32[]{:S(2)}) async-start(bf16[128,8,2048]{2,1,0:T(8,128)(2,1)} %bitcast.133), calls=%async_computation.1 | async-start | bytes 8388608 | tf_op jit(solution)/shard_map/all_to_all | solution.py:435

commit v16 on v15

--- a/solution.py
+++ b/solution.py
@@ -212,7 +212,7 @@
     )
 
 
-def ffn_half(inputs, gate_part, up_part, down_part, tile=256):
+def ffn_half(inputs, gate_part, up_part, down_part, tile=512):
     flat_rows = inputs.reshape(-1, inputs.shape[-1])
     rows, width = flat_rows.shape
     hidden = gate_part.shape[1]

time: 186 us -> 187 us (level)
  no operation moved by 1% of the time
where the time goes in v16:
time: 187 us; the launch traced here: 186 us
  waiting for transfers between devices  91.7 us (49%)
  Pallas kernels  23.1 us (12%)
  local copies, waits for them, and re-layouts  18.8 us (10%)
  other arithmetic  17.8 us (10%)
  matrix products  17.5 us (9%)
  starting transfers between devices  15.6 us (8%)
    all_to_all x1, waiting for transfers between devices, body(): lax.all_to_all(doubled, ('ctx', 'req'), split_axis=0, concat_axis=0, tile...  46.4 us
    all_to_all x1, waiting for transfers between devices, body(): lax.all_to_all(partial_out, ('ctx', 'req'), split_axis=0, concat_axis=0,...  45.3 us
    pallas_call x1, Pallas kernels, ffn_half(): pl.pallas_call(ffn_kernel, grid=(rows // tile,), in_specs=[pl.BlockSpec((...  14 us
    unnamed x34, local copies, waits for them, and re-layouts  13.4 us
    all_to_all x1, starting transfers between devices, body(): lax.all_to_all(doubled, ('ctx', 'req'), split_axis=0, concat_axis=0, tile...  10.5 us
    pallas_call x1, Pallas kernels, context_exchange(): pl.pallas_call(functools.partial(context_kernel, n_ctx), out_shape=(jax.S...  9.16 us
    all_to_all x1, starting transfers between devices, body(): lax.all_to_all(partial_out, ('ctx', 'req'), split_axis=0, concat_axis=0,...  5.07 us
    select_n x1, other arithmetic, body(): jnp.where(row_ids == target[request], new_rows[request][None, :], flat_pool)  4.6 us
  transfers between devices with their start and end apart: 2, of which 2 were waited for; matrix products, arithmetic and copies ran while one was open for 10% of the time, Pallas kernels for 0%

profile of v16, /device:TPU:8, one launch (start us, length us, event | category | flops | bytes accessed | tf_op | source)
XLA Modules:
  0.0 185.7 jit_solution(7440827591793161130)
XLA Ops:
  0.7 0.8 slice_bitcast_fusion.7
  1.4 0.7 fusion.95
  2.1 0.8 select_reduce_fusion.4
  2.9 0.8 fusion.73
  3.7 0.7 convert_bitcast_fusion.1
  4.6 0.9 fusion.65
  5.5 1.0 fusion.47
  7.0 0.9 select_reduce_fusion.7
  7.8 0.7 compare_select_fusion.2
  8.6 0.7 fusion.63
  9.4 2.7 %fusion.100 = (f32[32]{0:T(128)S(1)}, f32[2048,32]{0,1:T(8,128)S(1)}) fusion(bf16[2048,576]{1,0:T(8,128)(2,1)} %bitcast.131, bf16[32,32]{1,0:T(8,128)(2,1)S(1)} %bitcast.150, bf16[32,32]{1,0:T(8,128)(2,1)S(1)} %bitcast.149, bf16[32,512]{1,0:T(8,128)(2,1)} %bitcast.148, f32[32]{0:T(128)S(1)} %broadcast_in_dim.277, ...), kind=kOutput, calls=%fused_computation.212 | convolution fusion | flops 75870176 | bytes 2674944 | tf_op jit(solution)/shard_map/dot_general | solution.py:317
  12.2 0.3 convert_reduce_fusion
  12.8 0.2 multiply_cosine_fusion
  13.3 0.2 copy.47
  13.5 2.1 %fusion.14 = f32[4,8,512]{2,1,0:T(8,128)S(1)} fusion(bf16[2048,576]{1,0:T(8,128)(2,1)} %bitcast.132, pred[2048,4]{0,1:T(4,128)(4,1)S(1)} %iota_compare_fusion.4, f32[4,512]{1,0:T(4,128)S(1)} %get-tuple-element.26, f32[4,8]{1,0:T(4,128)S(1)} %mul.313, f32[2048,32]{0,1:T(8,128)S(1)} %get-tuple-element.43, f32[32]{0:T(128)S(1)} %get-tuple-element.42, ...), kind=kOutput, calls=%fused_computation.24 | convolution fusion | flops 67403776 | bytes 2449664 | tf_op jit(solution)/shard_map/dot_general | solution.py:331
  15.7 0.7 pad_maximum_fusion.keys_ref
  16.4 0.7 maximum_maximum_fusion.parts_ref
  17.1 9.2 %shard_map.211 = (bf16[4,64,576]{2,1,0:T(8,128)(2,1)}, f32[4,8,640]{2,1,0:T(8,128)}) custom-call(bf16[64,576]{1,0:T(8,128)(2,1)} %pad_maximum_fusion.keys_ref, f32[4,8,640]{2,1,0:T(8,128)} %maximum_maximum_fusion.parts_ref), custom_call_target="tpu_custom_call" | custom-call | tf_op jit(solution)/shard_map/pallas_call | solution.py:192
  26.3 0.7 bitcast_dynamic-update-slice_fusion
  27.0 1.3 convolution_bitcast_fusion
  28.5 1.2 fusion.101
  29.9 0.4 fusion.10
  30.3 0.2 copy.48
  30.4 0.3 copy-done.9
  30.7 1.2 bitcast_dynamic-update-slice_fusion.1
  32.0 0.2 slice_reduce_fusion
  32.4 0.3 fusion.13
  32.9 1.0 multiply_reduce_fusion
  34.2 0.2 fusion.18
  34.6 3.3 %convert_bitcast_fusion = bf16[128,8,2048]{2,1,0:T(8,128)(2,1)} fusion(bf16[65,1024]{0,1:T(8,128)(2,1)S(1)} %bitcast.135, f32[65,2048]{1,0:T(8,128)S(1)} %get-tuple-element.47, f32[2048]{0:T(1024)S(1)} %copy-done.12, f32[65]{0:T(128)S(1)} %add_rsqrt_fusion), kind=kOutput, calls=%fused_computation.1 | convolution fusion | flops 275126272 | bytes 4868356 | tf_op jit(solution)/shard_map/dot_general | solution.py:426
  37.9 10.5 %all-to-all-start = ((bf16[128,8,2048]{2,1,0:T(8,128)(2,1)}), bf16[128,8,2048]{2,1,0:T(8,128)(2,1)}, u32[]{:S(2)}, u32[]{:S(2)}) async-start(bf16[128,8,2048]{2,1,0:T(8,128)(2,1)} %convert_bitcast_fusion), calls=%async_computation | async-start | bytes 8388608 | tf_op jit(solution)/shard_map/all_to_all | solution.py:430
  48.4 4.6 %copy.51 = bf16[1,2048,704]{2,1,0:T(8,128)(2,1)} copy(bf16[1,2048,704]{1,2,0:T(8,128)(2,1)} %param.37) | data formatting | bytes 5767168 | tf_op args[17]
  53.0 4.6 %copy.52 = bf16[1,2048,704]{2,1,0:T(8,128)(2,1)} copy(bf16[1,2048,704]{1,2,0:T(8,128)(2,1)} %param.38) | data formatting | bytes 5767168 | tf_op args[18]
  57.7 46.4 %all-to-all-done = bf16[128,8,2048]{2,1,0:T(8,128)(2,1)} async-done(((bf16[128,8,2048]{2,1,0:T(8,128)(2,1)}), bf16[128,8,2048]{2,1,0:T(8,128)(2,1)}, u32[]{:S(2)}, u32[]{:S(2)}) %all-to-all-start) | async-done | bytes 4194336 | tf_op jit(solution)/shard_map/all_to_all | solution.py:430
  104.1 1.9 %copy-done.1 = bf16[1,2048,704]{2,1,0:T(8,128)(2,1)S(1)} copy-done((bf16[1,2048,704]{2,1,0:T(8,128)(2,1)S(1)}, bf16[1,2048,704]{2,1,0:T(8,128)(2,1)}, u32[]{:S(2)}) %copy-start.1) | copy-done | bytes 2883608
  106.0 1.8 copy-done.2
  107.8 14.0 %shard_map.212 = bf16[1024,2048]{1,0:T(8,128)(2,1)} custom-call(bf16[1024,2048]{1,0:T(8,128)(2,1)} %bitcast.40.x_ref, bf16[2048,704]{1,0:T(8,128)(2,1)S(1)} %bitcast.129, bf16[2048,704]{1,0:T(8,128)(2,1)} %bitcast.134, bf16[704,2048]{1,0:T(8,128)(2,1)S(1)} %bitcast.130), custom_call_target="tpu_custom_call" | custom-call | flops 8858370048 | bytes 17039360 | tf_op jit(solution)/shard_map/pallas_call | solution.py:220
  121.7 5.1 %all-to-all-start.1 = ((bf16[128,8,2048]{2,1,0:T(8,128)(2,1)}), bf16[128,8,2048]{2,1,0:T(8,128)(2,1)}, u32[]{:S(2)}, u32[]{:S(2)}) async-start(bf16[128,8,2048]{2,1,0:T(8,128)(2,1)} %bitcast.133), calls=%async_computation.1 | async-start | bytes 8388608 | tf_op jit(solution)/shard_map/all_to_all | solution.py:435
  126.9 0.6 fusion.99
  127.5 1.3 fusion.68
  128.8 1.2 fusion.70
  130.1 0.5 fusion.17
  130.6 0.2 select_reduce_fusion
  130.8 4.6 %select_select_fusion = bf16[32,64,576]{2,1,0:T(8,128)(2,1)} fusion(bf16[32,64,576]{2,1,0:T(8,128)(2,1)} %param.31, pred[32,64]{1,0:T(8,128)(4,1)S(1)} %get-tuple-element.48, pred[32,64]{1,0:T(8,128)(4,1)S(1)} %get-tuple-element.49, pred[32,64]{1,0:T(8,128)(4,1)S(1)} %get-tuple-element.50, pred[32,64]{1,0:T(8,128)(4,1)S(1)} %get-tuple-element.51, ...), kind=kLoop, calls=%fused_computation.2 | loop fusion | flops 4718592 | bytes 4731392 | tf_op jit(solution)/shard_map/jit(_where)/select_n | solution.py:300
  135.4 45.3 %all-to-all-done.1 = bf16[128,8,2048]{2,1,0:T(8,128)(2,1)} async-done(((bf16[128,8,2048]{2,1,0:T(8,128)(2,1)}), bf16[128,8,2048]{2,1,0:T(8,128)(2,1)}, u32[]{:S(2)}, u32[]{:S(2)}) %all-to-all-start.1) | async-done | bytes 4194336 | tf_op jit(solution)/shard_map/all_to_all | solution.py:435
  180.7 3.6 %fusion = bf16[65,2048]{1,0:T(8,128)(2,1)S(1)} fusion(f32[65,2048]{1,0:T(8,128)S(1)} %get-tuple-element.47, f32[65,512]{1,0:T(8,128)S(1)} %select_reduce_fusion, bf16[64,2,8,2048]{3,2,1,0:T(8,128)(2,1)} %bitcast.45), kind=kOutput, calls=%fused_computation.5 | convolution fusion | flops 822349824 | bytes 5126144 | tf_op jit(solution)/shard_map/dot_general | solution.py:442
  184.4 0.7 slice_bitcast_fusion.4
  185.1 0.6 slice_bitcast_fusion.5
  (76 shorter events, 2.9 us)
Async XLA Ops:
  0.6 31.8 %copy-start = (bf16[8,512,128]{2,1,0:T(8,128)(2,1)S(1)}, bf16[8,512,128]{2,1,0:T(8,128)(2,1)}, u32[]{:S(2)}) copy-start(bf16[8,512,128]{2,1,0:T(8,128)(2,1)} %param.32) | copy-start | bytes 3145732
  0.6 12.0 %copy-start.14 = (s32[8]{0:T(128)S(1)}, s32[8]{0:T(128)}, u32[]{:S(2)}) copy-start(s32[8]{0:T(128)} %param.24) | copy-start | bytes 100
  0.7 12.2 %copy-start.10 = (bf16[1,64,576]{2,1,0:T(8,128)(2,1)S(1)}, bf16[1,64,576]{2,1,0:T(8,128)(2,1)}, u32[]{:S(2)}) copy-start(bf16[1,64,576]{2,1,0:T(8,128)(2,1)} %param.20) | copy-start | bytes 221188
  12.1 14.9 %copy-start.4 = (bf16[1,64,8,512]{3,2,1,0:T(8,128)(2,1)S(1)}, bf16[1,64,8,512]{3,2,1,0:T(8,128)(2,1)}, u32[]{:S(2)}) copy-start(bf16[1,64,8,512]{3,2,1,0:T(8,128)(2,1)} %param.21) | copy-start | bytes 1572868
  12.8 15.5 %copy-start.6 = (bf16[1,64,8,64]{3,2,1,0:T(8,128)(2,1)S(1)}, bf16[1,64,8,64]{3,2,1,0:T(8,128)(2,1)}, u32[]{:S(2)}) copy-start(bf16[1,64,8,64]{3,2,1,0:T(8,128)(2,1)} %param.22) | copy-start | bytes 196612
  27.0 2.9 %copy-start.7 = (bf16[4,64,576]{2,1,0:T(8,128)(2,1)S(1)}, bf16[4,64,576]{2,1,0:T(8,128)(2,1)}, u32[]{:S(2)}) copy-start(bf16[4,64,576]{2,1,0:T(8,128)(2,1)} %bitcast_dynamic-update-slice_fusion) | copy-start | bytes 884740
  29.9 0.9 copy-start.9
  29.9 3.0 %copy-start.3 = (bf16[1024,2048]{1,0:T(8,128)(2,1)S(1)}, bf16[1024,2048]{1,0:T(8,128)(2,1)}, u32[]{:S(2)}) copy-start(bf16[1024,2048]{1,0:T(8,128)(2,1)} %param.33) | copy-start | bytes 12582916
  30.2 2.6 %copy-start.13 = (bf16[4,1,2048]{2,0,1:T(4,128)(2,1)S(1)}, bf16[4,1,2048]{2,0,1:T(4,128)(2,1)}, u32[]{:S(2)}) copy-start(bf16[4,1,2048]{2,0,1:T(4,128)(2,1)} %param.28) | copy-start | bytes 49156
  30.3 2.7 %copy-start.8 = (bf16[1,64,2048]{2,1,0:T(8,128)(2,1)S(1)}, bf16[1,64,2048]{2,1,0:T(8,128)(2,1)}, u32[]{:S(2)}) copy-start(bf16[1,64,2048]{2,1,0:T(8,128)(2,1)} %param.23) | copy-start | bytes 786436
  32.9 1.1 copy-start.11
  32.9 1.7 copy-start.12
  37.9 66.2 %all-to-all-start = ((bf16[128,8,2048]{2,1,0:T(8,128)(2,1)}), bf16[128,8,2048]{2,1,0:T(8,128)(2,1)}, u32[]{:S(2)}, u32[]{:S(2)}) async-start(bf16[128,8,2048]{2,1,0:T(8,128)(2,1)} %convert_bitcast_fusion), calls=%async_computation | async-start | bytes 8388608 | tf_op jit(solution)/shard_map/all_to_all | solution.py:430
  104.1 1.9 %copy-start.1 = (bf16[1,2048,704]{2,1,0:T(8,128)(2,1)S(1)}, bf16[1,2048,704]{2,1,0:T(8,128)(2,1)}, u32[]{:S(2)}) copy-start(bf16[1,2048,704]{2,1,0:T(8,128)(2,1)} %copy.51) | copy-start | bytes 8650756
  106.0 1.8 copy-start.2
  121.7 8.3 %copy-start.5 = (f32[2048,64]{0,1:T(8,128)S(1)}, f32[2048,64]{0,1:T(8,128)}, u32[]{:S(2)}) copy-start(f32[2048,64]{0,1:T(8,128)} %param.35) | copy-start | bytes 1572868
  121.7 59.0 %all-to-all-start.1 = ((bf16[128,8,2048]{2,1,0:T(8,128)(2,1)}), bf16[128,8,2048]{2,1,0:T(8,128)(2,1)}, u32[]{:S(2)}, u32[]{:S(2)}) async-start(bf16[128,8,2048]{2,1,0:T(8,128)(2,1)} %bitcast.133), calls=%async_computation.1 | async-start | bytes 8388608 | tf_op jit(solution)/shard_map/all_to_all | solution.py:435

commit v17 on v15

--- a/solution.py
+++ b/solution.py
@@ -376,7 +376,7 @@
             preferred_element_type=jnp.float32,
         )
     ) * score_scale
-    visible = jnp.repeat(key_pos_pre[None, :] <= own_pos[:, None], head_count, axis=0)
+    visible = key_pos_pre[None, :] <= jnp.repeat(own_pos, head_count)[:, None]
     masked = jnp.where(visible, scores, NEG_FILL)
     new_peak = jnp.max(masked, axis=-1)
     weights = jnp.where(visible, jnp.exp(masked - new_peak[..., None]), 0.0)

time: 186 us -> 186 us (level)
  no operation moved by 1% of the time
where the time goes in v17:
time: 186 us; the launch traced here: 185 us
  waiting for transfers between devices  91.9 us (49%)
  Pallas kernels  22.8 us (12%)
  local copies, waits for them, and re-layouts  18.6 us (10%)
  other arithmetic  17.7 us (10%)
  matrix products  17.6 us (9%)
  starting transfers between devices  15.4 us (8%)
    all_to_all x1, waiting for transfers between devices, body(): lax.all_to_all(doubled, ('ctx', 'req'), split_axis=0, concat_axis=0, tile...  46.4 us
    all_to_all x1, waiting for transfers between devices, body(): lax.all_to_all(partial_out, ('ctx', 'req'), split_axis=0, concat_axis=0,...  45.5 us
    pallas_call x1, Pallas kernels, ffn_half(): pl.pallas_call(ffn_kernel, grid=(rows // tile,), in_specs=[pl.BlockSpec((...  13.7 us
    unnamed x34, local copies, waits for them, and re-layouts  13.3 us
    all_to_all x1, starting transfers between devices, body(): lax.all_to_all(doubled, ('ctx', 'req'), split_axis=0, concat_axis=0, tile...  10.5 us
    pallas_call x1, Pallas kernels, context_exchange(): pl.pallas_call(functools.partial(context_kernel, n_ctx), out_shape=(jax.S...  9.16 us
    all_to_all x1, starting transfers between devices, body(): lax.all_to_all(partial_out, ('ctx', 'req'), split_axis=0, concat_axis=0,...  4.89 us
    select_n x1, other arithmetic, body(): jnp.where(row_ids == target[request], new_rows[request][None, :], flat_pool)  4.6 us
  transfers between devices with their start and end apart: 2, of which 2 were waited for; matrix products, arithmetic and copies ran while one was open for 10% of the time, Pallas kernels for 0%

profile of v17, /device:TPU:8, one launch (start us, length us, event | category | flops | bytes accessed | tf_op | source)
XLA Modules:
  0.0 185.2 jit_solution(4164717241933203330)
XLA Ops:
  0.7 0.8 slice_bitcast_fusion.7
  1.4 0.7 fusion.97
  2.1 0.8 select_reduce_fusion.4
  2.9 0.8 fusion.75
  3.7 0.7 convert_bitcast_fusion.1
  4.6 0.9 fusion.67
  5.5 1.0 fusion.49
  7.0 0.9 select_reduce_fusion.7
  7.8 0.7 compare_select_fusion.3
  8.6 0.7 fusion.65
  9.4 2.7 %fusion.102 = (f32[32]{0:T(128)S(1)}, f32[2048,32]{0,1:T(8,128)S(1)}) fusion(bf16[2048,576]{1,0:T(8,128)(2,1)} %bitcast.129, bf16[32,32]{1,0:T(8,128)(2,1)S(1)} %bitcast.148, bf16[32,32]{1,0:T(8,128)(2,1)S(1)} %bitcast.147, bf16[32,512]{1,0:T(8,128)(2,1)} %bitcast.146, f32[32]{0:T(128)S(1)} %broadcast_in_dim.276, ...), kind=kOutput, calls=%fused_computation.212 | convolution fusion | flops 75870176 | bytes 2674944 | tf_op jit(solution)/shard_map/dot_general | solution.py:317
  12.2 0.3 convert_reduce_fusion
  12.8 0.2 multiply_cosine_fusion
  13.3 2.1 %fusion.14 = f32[4,8,512]{2,1,0:T(8,128)S(1)} fusion(bf16[2048,576]{1,0:T(8,128)(2,1)} %bitcast.130, pred[2048,4]{0,1:T(4,128)(4,1)S(1)} %iota_compare_fusion.4, f32[4,512]{1,0:T(4,128)S(1)} %get-tuple-element.26, f32[4,8]{1,0:T(4,128)S(1)} %mul.310, f32[2048,32]{0,1:T(8,128)S(1)} %get-tuple-element.43, f32[32]{0:T(128)S(1)} %get-tuple-element.42, ...), kind=kOutput, calls=%fused_computation.24 | convolution fusion | flops 67403776 | bytes 2449664 | tf_op jit(solution)/shard_map/dot_general | solution.py:331
  15.5 0.7 pad_maximum_fusion.keys_ref
  16.2 0.7 maximum_maximum_fusion.parts_ref
  16.9 9.2 %shard_map.211 = (bf16[4,64,576]{2,1,0:T(8,128)(2,1)}, f32[4,8,640]{2,1,0:T(8,128)}) custom-call(bf16[64,576]{1,0:T(8,128)(2,1)} %pad_maximum_fusion.keys_ref, f32[4,8,640]{2,1,0:T(8,128)} %maximum_maximum_fusion.parts_ref), custom_call_target="tpu_custom_call" | custom-call | tf_op jit(solution)/shard_map/pallas_call | solution.py:192
  26.1 0.7 bitcast_dynamic-update-slice_fusion
  26.8 1.3 convolution_bitcast_fusion
  28.1 0.2 fusion.39
  28.3 1.2 fusion.103
  29.7 0.4 fusion.10
  30.1 0.2 copy.44
  30.3 0.3 copy-done.9
  30.5 1.2 bitcast_dynamic-update-slice_fusion.1
  31.8 0.2 slice_reduce_fusion
  32.2 0.3 fusion.13
  32.7 1.0 multiply_reduce_fusion
  34.0 0.2 fusion.18
  34.4 3.3 %convert_bitcast_fusion = bf16[128,8,2048]{2,1,0:T(8,128)(2,1)} fusion(bf16[65,1024]{0,1:T(8,128)(2,1)S(1)} %bitcast.133, f32[65,2048]{1,0:T(8,128)S(1)} %get-tuple-element.47, f32[2048]{0:T(1024)S(1)} %copy-done.12, f32[65]{0:T(128)S(1)} %add_rsqrt_fusion), kind=kOutput, calls=%fused_computation.1 | convolution fusion | flops 275126272 | bytes 4868356 | tf_op jit(solution)/shard_map/dot_general | solution.py:426
  37.7 10.5 %all-to-all-start = ((bf16[128,8,2048]{2,1,0:T(8,128)(2,1)}), bf16[128,8,2048]{2,1,0:T(8,128)(2,1)}, u32[]{:S(2)}, u32[]{:S(2)}) async-start(bf16[128,8,2048]{2,1,0:T(8,128)(2,1)} %convert_bitcast_fusion), calls=%async_computation | async-start | bytes 8388608 | tf_op jit(solution)/shard_map/all_to_all | solution.py:430
  48.2 4.6 %copy.47 = bf16[1,2048,704]{2,1,0:T(8,128)(2,1)} copy(bf16[1,2048,704]{1,2,0:T(8,128)(2,1)} %param.37) | data formatting | bytes 5767168 | tf_op args[17]
  52.8 4.6 %copy.48 = bf16[1,2048,704]{2,1,0:T(8,128)(2,1)} copy(bf16[1,2048,704]{1,2,0:T(8,128)(2,1)} %param.38) | data formatting | bytes 5767168 | tf_op args[18]
  57.5 46.4 %all-to-all-done = bf16[128,8,2048]{2,1,0:T(8,128)(2,1)} async-done(((bf16[128,8,2048]{2,1,0:T(8,128)(2,1)}), bf16[128,8,2048]{2,1,0:T(8,128)(2,1)}, u32[]{:S(2)}, u32[]{:S(2)}) %all-to-all-start) | async-done | bytes 4194336 | tf_op jit(solution)/shard_map/all_to_all | solution.py:430
  103.8 1.9 %copy-done.1 = bf16[1,2048,704]{2,1,0:T(8,128)(2,1)S(1)} copy-done((bf16[1,2048,704]{2,1,0:T(8,128)(2,1)S(1)}, bf16[1,2048,704]{2,1,0:T(8,128)(2,1)}, u32[]{:S(2)}) %copy-start.1) | copy-done | bytes 2883608
  105.7 1.8 copy-done.2
  107.5 13.7 %shard_map.212 = bf16[1024,2048]{1,0:T(8,128)(2,1)} custom-call(bf16[1024,2048]{1,0:T(8,128)(2,1)} %bitcast.39.x_ref, bf16[2048,704]{1,0:T(8,128)(2,1)S(1)} %bitcast.127, bf16[2048,704]{1,0:T(8,128)(2,1)} %bitcast.132, bf16[704,2048]{1,0:T(8,128)(2,1)S(1)} %bitcast.128), custom_call_target="tpu_custom_call" | custom-call | flops 8858370048 | bytes 17039360 | tf_op jit(solution)/shard_map/pallas_call | solution.py:220
  121.2 4.9 %all-to-all-start.1 = ((bf16[128,8,2048]{2,1,0:T(8,128)(2,1)}), bf16[128,8,2048]{2,1,0:T(8,128)(2,1)}, u32[]{:S(2)}, u32[]{:S(2)}) async-start(bf16[128,8,2048]{2,1,0:T(8,128)(2,1)} %bitcast.131), calls=%async_computation.1 | async-start | bytes 8388608 | tf_op jit(solution)/shard_map/all_to_all | solution.py:435
  126.2 0.6 fusion.101
  126.8 1.3 fusion.70
  128.1 1.2 fusion.72
  129.4 0.5 fusion.17
  129.9 0.2 select_reduce_fusion
  130.1 4.6 %select_select_fusion = bf16[32,64,576]{2,1,0:T(8,128)(2,1)} fusion(bf16[32,64,576]{2,1,0:T(8,128)(2,1)} %param.31, pred[32,64]{1,0:T(8,128)(4,1)S(1)} %get-tuple-element.48, pred[32,64]{1,0:T(8,128)(4,1)S(1)} %get-tuple-element.49, pred[32,64]{1,0:T(8,128)(4,1)S(1)} %get-tuple-element.50, pred[32,64]{1,0:T(8,128)(4,1)S(1)} %get-tuple-element.51, ...), kind=kLoop, calls=%fused_computation.2 | loop fusion | flops 4718592 | bytes 4731392 | tf_op jit(solution)/shard_map/jit(_where)/select_n | solution.py:300
  134.7 45.5 %all-to-all-done.1 = bf16[128,8,2048]{2,1,0:T(8,128)(2,1)} async-done(((bf16[128,8,2048]{2,1,0:T(8,128)(2,1)}), bf16[128,8,2048]{2,1,0:T(8,128)(2,1)}, u32[]{:S(2)}, u32[]{:S(2)}) %all-to-all-start.1) | async-done | bytes 4194336 | tf_op jit(solution)/shard_map/all_to_all | solution.py:435
  180.2 3.6 %fusion = bf16[65,2048]{1,0:T(8,128)(2,1)S(1)} fusion(f32[65,2048]{1,0:T(8,128)S(1)} %get-tuple-element.47, f32[65,512]{1,0:T(8,128)S(1)} %select_reduce_fusion, bf16[64,2,8,2048]{3,2,1,0:T(8,128)(2,1)} %bitcast.44), kind=kOutput, calls=%fused_computation.5 | convolution fusion | flops 822349824 | bytes 5126144 | tf_op jit(solution)/shard_map/dot_general | solution.py:442
  183.9 0.7 slice_bitcast_fusion.4
  184.6 0.6 slice_bitcast_fusion.5
  (75 shorter events, 2.8 us)
Async XLA Ops:
  0.6 31.6 %copy-start = (bf16[8,512,128]{2,1,0:T(8,128)(2,1)S(1)}, bf16[8,512,128]{2,1,0:T(8,128)(2,1)}, u32[]{:S(2)}) copy-start(bf16[8,512,128]{2,1,0:T(8,128)(2,1)} %param.32) | copy-start | bytes 3145732
  0.6 12.1 %copy-start.14 = (s32[8]{0:T(128)S(1)}, s32[8]{0:T(128)}, u32[]{:S(2)}) copy-start(s32[8]{0:T(128)} %param.24) | copy-start | bytes 100
  0.7 12.2 %copy-start.10 = (bf16[1,64,576]{2,1,0:T(8,128)(2,1)S(1)}, bf16[1,64,576]{2,1,0:T(8,128)(2,1)}, u32[]{:S(2)}) copy-start(bf16[1,64,576]{2,1,0:T(8,128)(2,1)} %param.20) | copy-start | bytes 221188
  12.1 14.7 %copy-start.4 = (bf16[1,64,8,512]{3,2,1,0:T(8,128)(2,1)S(1)}, bf16[1,64,8,512]{3,2,1,0:T(8,128)(2,1)}, u32[]{:S(2)}) copy-start(bf16[1,64,8,512]{3,2,1,0:T(8,128)(2,1)} %param.21) | copy-start | bytes 1572868
  12.2 15.9 %copy-start.6 = (bf16[1,64,8,64]{3,2,1,0:T(8,128)(2,1)S(1)}, bf16[1,64,8,64]{3,2,1,0:T(8,128)(2,1)}, u32[]{:S(2)}) copy-start(bf16[1,64,8,64]{3,2,1,0:T(8,128)(2,1)} %param.22) | copy-start | bytes 196612
  26.8 2.8 %copy-start.7 = (bf16[4,64,576]{2,1,0:T(8,128)(2,1)S(1)}, bf16[4,64,576]{2,1,0:T(8,128)(2,1)}, u32[]{:S(2)}) copy-start(bf16[4,64,576]{2,1,0:T(8,128)(2,1)} %bitcast_dynamic-update-slice_fusion) | copy-start | bytes 884740
  29.6 0.9 copy-start.9
  29.6 3.0 %copy-start.3 = (bf16[1024,2048]{1,0:T(8,128)(2,1)S(1)}, bf16[1024,2048]{1,0:T(8,128)(2,1)}, u32[]{:S(2)}) copy-start(bf16[1024,2048]{1,0:T(8,128)(2,1)} %param.33) | copy-start | bytes 12582916
  30.1 2.6 %copy-start.13 = (bf16[4,1,2048]{2,0,1:T(4,128)(2,1)S(1)}, bf16[4,1,2048]{2,0,1:T(4,128)(2,1)}, u32[]{:S(2)}) copy-start(bf16[4,1,2048]{2,0,1:T(4,128)(2,1)} %param.28) | copy-start | bytes 49156
  30.1 2.6 %copy-start.8 = (bf16[1,64,2048]{2,1,0:T(8,128)(2,1)S(1)}, bf16[1,64,2048]{2,1,0:T(8,128)(2,1)}, u32[]{:S(2)}) copy-start(bf16[1,64,2048]{2,1,0:T(8,128)(2,1)} %param.23) | copy-start | bytes 786436
  32.7 1.1 copy-start.11
  32.7 1.7 copy-start.12
  37.7 66.2 %all-to-all-start = ((bf16[128,8,2048]{2,1,0:T(8,128)(2,1)}), bf16[128,8,2048]{2,1,0:T(8,128)(2,1)}, u32[]{:S(2)}, u32[]{:S(2)}) async-start(bf16[128,8,2048]{2,1,0:T(8,128)(2,1)} %convert_bitcast_fusion), calls=%async_computation | async-start | bytes 8388608 | tf_op jit(solution)/shard_map/all_to_all | solution.py:430
  103.8 1.9 %copy-start.1 = (bf16[1,2048,704]{2,1,0:T(8,128)(2,1)S(1)}, bf16[1,2048,704]{2,1,0:T(8,128)(2,1)}, u32[]{:S(2)}) copy-start(bf16[1,2048,704]{2,1,0:T(8,128)(2,1)} %copy.47) | copy-start | bytes 8650756
  105.7 1.8 copy-start.2
  121.2 8.2 %copy-start.5 = (f32[2048,64]{0,1:T(8,128)S(1)}, f32[2048,64]{0,1:T(8,128)}, u32[]{:S(2)}) copy-start(f32[2048,64]{0,1:T(8,128)} %param.35) | copy-start | bytes 1572868
  121.2 59.0 %all-to-all-start.1 = ((bf16[128,8,2048]{2,1,0:T(8,128)(2,1)}), bf16[128,8,2048]{2,1,0:T(8,128)(2,1)}, u32[]{:S(2)}, u32[]{:S(2)}) async-start(bf16[128,8,2048]{2,1,0:T(8,128)(2,1)} %bitcast.131), calls=%async_computation.1 | async-start | bytes 8388608 | tf_op jit(solution)/shard_map/all_to_all | solution.py:435

commit v18 on v17

--- a/solution.py
+++ b/solution.py
@@ -421,11 +421,14 @@
     slot_index = jnp.sum(jnp.where(route_hit, before[:, None, :], 0), axis=-1)
     target_slot = routes * capacity + slot_index
     slot_hit = target_slot[:, :, None] == jnp.arange(expert_count * capacity)[None, None, :]
-    dispatch = jnp.any(slot_hit, axis=1).astype(jnp.bfloat16).reshape(row_count, expert_count, 1, capacity)
-    dispatch = jnp.broadcast_to(dispatch, (row_count, expert_count, 2, capacity)).reshape(row_count, -1)
-    doubled = lax.dot_general(
-        dispatch, normed, (((0,), (0,)), ((), ())), preferred_element_type=jnp.float32
-    ).astype(jnp.bfloat16).reshape(devices, capacity, width)
+    slot_ids = jnp.broadcast_to(
+        (jnp.arange(expert_count) * capacity)[:, None, None] + jnp.arange(capacity)[None, None, :],
+        (expert_count, 2, capacity),
+    ).reshape(-1)
+    dispatch = jnp.any(slot_ids[:, None, None] == target_slot[None], axis=2).astype(jnp.bfloat16)
+    doubled = jnp.dot(dispatch, normed, preferred_element_type=jnp.float32).astype(
+        jnp.bfloat16
+    ).reshape(devices, capacity, width)
     partial_out = ffn_half(
         lax.all_to_all(doubled, ("ctx", "req"), split_axis=0, concat_axis=0, tiled=True),
         w_gate[0],

time: 186 us -> 186 us (level)
  no operation moved by 1% of the time
where the time goes in v18:
time: 186 us; the launch traced here: 185 us
  waiting for transfers between devices  91.9 us (49%)
  Pallas kernels  22.8 us (12%)
  local copies, waits for them, and re-layouts  18.6 us (10%)
  other arithmetic  17.9 us (10%)
  matrix products  17.6 us (9%)
  starting transfers between devices  15.4 us (8%)
    all_to_all x1, waiting for transfers between devices, body(): lax.all_to_all(doubled, ('ctx', 'req'), split_axis=0, concat_axis=0, tile...  46.4 us
    all_to_all x1, waiting for transfers between devices, body(): lax.all_to_all(partial_out, ('ctx', 'req'), split_axis=0, concat_axis=0,...  45.5 us
    pallas_call x1, Pallas kernels, ffn_half(): pl.pallas_call(ffn_kernel, grid=(rows // tile,), in_specs=[pl.BlockSpec((...  13.7 us
    unnamed x34, local copies, waits for them, and re-layouts  13.3 us
    all_to_all x1, starting transfers between devices, body(): lax.all_to_all(doubled, ('ctx', 'req'), split_axis=0, concat_axis=0, tile...  10.5 us
    pallas_call x1, Pallas kernels, context_exchange(): pl.pallas_call(functools.partial(context_kernel, n_ctx), out_shape=(jax.S...  9.16 us
    all_to_all x1, starting transfers between devices, body(): lax.all_to_all(partial_out, ('ctx', 'req'), split_axis=0, concat_axis=0,...  4.89 us
    select_n x1, other arithmetic, body(): jnp.where(row_ids == target[request], new_rows[request][None, :], flat_pool)  4.6 us
  transfers between devices with their start and end apart: 2, of which 2 were waited for; matrix products, arithmetic and copies ran while one was open for 10% of the time, Pallas kernels for 0%

profile of v18, /device:TPU:8, one launch (start us, length us, event | category | flops | bytes accessed | tf_op | source)
XLA Modules:
  0.0 185.3 jit_solution(13576456285537445179)
XLA Ops:
  0.7 0.8 slice_bitcast_fusion.7
  1.4 0.7 fusion.96
  2.1 0.8 select_reduce_fusion.4
  2.9 0.8 fusion.74
  3.7 0.7 convert_bitcast_fusion.1
  4.6 0.9 fusion.66
  5.5 1.0 fusion.48
  7.0 0.9 select_reduce_fusion.7
  7.9 0.7 compare_select_fusion.3
  8.6 0.7 fusion.64
  9.4 2.7 %fusion.101 = (f32[32]{0:T(128)S(1)}, f32[2048,32]{0,1:T(8,128)S(1)}) fusion(bf16[2048,576]{1,0:T(8,128)(2,1)} %bitcast.127, bf16[32,32]{1,0:T(8,128)(2,1)S(1)} %bitcast.144, bf16[32,32]{1,0:T(8,128)(2,1)S(1)} %bitcast.143, bf16[32,512]{1,0:T(8,128)(2,1)} %bitcast.142, f32[32]{0:T(128)S(1)} %broadcast_in_dim.279, ...), kind=kOutput, calls=%fused_computation.214 | convolution fusion | flops 75870176 | bytes 2674944 | tf_op jit(solution)/shard_map/dot_general | solution.py:317
  12.2 0.3 convert_reduce_fusion
  12.8 0.2 multiply_cosine_fusion
  13.3 2.1 %fusion.14 = f32[4,8,512]{2,1,0:T(8,128)S(1)} fusion(bf16[2048,576]{1,0:T(8,128)(2,1)} %bitcast.128, pred[2048,4]{0,1:T(4,128)(4,1)S(1)} %iota_compare_fusion.4, f32[4,512]{1,0:T(4,128)S(1)} %get-tuple-element.26, f32[4,8]{1,0:T(4,128)S(1)} %mul.320, f32[2048,32]{0,1:T(8,128)S(1)} %get-tuple-element.43, f32[32]{0:T(128)S(1)} %get-tuple-element.42, ...), kind=kOutput, calls=%fused_computation.25 | convolution fusion | flops 67403776 | bytes 2449664 | tf_op jit(solution)/shard_map/dot_general | solution.py:331
  15.5 0.7 pad_maximum_fusion.keys_ref
  16.2 0.7 maximum_maximum_fusion.parts_ref
  16.9 9.2 %shard_map.211 = (bf16[4,64,576]{2,1,0:T(8,128)(2,1)}, f32[4,8,640]{2,1,0:T(8,128)}) custom-call(bf16[64,576]{1,0:T(8,128)(2,1)} %pad_maximum_fusion.keys_ref, f32[4,8,640]{2,1,0:T(8,128)} %maximum_maximum_fusion.parts_ref), custom_call_target="tpu_custom_call" | custom-call | tf_op jit(solution)/shard_map/pallas_call | solution.py:192
  26.1 0.7 bitcast_dynamic-update-slice_fusion
  26.8 1.3 convolution_bitcast_fusion
  28.2 0.2 fusion.38
  28.3 1.2 fusion.102
  29.7 0.4 fusion.10
  30.1 0.2 copy.46
  30.3 0.3 copy-done.9
  30.5 1.2 bitcast_dynamic-update-slice_fusion.1
  31.8 0.2 slice_reduce_fusion
  32.2 0.3 fusion.13
  32.7 1.0 multiply_reduce_fusion
  34.2 0.3 compare_reduce_fusion
  34.5 3.3 %convert_bitcast_fusion = bf16[128,8,2048]{2,1,0:T(8,128)(2,1)} fusion(pred[1024,65]{0,1:T(8,128)(4,1)S(1)} %compare_reduce_fusion, f32[65,2048]{1,0:T(8,128)S(1)} %get-tuple-element.47, f32[2048]{0:T(1024)S(1)} %copy-done.12, f32[65]{0:T(128)S(1)} %add_rsqrt_fusion), kind=kOutput, calls=%fused_computation.1 | convolution fusion | flops 275126272 | bytes 4801796 | tf_op jit(solution)/shard_map/dot_general | solution.py:429
  37.8 10.5 %all-to-all-start = ((bf16[128,8,2048]{2,1,0:T(8,128)(2,1)}), bf16[128,8,2048]{2,1,0:T(8,128)(2,1)}, u32[]{:S(2)}, u32[]{:S(2)}) async-start(bf16[128,8,2048]{2,1,0:T(8,128)(2,1)} %convert_bitcast_fusion), calls=%async_computation | async-start | bytes 8388608 | tf_op jit(solution)/shard_map/all_to_all | solution.py:433
  48.4 4.6 %copy.48 = bf16[1,2048,704]{2,1,0:T(8,128)(2,1)} copy(bf16[1,2048,704]{1,2,0:T(8,128)(2,1)} %param.37) | data formatting | bytes 5767168 | tf_op args[17]
  53.0 4.6 %copy.49 = bf16[1,2048,704]{2,1,0:T(8,128)(2,1)} copy(bf16[1,2048,704]{1,2,0:T(8,128)(2,1)} %param.38) | data formatting | bytes 5767168 | tf_op args[18]
  57.6 46.4 %all-to-all-done = bf16[128,8,2048]{2,1,0:T(8,128)(2,1)} async-done(((bf16[128,8,2048]{2,1,0:T(8,128)(2,1)}), bf16[128,8,2048]{2,1,0:T(8,128)(2,1)}, u32[]{:S(2)}, u32[]{:S(2)}) %all-to-all-start) | async-done | bytes 4194336 | tf_op jit(solution)/shard_map/all_to_all | solution.py:433
  104.0 1.9 %copy-done.1 = bf16[1,2048,704]{2,1,0:T(8,128)(2,1)S(1)} copy-done((bf16[1,2048,704]{2,1,0:T(8,128)(2,1)S(1)}, bf16[1,2048,704]{2,1,0:T(8,128)(2,1)}, u32[]{:S(2)}) %copy-start.1) | copy-done | bytes 2883608
  105.9 1.8 copy-done.2
  107.7 13.7 %shard_map.212 = bf16[1024,2048]{1,0:T(8,128)(2,1)} custom-call(bf16[1024,2048]{1,0:T(8,128)(2,1)} %bitcast.37.x_ref, bf16[2048,704]{1,0:T(8,128)(2,1)S(1)} %bitcast.125, bf16[2048,704]{1,0:T(8,128)(2,1)} %bitcast.130, bf16[704,2048]{1,0:T(8,128)(2,1)S(1)} %bitcast.126), custom_call_target="tpu_custom_call" | custom-call | flops 8858370048 | bytes 17039360 | tf_op jit(solution)/shard_map/pallas_call | solution.py:220
  121.4 4.9 %all-to-all-start.1 = ((bf16[128,8,2048]{2,1,0:T(8,128)(2,1)}), bf16[128,8,2048]{2,1,0:T(8,128)(2,1)}, u32[]{:S(2)}, u32[]{:S(2)}) async-start(bf16[128,8,2048]{2,1,0:T(8,128)(2,1)} %bitcast.129), calls=%async_computation.1 | async-start | bytes 8388608 | tf_op jit(solution)/shard_map/all_to_all | solution.py:438
  126.4 0.6 fusion.100
  127.0 1.3 fusion.69
  128.3 1.2 fusion.71
  129.5 0.5 fusion.17
  130.1 0.2 select_reduce_fusion
  130.3 4.6 %select_select_fusion = bf16[32,64,576]{2,1,0:T(8,128)(2,1)} fusion(bf16[32,64,576]{2,1,0:T(8,128)(2,1)} %param.31, pred[32,64]{1,0:T(8,128)(4,1)S(1)} %get-tuple-element.48, pred[32,64]{1,0:T(8,128)(4,1)S(1)} %get-tuple-element.49, pred[32,64]{1,0:T(8,128)(4,1)S(1)} %get-tuple-element.50, pred[32,64]{1,0:T(8,128)(4,1)S(1)} %get-tuple-element.51, ...), kind=kLoop, calls=%fused_computation.2 | loop fusion | flops 4718592 | bytes 4731392 | tf_op jit(solution)/shard_map/jit(_where)/select_n | solution.py:300
  134.9 45.5 %all-to-all-done.1 = bf16[128,8,2048]{2,1,0:T(8,128)(2,1)} async-done(((bf16[128,8,2048]{2,1,0:T(8,128)(2,1)}), bf16[128,8,2048]{2,1,0:T(8,128)(2,1)}, u32[]{:S(2)}, u32[]{:S(2)}) %all-to-all-start.1) | async-done | bytes 4194336 | tf_op jit(solution)/shard_map/all_to_all | solution.py:438
  180.4 3.6 %fusion = bf16[65,2048]{1,0:T(8,128)(2,1)S(1)} fusion(f32[65,2048]{1,0:T(8,128)S(1)} %get-tuple-element.47, f32[65,512]{1,0:T(8,128)S(1)} %select_reduce_fusion, bf16[64,2,8,2048]{3,2,1,0:T(8,128)(2,1)} %bitcast.42), kind=kOutput, calls=%fused_computation.5 | convolution fusion | flops 822349824 | bytes 5126144 | tf_op jit(solution)/shard_map/dot_general | solution.py:445
  184.0 0.7 slice_bitcast_fusion.4
  184.7 0.6 slice_bitcast_fusion.5
  (76 shorter events, 2.8 us)
Async XLA Ops:
  0.6 31.6 %copy-start = (bf16[8,512,128]{2,1,0:T(8,128)(2,1)S(1)}, bf16[8,512,128]{2,1,0:T(8,128)(2,1)}, u32[]{:S(2)}) copy-start(bf16[8,512,128]{2,1,0:T(8,128)(2,1)} %param.32) | copy-start | bytes 3145732
  0.6 12.1 %copy-start.14 = (s32[8]{0:T(128)S(1)}, s32[8]{0:T(128)}, u32[]{:S(2)}) copy-start(s32[8]{0:T(128)} %param.24) | copy-start | bytes 100
  0.7 12.2 %copy-start.10 = (bf16[1,64,576]{2,1,0:T(8,128)(2,1)S(1)}, bf16[1,64,576]{2,1,0:T(8,128)(2,1)}, u32[]{:S(2)}) copy-start(bf16[1,64,576]{2,1,0:T(8,128)(2,1)} %param.20) | copy-start | bytes 221188
  12.1 14.7 %copy-start.4 = (bf16[1,64,8,512]{3,2,1,0:T(8,128)(2,1)S(1)}, bf16[1,64,8,512]{3,2,1,0:T(8,128)(2,1)}, u32[]{:S(2)}) copy-start(bf16[1,64,8,512]{3,2,1,0:T(8,128)(2,1)} %param.21) | copy-start | bytes 1572868
  12.2 15.9 %copy-start.6 = (bf16[1,64,8,64]{3,2,1,0:T(8,128)(2,1)S(1)}, bf16[1,64,8,64]{3,2,1,0:T(8,128)(2,1)}, u32[]{:S(2)}) copy-start(bf16[1,64,8,64]{3,2,1,0:T(8,128)(2,1)} %param.22) | copy-start | bytes 196612
  26.8 2.8 %copy-start.7 = (bf16[4,64,576]{2,1,0:T(8,128)(2,1)S(1)}, bf16[4,64,576]{2,1,0:T(8,128)(2,1)}, u32[]{:S(2)}) copy-start(bf16[4,64,576]{2,1,0:T(8,128)(2,1)} %bitcast_dynamic-update-slice_fusion) | copy-start | bytes 884740
  29.6 0.9 copy-start.9
  29.7 3.0 %copy-start.3 = (bf16[1024,2048]{1,0:T(8,128)(2,1)S(1)}, bf16[1024,2048]{1,0:T(8,128)(2,1)}, u32[]{:S(2)}) copy-start(bf16[1024,2048]{1,0:T(8,128)(2,1)} %param.33) | copy-start | bytes 12582916
  30.1 2.6 %copy-start.13 = (bf16[4,1,2048]{2,0,1:T(4,128)(2,1)S(1)}, bf16[4,1,2048]{2,0,1:T(4,128)(2,1)}, u32[]{:S(2)}) copy-start(bf16[4,1,2048]{2,0,1:T(4,128)(2,1)} %param.28) | copy-start | bytes 49156
  30.1 2.6 %copy-start.8 = (bf16[1,64,2048]{2,1,0:T(8,128)(2,1)S(1)}, bf16[1,64,2048]{2,1,0:T(8,128)(2,1)}, u32[]{:S(2)}) copy-start(bf16[1,64,2048]{2,1,0:T(8,128)(2,1)} %param.23) | copy-start | bytes 786436
  32.7 1.1 copy-start.11
  32.7 1.8 copy-start.12
  37.8 66.2 %all-to-all-start = ((bf16[128,8,2048]{2,1,0:T(8,128)(2,1)}), bf16[128,8,2048]{2,1,0:T(8,128)(2,1)}, u32[]{:S(2)}, u32[]{:S(2)}) async-start(bf16[128,8,2048]{2,1,0:T(8,128)(2,1)} %convert_bitcast_fusion), calls=%async_computation | async-start | bytes 8388608 | tf_op jit(solution)/shard_map/all_to_all | solution.py:433
  104.0 1.9 %copy-start.1 = (bf16[1,2048,704]{2,1,0:T(8,128)(2,1)S(1)}, bf16[1,2048,704]{2,1,0:T(8,128)(2,1)}, u32[]{:S(2)}) copy-start(bf16[1,2048,704]{2,1,0:T(8,128)(2,1)} %copy.48) | copy-start | bytes 8650756
  105.9 1.8 copy-start.2
  121.4 8.2 %copy-start.5 = (f32[2048,64]{0,1:T(8,128)S(1)}, f32[2048,64]{0,1:T(8,128)}, u32[]{:S(2)}) copy-start(f32[2048,64]{0,1:T(8,128)} %param.35) | copy-start | bytes 1572868
  121.4 59.0 %all-to-all-start.1 = ((bf16[128,8,2048]{2,1,0:T(8,128)(2,1)}), bf16[128,8,2048]{2,1,0:T(8,128)(2,1)}, u32[]{:S(2)}, u32[]{:S(2)}) async-start(bf16[128,8,2048]{2,1,0:T(8,128)(2,1)} %bitcast.129), calls=%async_computation.1 | async-start | bytes 8388608 | tf_op jit(solution)/shard_map/all_to_all | solution.py:438
